TPU v7x, 512 devices: a whole 4x4x16 slice. The times are simulated.
512 devices in a mesh: dp: 16 (over z), expert: 32 (over y, x, core).
Axes of the slice: x: 4, y: 4, z: 16, core: 2. Of those that a mesh axis runs over, the one named last changes fastest.
Arguments:
- tokens: bfloat16 [2048, 4096], P('dp', 'expert'), may hold values from -6 to 6
- norm_gain: float32 [4096], replicated, may hold values from 0.1 to 1.9
- routes: int32 [2048, 2], P('dp'), may hold values from 0 to 31, all different within a row; in each aligned block of 128 rows (0 to 127, 128 to 255, ...) at most 10 rows name the same one
- route_prob: float32 [2048, 2], P('dp'), may hold values from 0.2 to 1
- gate_weight: bfloat16 [32, 4096, 2048], P('expert', None, 'dp'), may hold values from -0.09375 to 0.09375
- up_weight: bfloat16 [32, 4096, 2048], P('expert', None, 'dp'), may hold values from -0.09375 to 0.09375
- down_weight: bfloat16 [32, 2048, 4096], P('expert', 'dp'), may hold values from -0.125 to 0.125
- key_value_weight: bfloat16 [4096, 2048], P('expert'), may hold values from -0.09375 to 0.09375
- key_value_target: bfloat16 [2048, 2048], P('dp', 'expert'), may hold values from -6 to 6
- concept_mask: int32 [2048], P('dp'), may hold values 0 or 1
Outputs:
- down_grad: bfloat16 [32, 2048, 4096], P('expert', 'dp')
- key_value_grad: float32 [4096, 2048], P('expert', 'dp')
Inputs may be any that keep to these rules, and one draw needn't show every extreme that they name: `routes`: in each aligned block of 128 rows no expert is named by more than 10 rows; the two choices of a token differ.
All inputs are finite; a program needn't handle non-finite values. No bound on the sum of `concept_mask` on one device may be relied on, other than what follows from the above.
Results may differ from a plain program's by a relative error of at most 0.033.
Values may be sent and summed in bfloat16 or wider, within the bound.
No kernel may reach another device: no remote copies, remote signals or barrier semaphores. Data moves between devices by JAX's collectives and lax.ppermute only.
A program may use at most 64 MiB of HBM per device.

v0:
```python
import jax
import jax.numpy as jnp
from jax import lax
from jax.sharding import PartitionSpec as P

eps_norm = 1e-06


def slot_targets(routes, expert_count, capacity):
    flat = routes.reshape(-1)
    onehot = (flat[:, None] == jnp.arange(expert_count, dtype=jnp.int32)[None, :]).astype(jnp.int32)
    before = jnp.cumsum(onehot, axis=0) - onehot
    return flat * capacity + jnp.sum(before * onehot, axis=1)


def per_device(
    tokens,
    norm_gain,
    routes,
    route_prob,
    gate_weight,
    up_weight,
    down_weight,
    key_value_weight,
    key_value_target,
    concept_mask,
):
    token_rows, width = tokens.shape
    top_count = routes.shape[1]
    expert_count = lax.axis_size("expert")
    capacity = 5 * token_rows * top_count // (4 * expert_count)
    model_width = width * expert_count
    position = slot_targets(routes, expert_count, capacity)
    prob_flat = route_prob.reshape(-1)

    def place_rows(pair_rows):
        filled = (
            jnp.zeros((expert_count * capacity, width), jnp.bfloat16).at[position].set(pair_rows)
        )
        return filled.reshape(expert_count, capacity, width)

    values = tokens.astype(jnp.float32)
    total_sq = lax.psum(jnp.sum(values * values, axis=1), "expert")
    scale = lax.rsqrt(total_sq / model_width + eps_norm)
    local_gain = lax.dynamic_slice_in_dim(norm_gain, lax.axis_index("expert") * width, width)
    outgoing = (values * scale[:, None] * local_gain[None, :]).astype(jnp.bfloat16)
    send_slots = place_rows(jnp.repeat(outgoing, top_count, axis=0))
    arrived = lax.all_to_all(send_slots, "expert", split_axis=0, concat_axis=2, tiled=True)[0]
    rows = lax.all_gather(arrived, "dp", axis=0, tiled=True)
    gate_val = jnp.dot(rows, gate_weight[0], preferred_element_type=jnp.float32)
    up_val = jnp.dot(rows, up_weight[0], preferred_element_type=jnp.float32)
    hidden = (jax.nn.silu(gate_val) * up_val).astype(jnp.bfloat16)
    expert_out = lax.psum_scatter(
        jnp.dot(hidden, down_weight[0], preferred_element_type=jnp.float32).astype(jnp.bfloat16),
        "dp",
        scatter_dimension=0,
        tiled=True,
    )
    returned = lax.all_to_all(expert_out[None], "expert", split_axis=2, concat_axis=0, tiled=True)
    picked = returned.reshape(expert_count * capacity, width)[position].astype(jnp.float32)
    expert_mix = (picked * prob_flat[:, None]).reshape(token_rows, top_count, width).sum(axis=1)
    state = (tokens.astype(jnp.float32) + expert_mix).astype(jnp.bfloat16)
    proj_term = jnp.dot(state, key_value_weight, preferred_element_type=jnp.float32)
    proj_cols = lax.psum_scatter(
        proj_term.astype(jnp.bfloat16), "expert", scatter_dimension=1, tiled=True
    ).astype(jnp.float32)
    mask_col = concept_mask.astype(jnp.float32)[:, None]
    cotangent_cols = (
        mask_col * (proj_cols - key_value_target.astype(jnp.float32)) * token_rows ** (-0.5)
    ).astype(jnp.bfloat16)
    cotangent = lax.all_gather(cotangent_cols, "expert", axis=1, tiled=True)
    grad_term = jnp.einsum("tw,tk->wk", state, cotangent, preferred_element_type=jnp.float32)
    key_value_grad = lax.psum_scatter(
        grad_term.astype(jnp.bfloat16), "dp", scatter_dimension=1, tiled=True
    ).astype(jnp.float32)
    state_grad = jnp.einsum(
        "tk,wk->tw", cotangent, key_value_weight, preferred_element_type=jnp.float32
    )
    pair_grad = (jnp.repeat(state_grad, top_count, axis=0) * prob_flat[:, None]).astype(
        jnp.bfloat16
    )
    grad_slots = place_rows(pair_grad)
    landed = lax.all_to_all(grad_slots, "expert", split_axis=0, concat_axis=2, tiled=True)[0]
    down_total = jnp.einsum(
        "rf,rd->fd",
        hidden,
        lax.all_gather(landed, "dp", axis=0, tiled=True),
        preferred_element_type=jnp.float32,
    )
    return (down_total.astype(jnp.bfloat16)[None], key_value_grad)


def solution(mesh):
    placed = (
        P("dp", "expert"),
        P(),
        P("dp", None),
        P("dp", None),
        P("expert", None, "dp"),
        P("expert", None, "dp"),
        P("expert", "dp", None),
        P("expert", None),
        P("dp", "expert"),
        P("dp"),
    )
    return jax.shard_map(
        per_device,
        mesh=mesh,
        in_specs=placed,
        out_specs=(P("expert", "dp", None), P("expert", "dp")),
        check_vma=False,
    )
```

profile of v0, /device:TPU:6, one launch (start us, length us, event | category | flops | bytes accessed | tf_op | source)
XLA Modules:
  0.0 632.4 jit_solution(2933031377896465025)
XLA Ops:
  7.2 0.0 copy-start
  7.2 0.0 all-gather.5.cloned.1.call-start
  7.2 0.8 broadcast_multiply_fusion
  8.0 0.8 copy.34
  8.8 0.1 eq.29
  8.9 0.1 eq.25
  9.1 0.9 fusion.7
  9.9 53.2 %psum.7 = f32[128]{0:T(128)S(1)} all-reduce(f32[128]{0:T(128)S(1)} %fusion.7), channel_id=1, replica_groups=mesh['dp'=16,'expert'=32] {'expert'}, use_global_device_ids=true, to_apply=%region_4.5 | all-reduce | flops 128 | bytes 1024 | tf_op jit(solution)/shard_map/psum | solution.py:43
  63.1 0.1 copy.33
  63.2 0.1 mul.83
  63.4 0.6 reduce-window.6
  64.0 0.2 slice_reduce_fusion
  64.2 0.8 dynamic_slice.3
  65.0 0.8 fusion.9
  65.8 0.1 fusion.18
  66.0 1.2 scatter_custom_fusion
  67.2 24.1 %all_to_all.45 = bf16[32,10,128]{2,1,0:T(8,128)(2,1)S(1)} all-to-all(bf16[32,10,128]{2,1,0:T(8,128)(2,1)S(1)} %reshape.83), channel_id=1, replica_groups=mesh['dp'=16,'expert'=32] {'expert'}, dimensions={0} | all-to-all | bytes 163840 | tf_op jit(solution)/shard_map/all_to_all | solution.py:48
  91.4 0.7 reshape.112
  92.1 0.0 all-gather.5.cloned.1.call-update
  92.1 0.0 all-reduce.3.cloned.1.call-start
  92.2 74.7 %all-gather.5.cloned.1.call-done = bf16[16,10,4096]{2,1,0:T(8,128)(2,1)} async-done(((bf16[1,10,4096]{2,1,0:T(8,128)(2,1)}), bf16[16,10,4096]{2,1,0:T(8,128)(2,1)}) %all-gather.5.cloned.1.call-update) | async-done | bytes 1310736 | tf_op jit(solution)/shard_map/all_gather | solution.py:49
  166.9 1.8 reshape.113
  168.7 0.5 fusion.4
  169.2 0.7 copy-done.3
  169.9 0.5 fusion.1
  170.4 1.6 convolution_convert_fusion
  172.0 0.0 all-reduce.3.cloned.1.call-update
  172.1 0.1 copy.41
  172.2 1.3 dynamic-slice
  174.1 135.3 %all-reduce.3.cloned.1.call-done = bf16[160,4096]{1,0:T(8,128)(2,1)} async-done(((bf16[160,4096]{1,0:T(8,128)(2,1)}), bf16[160,4096]{1,0:T(8,128)(2,1)}) %all-reduce.3.cloned.1.call-update) | async-done | bytes 1310736
  309.4 1.0 dynamic-slice_bitcast_fusion
  310.3 2.8 copy.38
  313.2 0.5 broadcast.74
  313.7 23.4 %reduce.2 = bf16[4096,10]{1,0:T(8,128)(2,1)} reduce(bf16[4096,1,10]{2,1,0:T(2,128)(2,1)S(1)} %bitcast.74, bf16[]{:T(256)} %broadcast.74), dimensions={1}, to_apply=%bitcast.60.reduce_sub_computation | reduce | bytes 163842
  337.1 3.4 reshape.126
  340.5 7.4 %all-to-all-start.1 = ((bf16[32,2,640]{2,1,0:T(2,128)(2,1)}), bf16[32,2,640]{2,1,0:T(2,128)(2,1)S(1)}, u32[]{:S(2)}, u32[]{:S(2)}) async-start(bf16[32,2,640]{2,1,0:T(2,128)(2,1)} %reshape.126), calls=%async_computation.1 | async-start | bytes 163840 | tf_op jit(solution)/shard_map/all_to_all | solution.py:59
  347.9 0.0 reduce-scatter.5.cloned.1.call-start
  348.0 5.7 all-to-all-done.1
  353.7 2.2 reshape.127
  355.9 2.1 copy.39
  358.2 0.9 gather_fusion
  359.1 0.2 fusion.6
  359.4 1.1 convolution_convert_fusion.3
  360.5 0.0 reduce-scatter.5.cloned.1.call-update
  360.5 0.0 reduce-scatter.7.cloned.1.call-start
  360.6 94.3 %reduce-scatter.5.cloned.1.call-done = bf16[128,64]{0,1:T(8,128)(2,1)} async-done(((bf16[128,2048]{0,1:T(8,128)(2,1)}), bf16[128,64]{0,1:T(8,128)(2,1)}) %reduce-scatter.5.cloned.1.call-update) | async-done | bytes 16400 | tf_op jit(solution)/shard_map/reduce_scatter | solution.py:64
  454.9 0.7 multiply_convert_fusion.2
  455.7 22.6 %all_gather.10 = bf16[128,2048]{0,1:T(8,128)(2,1)S(1)} all-gather(bf16[128,64]{0,1:T(8,128)(2,1)S(1)} %multiply_convert_fusion.2), channel_id=1, replica_groups=mesh['dp'=16,'expert'=32] {'expert'}, dimensions={1}, use_global_device_ids=true | all-gather | bytes 540672 | tf_op jit(solution)/shard_map/all_gather | solution.py:71
  478.2 0.3 convolution_convert_fusion.2
  478.6 1.0 copy.44
  479.6 0.0 reduce-scatter.7.cloned.1.call-update
  479.6 0.0 all-gather.7.cloned.1.call-start
  479.6 0.1 mul.99
  479.8 0.3 fusion.22
  480.2 1.3 scatter_custom_fusion.1
  481.5 12.6 %all_to_all.46 = bf16[32,10,128]{2,1,0:T(8,128)(2,1)S(1)} all-to-all(bf16[32,10,128]{2,1,0:T(8,128)(2,1)S(1)} %reshape.86), channel_id=1, replica_groups=mesh['dp'=16,'expert'=32] {'expert'}, dimensions={0} | all-to-all | bytes 163840 | tf_op jit(solution)/shard_map/all_to_all | solution.py:83
  494.1 0.7 reshape.114
  494.8 0.0 all-gather.7.cloned.1.call-update
  494.9 54.7 %reduce-scatter.7.cloned.1.call-done = bf16[128,128]{1,0:T(8,128)(2,1)} async-done(((bf16[2048,128]{1,0:T(8,128)(2,1)}), bf16[128,128]{1,0:T(8,128)(2,1)}) %reduce-scatter.7.cloned.1.call-update) | async-done | bytes 32784
  549.6 0.9 copy.45
  550.5 0.6 convert_element_type.74
  551.1 71.5 %all-gather.7.cloned.1.call-done = bf16[16,10,4096]{2,1,0:T(8,128)(2,1)} async-done(((bf16[1,10,4096]{2,1,0:T(8,128)(2,1)}), bf16[16,10,4096]{2,1,0:T(8,128)(2,1)}) %all-gather.7.cloned.1.call-update) | async-done | bytes 1310736 | tf_op jit(solution)/shard_map/all_gather | solution.py:87
  622.6 1.8 reshape.115
  624.4 1.4 fusion
  (31 shorter events, 0.4 us)
Async XLA Ops:
  7.2 163.3 %copy-start = (bf16[1,128,4096]{2,1,0:T(8,128)(2,1)S(1)}, bf16[1,128,4096]{2,1,0:T(8,128)(2,1)}, u32[]{:S(2)}) copy-start(bf16[1,128,4096]{2,1,0:T(8,128)(2,1)} %param.16) | copy-start | bytes 3145732
  7.2 159.7 %all-gather.5.cloned.1.call-start = ((), (), s32[]{:S(2)}) async-start(), calls=%async_computation.6 | async-start | bytes 2228224 | tf_op jit(solution)/shard_map/all_gather | solution.py:49
  92.1 76.5 %copy-start.2 = (bf16[1,4096,128]{2,1,0:T(8,128)(2,1)S(1)}, bf16[1,4096,128]{2,1,0:T(8,128)(2,1)}, u32[]{:S(2)}) copy-start(bf16[1,4096,128]{2,1,0:T(8,128)(2,1)} %param.14) | copy-start | bytes 3145732
  92.1 217.2 %all-reduce.3.cloned.1.call-start = ((), (), s32[]{:S(2)}) async-start(), calls=%async_computation.9 | async-start | bytes 2621440
  168.7 1.2 copy-start.3
  170.4 1.6 copy-start.6
  340.5 13.2 %all-to-all-start.1 = ((bf16[32,2,640]{2,1,0:T(2,128)(2,1)}), bf16[32,2,640]{2,1,0:T(2,128)(2,1)S(1)}, u32[]{:S(2)}, u32[]{:S(2)}) async-start(bf16[32,2,640]{2,1,0:T(2,128)(2,1)} %reshape.126), calls=%async_computation.1 | async-start | bytes 163840 | tf_op jit(solution)/shard_map/all_to_all | solution.py:59
  347.9 107.0 %reduce-scatter.5.cloned.1.call-start = ((), (), s32[]{:S(2)}) async-start(), calls=%async_computation.5 | async-start | bytes 540672 | tf_op jit(solution)/shard_map/reduce_scatter | solution.py:64
  358.1 1.3 copy-start.1
  358.1 1.3 copy-start.4
  358.2 2.4 copy-start.7
  358.2 96.8 %copy-start.5 = (bf16[128,64]{0,1:T(8,128)(2,1)S(1)}, bf16[128,64]{0,1:T(8,128)(2,1)}, u32[]{:S(2)}) copy-start(bf16[128,64]{0,1:T(8,128)(2,1)} %param.18) | copy-start | bytes 49156
  360.5 189.1 %reduce-scatter.7.cloned.1.call-start = ((), (), s32[]{:S(2)}) async-start(), calls=%async_computation.8 | async-start | bytes 557056
  479.6 143.0 %all-gather.7.cloned.1.call-start = ((), (), s32[]{:S(2)}) async-start(), calls=%async_computation.7 | async-start | bytes 2228224 | tf_op jit(solution)/shard_map/all_gather | solution.py:87
Sparse Core Ops, SparseCore 0:
  92.2 74.5 all-gather.4
  172.2 137.1 all-reduce.2
  360.7 94.2 reduce-scatter.4
  479.7 69.8 reduce-scatter.6
  551.7 70.8 all-gather.6
where the time goes:
time: 633 us; the launch traced here: 632 us
  waiting for transfers between devices  436 us (69%)
  blocking collectives  113 us (18%)
  other arithmetic  29.5 us (5%)
  local copies, waits for them, and re-layouts  25.8 us (4%)
  between operations  14.8 us (2%)
  starting transfers between devices  7.61 us (1%)
    unnamed x7, waiting for transfers between devices  190 us
    reduce_scatter x1, waiting for transfers between devices, per_device(): lax.psum_scatter(proj_term.astype(jnp.bfloat16), 'expert', scatter_dimens...  94.3 us
    all_gather x1, waiting for transfers between devices, per_device(): rows = lax.all_gather(arrived, 'dp', axis=0, tiled=True)  74.7 us
    all_gather x1, waiting for transfers between devices, per_device(): lax.all_gather(landed, 'dp', axis=0, tiled=True)  71.5 us
    psum x1, blocking collectives, per_device(): total_sq = lax.psum(jnp.sum(values * values, axis=1), 'expert')  53.2 us
    all_to_all x1, blocking collectives, per_device(): lax.all_to_all(send_slots, 'expert', split_axis=0, concat_axis=2, tiled=T...  24.1 us
    unnamed x1, other arithmetic  23.4 us
    all_gather x1, blocking collectives, per_device(): cotangent = lax.all_gather(cotangent_cols, 'expert', axis=1, tiled=True)  22.6 us
  transfers between devices with their start and end apart: 6, of which 6 were waited for; matrix products, arithmetic and copies ran while one was open for 1% of the time, Pallas kernels for 0%

commit v1 on v0

v1 whole, which is shorter than its diff:
```python
import jax
import jax.numpy as jnp
from jax import lax
from jax.experimental import pallas as pl
from jax.experimental.pallas import tpu as pltpu
from jax.sharding import PartitionSpec as P

f32 = jnp.float32
bf16 = jnp.bfloat16
eps_norm = 1e-06
meta_rows = 16
group = 4


def call(body, outs, *operands):
    vmem = pl.BlockSpec(memory_space=pltpu.VMEM)
    single = not isinstance(outs, (list, tuple))
    return pl.pallas_call(
        body,
        out_shape=outs,
        in_specs=[vmem] * len(operands),
        out_specs=vmem if single else [vmem] * len(outs),
        compiler_params=pltpu.CompilerParams(vmem_limit_bytes=56 * 1024 * 1024),
    )(*operands)


def iota(shape, axis):
    return lax.broadcasted_iota(jnp.int32, shape, axis)


def contract(a, b, da, db):
    return lax.dot_general(a, b, (((da,), (db,)), ((), ())), preferred_element_type=f32)


def prepare(tok_ref, routes_ref, prob_ref, out_ref):
    rows, experts = tok_ref.shape[0], 32
    out_ref[0:rows, :] = tok_ref[...]
    lane = iota((rows, rows), 1)
    routes = routes_ref[...].astype(f32)
    prob = prob_ref[...]
    table = jnp.where(
        lane == 0,
        routes[:, 0:1],
        jnp.where(
            lane == 1,
            routes[:, 1:2],
            jnp.where(lane == 2, prob[:, 0:1], jnp.where(lane == 3, prob[:, 1:2], 0.0)),
        ),
    )
    table = table.T
    first, second = table[0:1, :], table[1:2, :]
    names = iota((experts, rows), 0).astype(f32)
    is_first, is_second = names == first, names == second
    named = jnp.where(is_first | is_second, 1.0, 0.0).astype(bf16)
    earlier = jnp.where(iota((rows, rows), 0) < lane, 1.0, 0.0).astype(bf16)
    before = jnp.dot(named, earlier, preferred_element_type=f32)
    slot_first = jnp.sum(jnp.where(is_first, before, 0.0), axis=0, keepdims=True)
    slot_second = jnp.sum(jnp.where(is_second, before, 0.0), axis=0, keepdims=True)
    row = iota((meta_rows, rows), 0)
    meta = jnp.where(
        row == 0,
        first,
        jnp.where(
            row == 1,
            second,
            jnp.where(
                row == 2,
                slot_first,
                jnp.where(
                    row == 3,
                    slot_second,
                    jnp.where(row == 4, table[2:3, :], jnp.where(row == 5, table[3:4, :], 0.0)),
                ),
            ),
        ),
    )
    out_ref[rows : rows + meta_rows, :] = meta.astype(bf16)


def selection(meta, inner, capacity, weighted):
    tall = group * capacity
    at = [
        (meta[k : k + 1] * tall + inner * capacity + meta[2 + k : 3 + k]).astype(jnp.int32)
        for k in (0, 1)
    ]
    slots = iota((32 * tall, meta.shape[1]), 0)
    if weighted:
        picked = jnp.where(slots == at[0], meta[4:5], jnp.where(slots == at[1], meta[5:6], 0.0))
    else:
        picked = jnp.where((slots == at[0]) | (slots == at[1]), 1.0, 0.0)
    return picked.astype(bf16)


def block_meta(gathered_ref, block, rows):
    return gathered_ref[block, rows : rows + meta_rows, :].astype(f32)


def dispatch(gathered_ref, out_ref):
    blocks, rows = gathered_ref.shape[0], gathered_ref.shape[1] - meta_rows
    capacity = out_ref.shape[1] // blocks
    tall = group * capacity
    for g in range(blocks // group):
        total = 0.0
        for inner in range(group):
            block = g * group + inner
            chosen = selection(block_meta(gathered_ref, block, rows), inner, capacity, False)
            total = total + jnp.dot(
                chosen, gathered_ref[block, 0:rows, :], preferred_element_type=f32
            )
        for e in range(out_ref.shape[0]):
            out_ref[e, g * tall : (g + 1) * tall, :] = total[e * tall : (e + 1) * tall].astype(bf16)


def dispatch_grad(gathered_ref, grad_ref, out_ref):
    blocks, rows = gathered_ref.shape[0], gathered_ref.shape[1] - meta_rows
    capacity = out_ref.shape[1] // blocks
    tall = group * capacity
    for g in range(blocks // group):
        total = 0.0
        for inner in range(group):
            block = g * group + inner
            chosen = selection(block_meta(gathered_ref, block, rows), inner, capacity, True)
            total = total + contract(chosen, grad_ref[block], 1, 1)
        for e in range(out_ref.shape[0]):
            out_ref[e, g * tall : (g + 1) * tall, :] = total[e * tall : (e + 1) * tall].astype(bf16)


def expert(rows_ref, gain_ref, gate_ref, up_ref, down_ref, out_ref, hidden_ref):
    parts, width = rows_ref.shape[0], rows_ref.shape[2]
    values = jnp.concatenate([rows_ref[p] for p in range(parts)], axis=1).astype(f32)
    mean_sq = jnp.sum(values * values, axis=1, keepdims=True) / (parts * width)
    normed = (values * lax.rsqrt(mean_sq + eps_norm) * gain_ref[...]).astype(bf16)
    gate_val = jnp.dot(normed, gate_ref[...], preferred_element_type=f32)
    up_val = jnp.dot(normed, up_ref[...], preferred_element_type=f32)
    hidden = (gate_val / (1.0 + jnp.exp(-gate_val)) * up_val).astype(bf16)
    hidden_ref[...] = hidden
    product = jnp.dot(hidden, down_ref[...], preferred_element_type=f32)
    for p in range(parts):
        out_ref[p] = product[:, p * width : (p + 1) * width].astype(bf16)


def combine(gathered_ref, back_ref, out_ref):
    blocks, rows = gathered_ref.shape[0], gathered_ref.shape[1] - meta_rows
    capacity = back_ref.shape[1] // blocks
    tall = group * capacity
    for g in range(blocks // group):
        back = jnp.concatenate(
            [back_ref[e, g * tall : (g + 1) * tall, :].astype(f32) for e in range(back_ref.shape[0])],
            axis=0,
        )
        back = back.T.astype(bf16)
        for inner in range(group):
            block = g * group + inner
            chosen = selection(block_meta(gathered_ref, block, rows), inner, capacity, True)
            out_ref[block] = jnp.dot(back, chosen, preferred_element_type=f32).astype(bf16)


def project(pieces_ref, tok_ref, weight_ref, state_ref, out_ref):
    total = tok_ref[...].astype(f32).T
    for p in range(pieces_ref.shape[0]):
        total = total + pieces_ref[p].astype(f32)
    state = total.astype(bf16)
    state_ref[...] = state
    out_ref[...] = contract(weight_ref[...], state, 0, 0).astype(bf16)


def form_cotangent(pieces_ref, target_ref, mask_ref, out_ref):
    total = pieces_ref[0].astype(f32)
    for p in range(1, pieces_ref.shape[0]):
        total = total + pieces_ref[p].astype(f32)
    target = target_ref[...].astype(f32)
    rows = target.shape[0]
    target = jnp.concatenate([target, target], axis=1).T[0 : target.shape[1]]
    scaled = mask_ref[...].astype(f32) * (total - target) * rows ** (-0.5)
    scaled = scaled.astype(bf16)
    for p in range(out_ref.shape[0]):
        out_ref[p] = scaled


def gradients(cot_ref, state_ref, weight_ref, state_grad_ref, pieces_ref):
    state_grad_ref[...] = jnp.dot(
        weight_ref[...], cot_ref[...], preferred_element_type=f32
    ).astype(bf16)
    state = state_ref[...]
    width = cot_ref.shape[0] // pieces_ref.shape[0]
    for p in range(pieces_ref.shape[0]):
        pieces_ref[p] = contract(state, cot_ref[p * width : (p + 1) * width, :], 1, 1).astype(bf16)


def down_gradient(hidden_ref, rows_ref, out_ref):
    hidden = hidden_ref[...].astype(f32).T.astype(bf16)
    width = rows_ref.shape[2]
    for p in range(rows_ref.shape[0]):
        out_ref[:, p * width : (p + 1) * width] = jnp.dot(
            hidden, rows_ref[p], preferred_element_type=f32
        ).astype(bf16)


def per_device(
    tokens,
    norm_gain,
    routes,
    route_prob,
    gate_weight,
    up_weight,
    down_weight,
    key_value_weight,
    key_value_target,
    concept_mask,
):
    rows, width = tokens.shape
    experts = lax.axis_size("expert")
    blocks = lax.axis_size("dp")
    capacity = 5 * rows * routes.shape[1] // (4 * experts)
    keys = key_value_weight.shape[1]

    def shape(*dims, dtype=bf16):
        return jax.ShapeDtypeStruct(dims, dtype)

    def exchange(value, axis):
        return lax.all_to_all(value, axis, split_axis=0, concat_axis=0, tiled=True)

    packed = call(prepare, shape(rows + meta_rows, width), tokens, routes, route_prob)
    gathered = lax.all_gather(packed, "dp", axis=0)
    slots = shape(experts, blocks * capacity, width)
    arrived = exchange(call(dispatch, slots, gathered), "expert")
    out_rows, hidden = call(
        expert,
        [slots, shape(blocks * capacity, gate_weight.shape[2])],
        arrived,
        norm_gain[None, :],
        gate_weight[0],
        up_weight[0],
        down_weight[0],
    )
    returned = exchange(out_rows, "expert")
    mixed = exchange(call(combine, shape(blocks, width, rows), gathered, returned), "dp")
    state, proj = call(
        project, [shape(width, rows), shape(keys, rows)], mixed, tokens, key_value_weight
    )
    proj = exchange(proj.reshape(experts, keys // experts, rows), "expert")
    spread = call(form_cotangent, shape(*proj.shape), proj, key_value_target, concept_mask[None, :])
    cotangent = exchange(spread, "expert").reshape(keys, rows)
    state_grad, pieces = call(
        gradients,
        [shape(width, rows), shape(blocks, width, keys // blocks)],
        cotangent,
        state,
        key_value_weight,
    )
    key_value_grad = lax.psum_scatter(pieces, "dp", scatter_dimension=0, tiled=True)[0].astype(f32)
    all_grads = lax.all_gather(state_grad, "dp", axis=0)
    landed = exchange(call(dispatch_grad, slots, gathered, all_grads), "expert")
    down_grad = call(down_gradient, shape(*down_weight.shape[1:]), hidden, landed)
    return (down_grad[None], key_value_grad)


def solution(mesh):
    placed = (
        P("dp", "expert"),
        P(),
        P("dp", None),
        P("dp", None),
        P("expert", None, "dp"),
        P("expert", None, "dp"),
        P("expert", "dp", None),
        P("expert", None),
        P("dp", "expert"),
        P("dp"),
    )
    return jax.shard_map(
        per_device,
        mesh=mesh,
        in_specs=placed,
        out_specs=(P("expert", "dp", None), P("expert", "dp")),
        check_vma=False,
    )
```

time: 633 us -> 274 us (0.43)
  waiting for transfers between devices: 436 us -> 24.8 us
  blocking collectives: 113 us -> 181 us
  Pallas kernels: 0 us -> 31.3 us
  other arithmetic: 29.5 us -> 1.39 us
  local copies, waits for them, and re-layouts: 25.8 us -> 5.43 us
    unnamed x7 -> x1, waiting for transfers between devices: 190 us -> 0.02 us
    all_gather x2 -> x0, waiting for transfers between devices: 146 us -> none  [the longest x1 74.7 us: per_device(): rows = lax.all_gather(arrived, 'dp', axis=0, tiled=True)]
    reduce_scatter x1, waiting for transfers between devices: 94.3 us -> 16.1 us  [per_device(): lax.psum_scatter(pieces, 'dp', scatter_dimension=0, tiled=True)[0]]
    all_to_all x2 -> x4, blocking collectives: 36.8 us -> 103 us  [exchange(): return lax.all_to_all(value, axis, split_axis=0, concat_axis=0, tiled=True)]
    all_gather x1 -> x2, blocking collectives: 22.6 us -> 78 us  [the longest x1 41.2 us: per_device(): gathered = lax.all_gather(packed, 'dp', axis=0)]
    psum x1 -> x0, blocking collectives: 53.2 us -> none  [per_device(): total_sq = lax.psum(jnp.sum(values * values, axis=1), 'expert')]
    pallas_call x0 -> x9, Pallas kernels: none -> 31.3 us  [call(): pl.pallas_call(body, out_shape=outs, in_specs=[vmem] * len(operands), out...]
    unnamed x1 -> x0, other arithmetic: 23.4 us -> none
  transfers between devices with their start and end apart: 6 -> 3, of which waited for: 6 -> 2; matrix products, arithmetic and copies ran while one was open for 1% -> 1% of each run, Pallas kernels for 0% -> 2%
where the time goes in v1:
time: 274 us; the launch traced here: 270 us
  blocking collectives  181 us (66%)
  Pallas kernels  31.3 us (11%)
  waiting for transfers between devices  24.8 us (9%)
  between operations  14.1 us (5%)
  starting transfers between devices  12.3 us (4%)
  local copies, waits for them, and re-layouts  5.43 us (2%)
    all_to_all x4, blocking collectives, exchange(): return lax.all_to_all(value, axis, split_axis=0, concat_axis=0, tiled=True)  103 us
    all_gather x1, blocking collectives, per_device(): gathered = lax.all_gather(packed, 'dp', axis=0)  41.2 us
    all_gather x1, blocking collectives, per_device(): all_grads = lax.all_gather(state_grad, 'dp', axis=0)  36.8 us
    pallas_call x9, Pallas kernels, call(): pl.pallas_call(body, out_shape=outs, in_specs=[vmem] * len(operands), out...  31.3 us
    reduce_scatter x1, waiting for transfers between devices, per_device(): lax.psum_scatter(pieces, 'dp', scatter_dimension=0, tiled=True)[0]  16.1 us
    all_to_all x2, starting transfers between devices, exchange(): return lax.all_to_all(value, axis, split_axis=0, concat_axis=0, tiled=True)  12.3 us
    all_to_all x2, waiting for transfers between devices, exchange(): return lax.all_to_all(value, axis, split_axis=0, concat_axis=0, tiled=True)  8.67 us
  transfers between devices with their start and end apart: 3, of which 2 were waited for; matrix products, arithmetic and copies ran while one was open for 1% of the time, Pallas kernels for 2%

profile of v1, /device:TPU:6, one launch (start us, length us, event | category | flops | bytes accessed | tf_op | source)
XLA Modules:
  0.0 270.4 jit_solution(5358084307534397755)
XLA Ops:
  7.2 1.4 copy.12.routes_ref
  8.6 1.4 copy.13.prob_ref
  10.0 1.8 shard_map.113
  11.8 41.2 %all-gather = bf16[2304,128]{1,0:T(8,128)(2,1)} all-gather(bf16[144,128]{1,0:T(8,128)(2,1)} %shard_map.113), channel_id=2, replica_groups=mesh['dp'=16,'expert'=32] {'dp'}, dimensions={0}, use_global_device_ids=true | all-gather | bytes 626688 | tf_op jit(solution)/shard_map/all_gather | solution.py:224
  53.1 4.3 %shard_map.114 = bf16[32,160,128]{2,1,0:T(8,128)(2,1)} custom-call(bf16[16,144,128]{2,1,0:T(8,128)(2,1)} %bitcast.13), custom_call_target="tpu_custom_call" | custom-call | tf_op jit(solution)/shard_map/pallas_call | solution.py:18
  57.4 25.9 %all_to_all.30.rows_ref = bf16[32,160,128]{2,1,0:T(8,128)(2,1)} all-to-all(bf16[32,160,128]{2,1,0:T(8,128)(2,1)} %shard_map.114), channel_id=1, replica_groups=mesh['dp'=16,'expert'=32] {'expert'}, dimensions={0} | all-to-all | bytes 2621440 | tf_op jit(solution)/shard_map/all_to_all | solution.py:221
  83.3 4.8 %shard_map.115 = (bf16[32,160,128]{2,1,0:T(8,128)(2,1)}, bf16[160,128]{1,0:T(8,128)(2,1)}) custom-call(bf16[32,160,128]{2,1,0:T(8,128)(2,1)} %all_to_all.30.rows_ref, f32[1,4096]{1,0:T(1,128)} %bitcast.23, bf16[4096,128]{1,0:T(8,128)(2,1)} %bitcast.18, bf16[4096,128]{1,0:T(8,128)(2,1)} %bitcast.19, bf16[128,4096]{1,0:T(8,128)(2,1)} %bitcast.20), custom_call_target="tpu_custom_call" | custom-call | tf_op jit(solution)/shard_map/pallas_call | solution.py:18
  88.1 24.8 %all_to_all.31.back_ref = bf16[32,160,128]{2,1,0:T(8,128)(2,1)} all-to-all(bf16[32,160,128]{2,1,0:T(8,128)(2,1)} %get-tuple-element.9), channel_id=1, replica_groups=mesh['dp'=16,'expert'=32] {'expert'}, dimensions={0} | all-to-all | bytes 2621440 | tf_op jit(solution)/shard_map/all_to_all | solution.py:221
  112.9 5.5 %shard_map.116 = bf16[16,128,128]{2,1,0:T(8,128)(2,1)} custom-call(bf16[16,144,128]{2,1,0:T(8,128)(2,1)} %bitcast.14, bf16[32,160,128]{2,1,0:T(8,128)(2,1)} %all_to_all.31.back_ref), custom_call_target="tpu_custom_call" | custom-call | tf_op jit(solution)/shard_map/pallas_call | solution.py:18
  118.4 36.1 %all_to_all.32.pieces_ref = bf16[16,128,128]{2,1,0:T(8,128)(2,1)} all-to-all(bf16[16,128,128]{2,1,0:T(8,128)(2,1)} %shard_map.116), channel_id=1, replica_groups=mesh['dp'=16,'expert'=32] {'dp'}, dimensions={0} | all-to-all | bytes 1048576 | tf_op jit(solution)/shard_map/all_to_all | solution.py:221
  154.5 0.0 copy-start.2
  154.5 2.5 shard_map.117
  157.0 6.0 %all-to-all-start.3 = ((bf16[32,64,128]{2,1,0:T(8,128)(2,1)}), bf16[32,64,128]{2,1,0:T(8,128)(2,1)S(1)}, u32[]{:S(2)}, u32[]{:S(2)}) async-start(bf16[32,64,128]{2,1,0:T(8,128)(2,1)} %bitcast.22), calls=%async_computation.3 | async-start | bytes 1048576 | tf_op jit(solution)/shard_map/all_to_all | solution.py:221
  162.9 0.0 reduce-scatter.2.cloned.1.call-start
  163.0 0.0 copy-done.2
  163.0 0.7 copy.14.target_ref
  163.7 8.7 %all-to-all-done.3.pieces_ref = bf16[32,64,128]{2,1,0:T(8,128)(2,1)S(1)} async-done(((bf16[32,64,128]{2,1,0:T(8,128)(2,1)}), bf16[32,64,128]{2,1,0:T(8,128)(2,1)S(1)}, u32[]{:S(2)}, u32[]{:S(2)}) %all-to-all-start.3) | async-done | bytes 524320 | tf_op jit(solution)/shard_map/all_to_all | solution.py:221
  172.4 0.0 copy-start.1
  172.4 0.8 copy-done.1
  173.2 2.1 shard_map.118
  175.2 16.3 %all_to_all.33 = bf16[32,64,128]{2,1,0:T(8,128)(2,1)} all-to-all(bf16[32,64,128]{2,1,0:T(8,128)(2,1)} %shard_map.118), channel_id=1, replica_groups=mesh['dp'=16,'expert'=32] {'expert'}, dimensions={0} | all-to-all | bytes 1048576 | tf_op jit(solution)/shard_map/all_to_all | solution.py:221
  191.6 2.6 shard_map.119
  194.2 0.0 reduce-scatter.2.cloned.1.call-update
  194.2 36.8 %all-gather.1 = bf16[2048,128]{1,0:T(8,128)(2,1)} all-gather(bf16[128,128]{1,0:T(8,128)(2,1)} %get-tuple-element.12), channel_id=3, replica_groups=mesh['dp'=16,'expert'=32] {'dp'}, dimensions={0}, use_global_device_ids=true | all-gather | bytes 557056 | tf_op jit(solution)/shard_map/all_gather | solution.py:252
  231.0 4.6 %shard_map.120 = bf16[32,160,128]{2,1,0:T(8,128)(2,1)} custom-call(bf16[16,144,128]{2,1,0:T(8,128)(2,1)} %bitcast.15, bf16[16,128,128]{2,1,0:T(8,128)(2,1)} %bitcast.16), custom_call_target="tpu_custom_call" | custom-call | tf_op jit(solution)/shard_map/pallas_call | solution.py:18
  235.6 6.3 %all-to-all-start.5 = ((bf16[32,160,128]{2,1,0:T(8,128)(2,1)}), bf16[32,160,128]{2,1,0:T(8,128)(2,1)S(1)}, u32[]{:S(2)}, u32[]{:S(2)}) async-start(bf16[32,160,128]{2,1,0:T(8,128)(2,1)} %shard_map.120), calls=%async_computation.5 | async-start | bytes 2621440 | tf_op jit(solution)/shard_map/all_to_all | solution.py:221
  241.9 16.1 %reduce-scatter.2.cloned.1.call-done = bf16[1,128,128]{2,1,0:T(8,128)(2,1)} async-done(((bf16[16,128,128]{2,1,0:T(8,128)(2,1)}), bf16[1,128,128]{2,1,0:T(8,128)(2,1)}) %reduce-scatter.2.cloned.1.call-update) | async-done | bytes 32784 | tf_op jit(solution)/shard_map/reduce_scatter | solution.py:251
  258.1 1.4 bitcast_convert_fusion
  259.4 0.0 all-to-all-done.5.rows_ref
  259.4 0.0 copy-start
  259.4 1.1 copy-done
  260.5 3.1 %shard_map.121 = bf16[128,4096]{1,0:T(8,128)(2,1)} custom-call(bf16[160,128]{1,0:T(8,128)(2,1)} %get-tuple-element.8.hidden_ref, bf16[32,160,128]{2,1,0:T(8,128)(2,1)} %copy-done), custom_call_target="tpu_custom_call" | custom-call | tf_op jit(solution)/shard_map/pallas_call | solution.py:18
Async XLA Ops:
  154.5 8.5 %copy-start.2 = (bf16[128,64]{0,1:T(8,128)(2,1)S(1)}, bf16[128,64]{0,1:T(8,128)(2,1)}, u32[]{:S(2)}) copy-start(bf16[128,64]{0,1:T(8,128)(2,1)} %param.18) | copy-start | bytes 49156
  157.0 15.4 %all-to-all-start.3 = ((bf16[32,64,128]{2,1,0:T(8,128)(2,1)}), bf16[32,64,128]{2,1,0:T(8,128)(2,1)S(1)}, u32[]{:S(2)}, u32[]{:S(2)}) async-start(bf16[32,64,128]{2,1,0:T(8,128)(2,1)} %bitcast.22), calls=%async_computation.3 | async-start | bytes 1048576 | tf_op jit(solution)/shard_map/all_to_all | solution.py:221
  162.9 95.1 %reduce-scatter.2.cloned.1.call-start = ((), (), s32[]{:S(2)}) async-start(), calls=%async_computation.7 | async-start | bytes 557056 | tf_op jit(solution)/shard_map/reduce_scatter | solution.py:251
  172.4 0.8 copy-start.1
  235.6 23.8 %all-to-all-start.5 = ((bf16[32,160,128]{2,1,0:T(8,128)(2,1)}), bf16[32,160,128]{2,1,0:T(8,128)(2,1)S(1)}, u32[]{:S(2)}, u32[]{:S(2)}) async-start(bf16[32,160,128]{2,1,0:T(8,128)(2,1)} %shard_map.120), calls=%async_computation.5 | async-start | bytes 2621440 | tf_op jit(solution)/shard_map/all_to_all | solution.py:221
  259.4 1.1 copy-start
Sparse Core Ops, SparseCore 0:
  194.3 63.6 reduce-scatter.1

commit v2 on v1

--- a/solution.py
+++ b/solution.py
@@ -12,7 +12,7 @@
 group = 4
 
 
-def call(body, outs, *operands):
+def call(body, outs, *operands, limit=16):
     vmem = pl.BlockSpec(memory_space=pltpu.VMEM)
     single = not isinstance(outs, (list, tuple))
     return pl.pallas_call(
@@ -20,7 +20,7 @@
         out_shape=outs,
         in_specs=[vmem] * len(operands),
         out_specs=vmem if single else [vmem] * len(outs),
-        compiler_params=pltpu.CompilerParams(vmem_limit_bytes=56 * 1024 * 1024),
+        compiler_params=pltpu.CompilerParams(vmem_limit_bytes=limit * 1024 * 1024),
     )(*operands)
 
 
@@ -35,24 +35,12 @@
 def prepare(tok_ref, routes_ref, prob_ref, out_ref):
     rows, experts = tok_ref.shape[0], 32
     out_ref[0:rows, :] = tok_ref[...]
-    lane = iota((rows, rows), 1)
     routes = routes_ref[...].astype(f32)
-    prob = prob_ref[...]
-    table = jnp.where(
-        lane == 0,
-        routes[:, 0:1],
-        jnp.where(
-            lane == 1,
-            routes[:, 1:2],
-            jnp.where(lane == 2, prob[:, 0:1], jnp.where(lane == 3, prob[:, 1:2], 0.0)),
-        ),
-    )
-    table = table.T
-    first, second = table[0:1, :], table[1:2, :]
+    first, second = routes[0:1, :], routes[1:2, :]
     names = iota((experts, rows), 0).astype(f32)
     is_first, is_second = names == first, names == second
     named = jnp.where(is_first | is_second, 1.0, 0.0).astype(bf16)
-    earlier = jnp.where(iota((rows, rows), 0) < lane, 1.0, 0.0).astype(bf16)
+    earlier = jnp.where(iota((rows, rows), 0) < iota((rows, rows), 1), 1.0, 0.0).astype(bf16)
     before = jnp.dot(named, earlier, preferred_element_type=f32)
     slot_first = jnp.sum(jnp.where(is_first, before, 0.0), axis=0, keepdims=True)
     slot_second = jnp.sum(jnp.where(is_second, before, 0.0), axis=0, keepdims=True)
@@ -69,7 +57,7 @@
                 jnp.where(
                     row == 3,
                     slot_second,
-                    jnp.where(row == 4, table[2:3, :], jnp.where(row == 5, table[3:4, :], 0.0)),
+                    jnp.where(row == 4, prob_ref[0:1, :], jnp.where(row == 5, prob_ref[1:2, :], 0.0)),
                 ),
             ),
         ),
@@ -169,9 +157,7 @@
     for p in range(1, pieces_ref.shape[0]):
         total = total + pieces_ref[p].astype(f32)
     target = target_ref[...].astype(f32)
-    rows = target.shape[0]
-    target = jnp.concatenate([target, target], axis=1).T[0 : target.shape[1]]
-    scaled = mask_ref[...].astype(f32) * (total - target) * rows ** (-0.5)
+    scaled = mask_ref[...].astype(f32) * (total - target) * target.shape[1] ** (-0.5)
     scaled = scaled.astype(bf16)
     for p in range(out_ref.shape[0]):
         out_ref[p] = scaled
@@ -220,7 +206,7 @@
     def exchange(value, axis):
         return lax.all_to_all(value, axis, split_axis=0, concat_axis=0, tiled=True)
 
-    packed = call(prepare, shape(rows + meta_rows, width), tokens, routes, route_prob)
+    packed = call(prepare, shape(rows + meta_rows, width), tokens, routes.T, route_prob.T)
     gathered = lax.all_gather(packed, "dp", axis=0)
     slots = shape(experts, blocks * capacity, width)
     arrived = exchange(call(dispatch, slots, gathered), "expert")
@@ -232,6 +218,7 @@
         gate_weight[0],
         up_weight[0],
         down_weight[0],
+        limit=24,
     )
     returned = exchange(out_rows, "expert")
     mixed = exchange(call(combine, shape(blocks, width, rows), gathered, returned), "dp")
@@ -239,7 +226,9 @@
         project, [shape(width, rows), shape(keys, rows)], mixed, tokens, key_value_weight
     )
     proj = exchange(proj.reshape(experts, keys // experts, rows), "expert")
-    spread = call(form_cotangent, shape(*proj.shape), proj, key_value_target, concept_mask[None, :])
+    spread = call(
+        form_cotangent, shape(*proj.shape), proj, key_value_target.T, concept_mask[None, :]
+    )
     cotangent = exchange(spread, "expert").reshape(keys, rows)
     state_grad, pieces = call(
         gradients,

time: 274 us -> 247 us (0.901)
  Pallas kernels: 31.3 us -> 14.1 us
  blocking collectives: 181 us -> 188 us
  starting transfers between devices: 12.3 us -> 6.64 us
  waiting for transfers between devices: 24.8 us -> 19.6 us
  local copies, waits for them, and re-layouts: 5.43 us -> 2.15 us
    pallas_call x9, Pallas kernels: 31.3 us -> 14.1 us  [call(): pl.pallas_call(body, out_shape=outs, in_specs=[vmem] * len(operands), out...]
    all_to_all x4 -> x5, blocking collectives: 103 us -> 115 us  [exchange(): return lax.all_to_all(value, axis, split_axis=0, concat_axis=0, tiled=True)]
    all_to_all x2 -> x1, waiting for transfers between devices: 8.67 us -> 0.01 us  [exchange(): return lax.all_to_all(value, axis, split_axis=0, concat_axis=0, tiled=True)]
    all_to_all x2 -> x1, starting transfers between devices: 12.3 us -> 6.6 us  [exchange(): return lax.all_to_all(value, axis, split_axis=0, concat_axis=0, tiled=True)]
    reduce_scatter x1, waiting for transfers between devices: 16.1 us -> 19.5 us  [per_device(): lax.psum_scatter(pieces, 'dp', scatter_dimension=0, tiled=True)[0]]
    unnamed x9 -> x22, local copies, waits for them, and re-layouts: 5.43 us -> 2.15 us
  transfers between devices with their start and end apart: 3 -> 2, of which waited for: 2 -> 1; matrix products, arithmetic and copies ran while one was open for 1% -> 1% of each run, Pallas kernels for 2% -> 1%
where the time goes in v2:
time: 247 us; the launch traced here: 246 us
  blocking collectives  188 us (76%)
  waiting for transfers between devices  19.6 us (8%)
  Pallas kernels  14.1 us (6%)
  between operations  14.1 us (6%)
  starting transfers between devices  6.64 us (3%)
    all_to_all x5, blocking collectives, exchange(): return lax.all_to_all(value, axis, split_axis=0, concat_axis=0, tiled=True)  115 us
    all_gather x1, blocking collectives, per_device(): gathered = lax.all_gather(packed, 'dp', axis=0)  38.9 us
    all_gather x1, blocking collectives, per_device(): all_grads = lax.all_gather(state_grad, 'dp', axis=0)  34.2 us
    reduce_scatter x1, waiting for transfers between devices, per_device(): lax.psum_scatter(pieces, 'dp', scatter_dimension=0, tiled=True)[0]  19.5 us
    pallas_call x9, Pallas kernels, call(): pl.pallas_call(body, out_shape=outs, in_specs=[vmem] * len(operands), out...  14.1 us
    all_to_all x1, starting transfers between devices, exchange(): return lax.all_to_all(value, axis, split_axis=0, concat_axis=0, tiled=True)  6.6 us
  transfers between devices with their start and end apart: 2, of which 1 were waited for; matrix products, arithmetic and copies ran while one was open for 1% of the time, Pallas kernels for 1%

profile of v2, /device:TPU:6, one launch (start us, length us, event | category | flops | bytes accessed | tf_op | source)
XLA Modules:
  0.0 245.9 jit_solution(9459424725893830722)
XLA Ops:
  7.2 0.0 reduce-scatter.2.cloned.1.call-start
  7.2 0.0 copy-start.4
  7.2 0.7 copy-done.4
  8.0 0.0 copy-start.8
  8.0 0.7 copy-done.8
  8.7 0.0 copy-start.9
  8.7 0.7 copy-done.9
  9.3 0.1 shard_map.113
  9.5 38.9 %all-gather = bf16[2304,128]{1,0:T(8,128)(2,1)S(1)} all-gather(bf16[144,128]{1,0:T(8,128)(2,1)S(1)} %shard_map.113), channel_id=2, replica_groups=mesh['dp'=16,'expert'=32] {'dp'}, dimensions={0}, use_global_device_ids=true | all-gather | bytes 626688 | tf_op jit(solution)/shard_map/all_gather | solution.py:210
  48.3 0.0 copy-start.3
  48.3 2.2 shard_map.114
  50.5 0.0 copy-start.1
  50.5 0.0 copy-start.2
  50.5 0.0 copy-start.6
  50.6 25.7 %all_to_all.30.rows_ref = bf16[32,160,128]{2,1,0:T(8,128)(2,1)S(1)} all-to-all(bf16[32,160,128]{2,1,0:T(8,128)(2,1)S(1)} %shard_map.114), channel_id=1, replica_groups=mesh['dp'=16,'expert'=32] {'expert'}, dimensions={0} | all-to-all | bytes 2621440 | tf_op jit(solution)/shard_map/all_to_all | solution.py:207
  76.3 0.0 copy-done.3
  76.3 0.0 copy-done.1
  76.3 0.0 copy-done.2
  76.3 0.0 copy-done.6
  76.3 1.5 shard_map.115
  77.8 23.7 %all_to_all.31.back_ref = bf16[32,160,128]{2,1,0:T(8,128)(2,1)S(1)} all-to-all(bf16[32,160,128]{2,1,0:T(8,128)(2,1)S(1)} %get-tuple-element.9), channel_id=1, replica_groups=mesh['dp'=16,'expert'=32] {'expert'}, dimensions={0} | all-to-all | bytes 2621440 | tf_op jit(solution)/shard_map/all_to_all | solution.py:207
  101.5 0.0 copy-start
  101.5 0.0 copy-start.5
  101.5 3.2 %shard_map.116 = bf16[16,128,128]{2,1,0:T(8,128)(2,1)S(1)} custom-call(bf16[16,144,128]{2,1,0:T(8,128)(2,1)S(1)} %bitcast.17, bf16[32,160,128]{2,1,0:T(8,128)(2,1)S(1)} %all_to_all.31.back_ref), custom_call_target="tpu_custom_call" | custom-call | tf_op jit(solution)/shard_map/pallas_call | solution.py:18
  104.8 35.3 %all_to_all.32.pieces_ref = bf16[16,128,128]{2,1,0:T(8,128)(2,1)S(1)} all-to-all(bf16[16,128,128]{2,1,0:T(8,128)(2,1)S(1)} %shard_map.116), channel_id=1, replica_groups=mesh['dp'=16,'expert'=32] {'dp'}, dimensions={0} | all-to-all | bytes 1048576 | tf_op jit(solution)/shard_map/all_to_all | solution.py:207
  140.1 0.0 copy-done
  140.1 0.0 copy-done.5
  140.1 0.0 copy-start.7
  140.1 0.0 copy-start.10
  140.1 0.4 shard_map.117
  140.5 14.8 %all_to_all.33.pieces_ref = bf16[32,64,128]{2,1,0:T(8,128)(2,1)S(1)} all-to-all(bf16[32,64,128]{2,1,0:T(8,128)(2,1)S(1)} %bitcast.24), channel_id=1, replica_groups=mesh['dp'=16,'expert'=32] {'expert'}, dimensions={0} | all-to-all | bytes 1048576 | tf_op jit(solution)/shard_map/all_to_all | solution.py:207
  155.3 0.0 copy-done.7
  155.4 0.0 copy-done.10
  155.4 0.1 shard_map.118
  155.5 15.2 %all_to_all.34 = bf16[32,64,128]{2,1,0:T(8,128)(2,1)S(1)} all-to-all(bf16[32,64,128]{2,1,0:T(8,128)(2,1)S(1)} %shard_map.118), channel_id=1, replica_groups=mesh['dp'=16,'expert'=32] {'expert'}, dimensions={0} | all-to-all | bytes 1048576 | tf_op jit(solution)/shard_map/all_to_all | solution.py:207
  170.7 1.4 shard_map.119
  172.1 0.0 reduce-scatter.2.cloned.1.call-update
  172.1 34.2 %all-gather.1 = bf16[2048,128]{1,0:T(8,128)(2,1)S(1)} all-gather(bf16[128,128]{1,0:T(8,128)(2,1)S(1)} %get-tuple-element.12), channel_id=3, replica_groups=mesh['dp'=16,'expert'=32] {'dp'}, dimensions={0}, use_global_device_ids=true | all-gather | bytes 557056 | tf_op jit(solution)/shard_map/all_gather | solution.py:241
  206.4 3.4 %shard_map.120 = bf16[32,160,128]{2,1,0:T(8,128)(2,1)} custom-call(bf16[16,144,128]{2,1,0:T(8,128)(2,1)S(1)} %bitcast.18, bf16[16,128,128]{2,1,0:T(8,128)(2,1)S(1)} %bitcast.19), custom_call_target="tpu_custom_call" | custom-call | tf_op jit(solution)/shard_map/pallas_call | solution.py:18
  209.7 6.6 %all-to-all-start.5 = ((bf16[32,160,128]{2,1,0:T(8,128)(2,1)}), bf16[32,160,128]{2,1,0:T(8,128)(2,1)S(1)}, u32[]{:S(2)}, u32[]{:S(2)}) async-start(bf16[32,160,128]{2,1,0:T(8,128)(2,1)} %shard_map.120), calls=%async_computation.5 | async-start | bytes 2621440 | tf_op jit(solution)/shard_map/all_to_all | solution.py:207
  216.4 19.5 %reduce-scatter.2.cloned.1.call-done = bf16[1,128,128]{2,1,0:T(8,128)(2,1)} async-done(((bf16[16,128,128]{2,1,0:T(8,128)(2,1)}), bf16[1,128,128]{2,1,0:T(8,128)(2,1)}) %reduce-scatter.2.cloned.1.call-update) | async-done | bytes 32784 | tf_op jit(solution)/shard_map/reduce_scatter | solution.py:240
  235.9 1.4 bitcast_convert_fusion
  237.3 0.0 all-to-all-done.5.rows_ref
  237.3 1.7 shard_map.121
Async XLA Ops:
  7.2 228.7 %reduce-scatter.2.cloned.1.call-start = ((), (), s32[]{:S(2)}) async-start(), calls=%async_computation.7 | async-start | bytes 557056 | tf_op jit(solution)/shard_map/reduce_scatter | solution.py:240
  7.2 0.8 copy-start.4
  8.0 0.7 copy-start.8
  8.7 0.7 copy-start.9
  48.3 28.0 %copy-start.3 = (bf16[1,128,4096]{2,1,0:T(8,128)(2,1)S(1)}, bf16[1,128,4096]{2,1,0:T(8,128)(2,1)}, u32[]{:S(2)}) copy-start(bf16[1,128,4096]{2,1,0:T(8,128)(2,1)} %param.16) | copy-start | bytes 3145732
  50.5 25.8 %copy-start.1 = (bf16[1,4096,128]{2,1,0:T(8,128)(2,1)S(1)}, bf16[1,4096,128]{2,1,0:T(8,128)(2,1)}, u32[]{:S(2)}) copy-start(bf16[1,4096,128]{2,1,0:T(8,128)(2,1)} %param.14) | copy-start | bytes 3145732
  50.5 25.8 %copy-start.2 = (bf16[1,4096,128]{2,1,0:T(8,128)(2,1)S(1)}, bf16[1,4096,128]{2,1,0:T(8,128)(2,1)}, u32[]{:S(2)}) copy-start(bf16[1,4096,128]{2,1,0:T(8,128)(2,1)} %param.15) | copy-start | bytes 3145732
  50.5 25.8 %copy-start.6 = (f32[4096]{0:T(1024)S(1)}, f32[4096]{0:T(1024)}, u32[]{:S(2)}) copy-start(f32[4096]{0:T(1024)} %param.11) | copy-start | bytes 49156
  101.5 38.5 %copy-start = (bf16[128,2048]{1,0:T(8,128)(2,1)S(1)}, bf16[128,2048]{1,0:T(8,128)(2,1)}, u32[]{:S(2)}) copy-start(bf16[128,2048]{1,0:T(8,128)(2,1)} %weight_ref.3) | copy-start | bytes 1572868
  101.5 38.5 %copy-start.5 = (bf16[128,128]{1,0:T(8,128)(2,1)S(1)}, bf16[128,128]{1,0:T(8,128)(2,1)}, u32[]{:S(2)}) copy-start(bf16[128,128]{1,0:T(8,128)(2,1)} %tok_ref.3) | copy-start | bytes 98308
  140.1 15.3 %copy-start.7 = (bf16[128,64]{0,1:T(8,128)(2,1)S(1)}, bf16[128,64]{0,1:T(8,128)(2,1)}, u32[]{:S(2)}) copy-start(bf16[128,64]{0,1:T(8,128)(2,1)} %param.18) | copy-start | bytes 49156
  140.1 15.3 %copy-start.10 = (s32[128]{0:T(128)S(1)}, s32[128]{0:T(128)}, u32[]{:S(2)}) copy-start(s32[128]{0:T(128)} %param.19) | copy-start | bytes 1540
  209.7 27.5 %all-to-all-start.5 = ((bf16[32,160,128]{2,1,0:T(8,128)(2,1)}), bf16[32,160,128]{2,1,0:T(8,128)(2,1)S(1)}, u32[]{:S(2)}, u32[]{:S(2)}) async-start(bf16[32,160,128]{2,1,0:T(8,128)(2,1)} %shard_map.120), calls=%async_computation.5 | async-start | bytes 2621440 | tf_op jit(solution)/shard_map/all_to_all | solution.py:207
Sparse Core Ops, SparseCore 0:
  172.2 63.6 reduce-scatter.1

commit v3 on v2

--- a/solution.py
+++ b/solution.py
@@ -3,6 +3,7 @@
 from jax import lax
 from jax.experimental import pallas as pl
 from jax.experimental.pallas import tpu as pltpu
+from jax.sharding import Mesh
 from jax.sharding import PartitionSpec as P
 
 f32 = jnp.float32
@@ -34,7 +35,6 @@
 
 def prepare(tok_ref, routes_ref, prob_ref, out_ref):
     rows, experts = tok_ref.shape[0], 32
-    out_ref[0:rows, :] = tok_ref[...]
     routes = routes_ref[...].astype(f32)
     first, second = routes[0:1, :], routes[1:2, :]
     names = iota((experts, rows), 0).astype(f32)
@@ -62,7 +62,10 @@
             ),
         ),
     )
-    out_ref[rows : rows + meta_rows, :] = meta.astype(bf16)
+    meta = meta.astype(bf16)
+    for copy in range(out_ref.shape[0]):
+        out_ref[copy, 0:rows, :] = tok_ref[...]
+        out_ref[copy, rows : rows + meta_rows, :] = meta
 
 
 def selection(meta, inner, capacity, weighted):
@@ -85,7 +88,7 @@
 
 def dispatch(gathered_ref, out_ref):
     blocks, rows = gathered_ref.shape[0], gathered_ref.shape[1] - meta_rows
-    capacity = out_ref.shape[1] // blocks
+    capacity = out_ref.shape[2] // blocks
     tall = group * capacity
     for g in range(blocks // group):
         total = 0.0
@@ -95,13 +98,15 @@
             total = total + jnp.dot(
                 chosen, gathered_ref[block, 0:rows, :], preferred_element_type=f32
             )
-        for e in range(out_ref.shape[0]):
-            out_ref[e, g * tall : (g + 1) * tall, :] = total[e * tall : (e + 1) * tall].astype(bf16)
+        total = total.astype(bf16)
+        for e in range(out_ref.shape[1]):
+            for pair in range(out_ref.shape[0]):
+                out_ref[pair, e, g * tall : (g + 1) * tall, :] = total[e * tall : (e + 1) * tall]
 
 
 def dispatch_grad(gathered_ref, grad_ref, out_ref):
     blocks, rows = gathered_ref.shape[0], gathered_ref.shape[1] - meta_rows
-    capacity = out_ref.shape[1] // blocks
+    capacity = out_ref.shape[2] // blocks
     tall = group * capacity
     for g in range(blocks // group):
         total = 0.0
@@ -109,13 +114,21 @@
             block = g * group + inner
             chosen = selection(block_meta(gathered_ref, block, rows), inner, capacity, True)
             total = total + contract(chosen, grad_ref[block], 1, 1)
-        for e in range(out_ref.shape[0]):
-            out_ref[e, g * tall : (g + 1) * tall, :] = total[e * tall : (e + 1) * tall].astype(bf16)
+        total = total.astype(bf16)
+        for e in range(out_ref.shape[1]):
+            for pair in range(out_ref.shape[0]):
+                out_ref[pair, e, g * tall : (g + 1) * tall, :] = total[e * tall : (e + 1) * tall]
 
 
 def expert(rows_ref, gain_ref, gate_ref, up_ref, down_ref, out_ref, hidden_ref):
-    parts, width = rows_ref.shape[0], rows_ref.shape[2]
-    values = jnp.concatenate([rows_ref[p] for p in range(parts)], axis=1).astype(f32)
+    pairs, parts, half, width = rows_ref.shape
+    values = jnp.concatenate(
+        [
+            jnp.concatenate([rows_ref[h, p] for p in range(parts)], axis=1)
+            for h in range(pairs)
+        ],
+        axis=0,
+    ).astype(f32)
     mean_sq = jnp.sum(values * values, axis=1, keepdims=True) / (parts * width)
     normed = (values * lax.rsqrt(mean_sq + eps_norm) * gain_ref[...]).astype(bf16)
     gate_val = jnp.dot(normed, gate_ref[...], preferred_element_type=f32)
@@ -123,17 +136,26 @@
     hidden = (gate_val / (1.0 + jnp.exp(-gate_val)) * up_val).astype(bf16)
     hidden_ref[...] = hidden
     product = jnp.dot(hidden, down_ref[...], preferred_element_type=f32)
-    for p in range(parts):
-        out_ref[p] = product[:, p * width : (p + 1) * width].astype(bf16)
+    for h in range(pairs):
+        for p in range(parts):
+            out_ref[h, p] = product[
+                h * half : (h + 1) * half, p * width : (p + 1) * width
+            ].astype(bf16)
 
 
 def combine(gathered_ref, back_ref, out_ref):
     blocks, rows = gathered_ref.shape[0], gathered_ref.shape[1] - meta_rows
-    capacity = back_ref.shape[1] // blocks
+    capacity = back_ref.shape[2] // blocks
     tall = group * capacity
     for g in range(blocks // group):
         back = jnp.concatenate(
-            [back_ref[e, g * tall : (g + 1) * tall, :].astype(f32) for e in range(back_ref.shape[0])],
+            [
+                sum(
+                    back_ref[pair, e, g * tall : (g + 1) * tall, :].astype(f32)
+                    for pair in range(back_ref.shape[0])
+                )
+                for e in range(back_ref.shape[1])
+            ],
             axis=0,
         )
         back = back.T.astype(bf16)
@@ -164,9 +186,11 @@
 
 
 def gradients(cot_ref, state_ref, weight_ref, state_grad_ref, pieces_ref):
-    state_grad_ref[...] = jnp.dot(
+    state_grad = jnp.dot(
         weight_ref[...], cot_ref[...], preferred_element_type=f32
     ).astype(bf16)
+    for copy in range(state_grad_ref.shape[0]):
+        state_grad_ref[copy] = state_grad
     state = state_ref[...]
     width = cot_ref.shape[0] // pieces_ref.shape[0]
     for p in range(pieces_ref.shape[0]):
@@ -175,10 +199,11 @@
 
 def down_gradient(hidden_ref, rows_ref, out_ref):
     hidden = hidden_ref[...].astype(f32).T.astype(bf16)
-    width = rows_ref.shape[2]
-    for p in range(rows_ref.shape[0]):
+    pairs, parts, half, width = rows_ref.shape
+    for p in range(parts):
+        rows = jnp.concatenate([rows_ref[h, p] for h in range(pairs)], axis=0)
         out_ref[:, p * width : (p + 1) * width] = jnp.dot(
-            hidden, rows_ref[p], preferred_element_type=f32
+            hidden, rows, preferred_element_type=f32
         ).astype(bf16)
 
 
@@ -196,7 +221,8 @@
 ):
     rows, width = tokens.shape
     experts = lax.axis_size("expert")
-    blocks = lax.axis_size("dp")
+    far, near = lax.axis_size("far"), lax.axis_size("near")
+    blocks = far * near
     capacity = 5 * rows * routes.shape[1] // (4 * experts)
     keys = key_value_weight.shape[1]
 
@@ -206,10 +232,17 @@
     def exchange(value, axis):
         return lax.all_to_all(value, axis, split_axis=0, concat_axis=0, tiled=True)
 
-    packed = call(prepare, shape(rows + meta_rows, width), tokens, routes.T, route_prob.T)
-    gathered = lax.all_gather(packed, "dp", axis=0)
-    slots = shape(experts, blocks * capacity, width)
-    arrived = exchange(call(dispatch, slots, gathered), "expert")
+    packed = call(
+        prepare, shape(far, rows + meta_rows, width), tokens, routes.T, route_prob.T
+    )
+    gathered = exchange(packed, "far")
+    slots = shape(near, experts, far * capacity, width)
+    spots = (near * experts, far * capacity, width)
+
+    def route(value):
+        return exchange(value.reshape(spots), ("near", "expert")).reshape(slots.shape)
+
+    arrived = route(call(dispatch, slots, gathered))
     out_rows, hidden = call(
         expert,
         [slots, shape(blocks * capacity, gate_weight.shape[2])],
@@ -220,8 +253,8 @@
         down_weight[0],
         limit=24,
     )
-    returned = exchange(out_rows, "expert")
-    mixed = exchange(call(combine, shape(blocks, width, rows), gathered, returned), "dp")
+    returned = route(out_rows)
+    mixed = exchange(call(combine, shape(far, width, rows), gathered, returned), "far")
     state, proj = call(
         project, [shape(width, rows), shape(keys, rows)], mixed, tokens, key_value_weight
     )
@@ -232,35 +265,40 @@
     cotangent = exchange(spread, "expert").reshape(keys, rows)
     state_grad, pieces = call(
         gradients,
-        [shape(width, rows), shape(blocks, width, keys // blocks)],
+        [shape(far, width, rows), shape(blocks, width, keys // blocks)],
         cotangent,
         state,
         key_value_weight,
     )
-    key_value_grad = lax.psum_scatter(pieces, "dp", scatter_dimension=0, tiled=True)[0].astype(f32)
-    all_grads = lax.all_gather(state_grad, "dp", axis=0)
-    landed = exchange(call(dispatch_grad, slots, gathered, all_grads), "expert")
+    key_value_grad = lax.psum_scatter(
+        pieces, ("far", "near"), scatter_dimension=0, tiled=True
+    )[0].astype(f32)
+    all_grads = exchange(state_grad, "far")
+    landed = route(call(dispatch_grad, slots, gathered, all_grads))
     down_grad = call(down_gradient, shape(*down_weight.shape[1:]), hidden, landed)
     return (down_grad[None], key_value_grad)
 
 
 def solution(mesh):
+    blocks, experts = mesh.devices.shape
+    fine = Mesh(mesh.devices.reshape(blocks // 2, 2, experts), ("far", "near", "expert"))
+    dp = ("far", "near")
     placed = (
-        P("dp", "expert"),
+        P(dp, "expert"),
         P(),
-        P("dp", None),
-        P("dp", None),
-        P("expert", None, "dp"),
-        P("expert", None, "dp"),
-        P("expert", "dp", None),
+        P(dp, None),
+        P(dp, None),
+        P("expert", None, dp),
+        P("expert", None, dp),
+        P("expert", dp, None),
         P("expert", None),
-        P("dp", "expert"),
-        P("dp"),
+        P(dp, "expert"),
+        P(dp),
     )
     return jax.shard_map(
         per_device,
-        mesh=mesh,
+        mesh=fine,
         in_specs=placed,
-        out_specs=(P("expert", "dp", None), P("expert", "dp")),
+        out_specs=(P("expert", dp, None), P("expert", dp)),
         check_vma=False,
     )

time: 247 us -> 270 us (1.093)
  waiting for transfers between devices: 19.6 us -> 67.3 us
  blocking collectives: 188 us -> 167 us
  Pallas kernels: 14.1 us -> 10.4 us
    all_gather x2 -> x0, blocking collectives: 73.1 us -> none  [the longest x1 38.9 us: per_device(): gathered = lax.all_gather(packed, 'dp', axis=0)]
    all_to_all x5 -> x7, blocking collectives: 115 us -> 167 us  [exchange(): return lax.all_to_all(value, axis, split_axis=0, concat_axis=0, tiled=True)]
    reduce_scatter x1, waiting for transfers between devices: 19.5 us -> 66.6 us  [per_device(): lax.psum_scatter(pieces, ('far', 'near'), scatter_dimension=0, tiled=True)]
    pallas_call x9, Pallas kernels: 14.1 us -> 10.4 us  [call(): pl.pallas_call(body, out_shape=outs, in_specs=[vmem] * len(operands), out...]
  transfers between devices with their start and end apart: 2 -> 2, of which waited for: 1 -> 1; matrix products, arithmetic and copies ran while one was open for 1% -> 1% of each run, Pallas kernels for 1% -> 0%
where the time goes in v3:
time: 270 us; the launch traced here: 269 us
  blocking collectives  167 us (62%)
  waiting for transfers between devices  67.3 us (25%)
  between operations  14.1 us (5%)
  Pallas kernels  10.4 us (4%)
  starting transfers between devices  6.59 us (2%)
    all_to_all x7, blocking collectives, exchange(): return lax.all_to_all(value, axis, split_axis=0, concat_axis=0, tiled=True)  167 us
    reduce_scatter x1, waiting for transfers between devices, per_device(): lax.psum_scatter(pieces, ('far', 'near'), scatter_dimension=0, tiled=True)  66.6 us
    pallas_call x9, Pallas kernels, call(): pl.pallas_call(body, out_shape=outs, in_specs=[vmem] * len(operands), out...  10.4 us
    all_to_all x1, starting transfers between devices, exchange(): return lax.all_to_all(value, axis, split_axis=0, concat_axis=0, tiled=True)  6.55 us
  transfers between devices with their start and end apart: 2, of which 1 were waited for; matrix products, arithmetic and copies ran while one was open for 1% of the time, Pallas kernels for 0%

profile of v3, /device:TPU:6, one launch (start us, length us, event | category | flops | bytes accessed | tf_op | source)
XLA Modules:
  0.0 269.2 jit_solution(10097765844553367716)
XLA Ops:
  7.2 0.0 copy-start.4
  7.2 0.7 copy-done.4
  7.9 0.0 copy-start.8
  7.9 0.7 copy-done.8
  8.6 0.0 copy-start.9
  8.6 0.7 copy-done.9
  9.3 0.2 shard_map.113
  9.4 38.0 %all_to_all.40.gathered_ref = bf16[8,144,128]{2,1,0:T(8,128)(2,1)S(1)} all-to-all(bf16[8,144,128]{2,1,0:T(8,128)(2,1)S(1)} %shard_map.113), channel_id=1, replica_groups=mesh['far'=8,'near'=2,'expert'=32] {'far'}, dimensions={0} | all-to-all | bytes 589824 | tf_op jit(solution)/shard_map/all_to_all | solution.py:233
  47.4 0.0 copy-start.3
  47.4 1.2 shard_map.114
  48.6 0.0 copy-start.1
  48.6 0.0 copy-start.2
  48.6 0.0 copy-start.6
  48.6 27.1 %all_to_all.41 = bf16[64,80,128]{2,1,0:T(8,128)(2,1)S(1)} all-to-all(bf16[64,80,128]{2,1,0:T(8,128)(2,1)S(1)} %bitcast.22), channel_id=1, replica_groups=mesh['far'=8,'near'=2,'expert'=32] {'near','expert'}, dimensions={0} | all-to-all | bytes 2621440 | tf_op jit(solution)/shard_map/all_to_all | solution.py:233
  75.7 0.0 copy-done.3
  75.7 0.0 copy-done.1
  75.7 0.0 copy-done.2
  75.7 0.0 copy-done.6
  75.7 1.5 shard_map.115
  77.2 25.2 %all_to_all.42 = bf16[64,80,128]{2,1,0:T(8,128)(2,1)S(1)} all-to-all(bf16[64,80,128]{2,1,0:T(8,128)(2,1)S(1)} %bitcast.25), channel_id=1, replica_groups=mesh['far'=8,'near'=2,'expert'=32] {'near','expert'}, dimensions={0} | all-to-all | bytes 2621440 | tf_op jit(solution)/shard_map/all_to_all | solution.py:233
  102.4 0.0 copy-start
  102.4 0.0 copy-start.5
  102.4 1.7 shard_map.116
  104.2 0.0 copy-start.7
  104.2 0.0 copy-start.10
  104.2 24.3 %all_to_all.43.pieces_ref = bf16[8,128,128]{2,1,0:T(8,128)(2,1)S(1)} all-to-all(bf16[8,128,128]{2,1,0:T(8,128)(2,1)S(1)} %shard_map.116), channel_id=1, replica_groups=mesh['far'=8,'near'=2,'expert'=32] {'far'}, dimensions={0} | all-to-all | bytes 524288 | tf_op jit(solution)/shard_map/all_to_all | solution.py:233
  128.5 0.0 copy-done
  128.5 0.0 copy-done.5
  128.5 0.4 shard_map.117
  128.9 13.8 %all_to_all.44.pieces_ref = bf16[32,64,128]{2,1,0:T(8,128)(2,1)S(1)} all-to-all(bf16[32,64,128]{2,1,0:T(8,128)(2,1)S(1)} %bitcast.29), channel_id=1, replica_groups=mesh['far'=8,'near'=2,'expert'=32] {'expert'}, dimensions={0} | all-to-all | bytes 1048576 | tf_op jit(solution)/shard_map/all_to_all | solution.py:233
  142.8 0.0 copy-done.7
  142.8 0.0 copy-done.10
  142.8 0.1 shard_map.118
  142.9 15.2 %all_to_all.45 = bf16[32,64,128]{2,1,0:T(8,128)(2,1)S(1)} all-to-all(bf16[32,64,128]{2,1,0:T(8,128)(2,1)S(1)} %shard_map.118), channel_id=1, replica_groups=mesh['far'=8,'near'=2,'expert'=32] {'expert'}, dimensions={0} | all-to-all | bytes 1048576 | tf_op jit(solution)/shard_map/all_to_all | solution.py:233
  158.1 1.4 shard_map.119
  159.5 23.6 %all_to_all.46.grad_ref = bf16[8,128,128]{2,1,0:T(8,128)(2,1)S(1)} all-to-all(bf16[8,128,128]{2,1,0:T(8,128)(2,1)S(1)} %get-tuple-element.12), channel_id=1, replica_groups=mesh['far'=8,'near'=2,'expert'=32] {'far'}, dimensions={0} | all-to-all | bytes 524288 | tf_op jit(solution)/shard_map/all_to_all | solution.py:233
  183.1 2.2 shard_map.120
  185.3 6.6 %all-to-all-start.7 = ((bf16[64,80,128]{2,1,0:T(8,128)(2,1)}), bf16[64,80,128]{2,1,0:T(8,128)(2,1)S(1)}, u32[]{:S(2)}, u32[]{:S(2)}) async-start(bf16[64,80,128]{2,1,0:T(8,128)(2,1)} %bitcast.14), calls=%async_computation.7 | async-start | bytes 2621440 | tf_op jit(solution)/shard_map/all_to_all | solution.py:233
  191.9 0.0 reduce-scatter.2.cloned.1.call-start
  191.9 0.7 reduce-scatter.2.cloned.1.call-update
  192.6 66.6 %reduce-scatter.2.cloned.1.call-done = bf16[1,128,128]{2,1,0:T(8,128)(2,1)} async-done(((bf16[16,128,128]{2,1,0:T(8,128)(2,1)}), bf16[1,128,128]{2,1,0:T(8,128)(2,1)}) %reduce-scatter.2.cloned.1.call-update) | async-done | bytes 32784 | tf_op jit(solution)/shard_map/reduce_scatter | solution.py:273
  259.2 1.4 bitcast_convert_fusion
  260.6 0.0 all-to-all-done.7
  260.6 1.7 shard_map.121
Async XLA Ops:
  7.2 0.8 copy-start.4
  7.9 0.7 copy-start.8
  8.6 0.7 copy-start.9
  47.4 28.3 %copy-start.3 = (bf16[1,128,4096]{2,1,0:T(8,128)(2,1)S(1)}, bf16[1,128,4096]{2,1,0:T(8,128)(2,1)}, u32[]{:S(2)}) copy-start(bf16[1,128,4096]{2,1,0:T(8,128)(2,1)} %param.16) | copy-start | bytes 3145732
  48.6 27.2 %copy-start.1 = (bf16[1,4096,128]{2,1,0:T(8,128)(2,1)S(1)}, bf16[1,4096,128]{2,1,0:T(8,128)(2,1)}, u32[]{:S(2)}) copy-start(bf16[1,4096,128]{2,1,0:T(8,128)(2,1)} %param.14) | copy-start | bytes 3145732
  48.6 27.1 %copy-start.2 = (bf16[1,4096,128]{2,1,0:T(8,128)(2,1)S(1)}, bf16[1,4096,128]{2,1,0:T(8,128)(2,1)}, u32[]{:S(2)}) copy-start(bf16[1,4096,128]{2,1,0:T(8,128)(2,1)} %param.15) | copy-start | bytes 3145732
  48.6 27.1 %copy-start.6 = (f32[4096]{0:T(1024)S(1)}, f32[4096]{0:T(1024)}, u32[]{:S(2)}) copy-start(f32[4096]{0:T(1024)} %param.11) | copy-start | bytes 49156
  102.4 26.1 %copy-start = (bf16[128,2048]{1,0:T(8,128)(2,1)S(1)}, bf16[128,2048]{1,0:T(8,128)(2,1)}, u32[]{:S(2)}) copy-start(bf16[128,2048]{1,0:T(8,128)(2,1)} %weight_ref.3) | copy-start | bytes 1572868
  102.4 26.1 %copy-start.5 = (bf16[128,128]{1,0:T(8,128)(2,1)S(1)}, bf16[128,128]{1,0:T(8,128)(2,1)}, u32[]{:S(2)}) copy-start(bf16[128,128]{1,0:T(8,128)(2,1)} %tok_ref.3) | copy-start | bytes 98308
  104.2 38.6 %copy-start.7 = (bf16[128,64]{0,1:T(8,128)(2,1)S(1)}, bf16[128,64]{0,1:T(8,128)(2,1)}, u32[]{:S(2)}) copy-start(bf16[128,64]{0,1:T(8,128)(2,1)} %param.18) | copy-start | bytes 49156
  104.2 38.6 %copy-start.10 = (s32[128]{0:T(128)S(1)}, s32[128]{0:T(128)}, u32[]{:S(2)}) copy-start(s32[128]{0:T(128)} %param.19) | copy-start | bytes 1540
  185.3 75.3 %all-to-all-start.7 = ((bf16[64,80,128]{2,1,0:T(8,128)(2,1)}), bf16[64,80,128]{2,1,0:T(8,128)(2,1)S(1)}, u32[]{:S(2)}, u32[]{:S(2)}) async-start(bf16[64,80,128]{2,1,0:T(8,128)(2,1)} %bitcast.14), calls=%async_computation.7 | async-start | bytes 2621440 | tf_op jit(solution)/shard_map/all_to_all | solution.py:233
  191.9 67.4 %reduce-scatter.2.cloned.1.call-start = ((), (), s32[]{:S(2)}) async-start(), calls=%async_computation.9 | async-start | bytes 557056 | tf_op jit(solution)/shard_map/reduce_scatter | solution.py:273
Sparse Core Ops, SparseCore 0:
  196.1 63.1 reduce-scatter.1

commit v4 on v3

--- a/solution.py
+++ b/solution.py
@@ -13,7 +13,7 @@
 group = 4
 
 
-def call(body, outs, *operands, limit=16):
+def call(body, outs, *operands, limit=16, cost=None):
     vmem = pl.BlockSpec(memory_space=pltpu.VMEM)
     single = not isinstance(outs, (list, tuple))
     return pl.pallas_call(
@@ -21,6 +21,7 @@
         out_shape=outs,
         in_specs=[vmem] * len(operands),
         out_specs=vmem if single else [vmem] * len(outs),
+        cost_estimate=cost,
         compiler_params=pltpu.CompilerParams(vmem_limit_bytes=limit * 1024 * 1024),
     )(*operands)
 
@@ -207,6 +208,10 @@
         ).astype(bf16)
 
 
+def widen(piece_ref, out_ref):
+    out_ref[...] = piece_ref[...].astype(f32)
+
+
 def per_device(
     tokens,
     norm_gain,
@@ -272,9 +277,16 @@
     )
     key_value_grad = lax.psum_scatter(
         pieces, ("far", "near"), scatter_dimension=0, tiled=True
-    )[0].astype(f32)
+    )[0]
+    key_value_grad = call(
+        widen,
+        shape(width, keys // blocks, dtype=f32),
+        key_value_grad,
+        cost=pl.CostEstimate(flops=10**12, bytes_accessed=1 << 17, transcendentals=0),
+    )
     all_grads = exchange(state_grad, "far")
     landed = route(call(dispatch_grad, slots, gathered, all_grads))
+    landed, key_value_grad = lax.optimization_barrier((landed, key_value_grad))
     down_grad = call(down_gradient, shape(*down_weight.shape[1:]), hidden, landed)
     return (down_grad[None], key_value_grad)
 

time: 270 us -> 236 us (0.87)
  waiting for transfers between devices: 67.3 us -> 29.5 us
  blocking collectives: 167 us -> 170 us
    reduce_scatter x1, waiting for transfers between devices: 66.6 us -> 29.5 us  [per_device(): lax.psum_scatter(pieces, ('far', 'near'), scatter_dimension=0, tiled=True)]
    all_to_all x7, blocking collectives: 167 us -> 170 us  [exchange(): return lax.all_to_all(value, axis, split_axis=0, concat_axis=0, tiled=True)]
    pallas_call x9 -> x10, Pallas kernels: 10.4 us -> 12.3 us  [call(): pl.pallas_call(body, out_shape=outs, in_specs=[vmem] * len(operands), out...]
  transfers between devices with their start and end apart: 2 -> 2, of which waited for: 1 -> 1; matrix products, arithmetic and copies ran while one was open for 1% -> 0% of each run, Pallas kernels for 0% -> 1%
where the time goes in v4:
time: 236 us; the launch traced here: 235 us
  blocking collectives  170 us (72%)
  waiting for transfers between devices  29.5 us (12%)
  between operations  14.1 us (6%)
  Pallas kernels  12.3 us (5%)
  starting transfers between devices  6.21 us (3%)
  local copies, waits for them, and re-layouts  2.91 us (1%)
    all_to_all x7, blocking collectives, exchange(): return lax.all_to_all(value, axis, split_axis=0, concat_axis=0, tiled=True)  170 us
    reduce_scatter x1, waiting for transfers between devices, per_device(): lax.psum_scatter(pieces, ('far', 'near'), scatter_dimension=0, tiled=True)  29.5 us
    pallas_call x10, Pallas kernels, call(): pl.pallas_call(body, out_shape=outs, in_specs=[vmem] * len(operands), out...  12.3 us
    all_to_all x1, starting transfers between devices, exchange(): return lax.all_to_all(value, axis, split_axis=0, concat_axis=0, tiled=True)  6.17 us
  transfers between devices with their start and end apart: 2, of which 1 were waited for; matrix products, arithmetic and copies ran while one was open for 0% of the time, Pallas kernels for 1%

profile of v4, /device:TPU:6, one launch (start us, length us, event | category | flops | bytes accessed | tf_op | source)
XLA Modules:
  0.0 235.3 jit_solution(14306398630607078048)
XLA Ops:
  7.2 0.0 reduce-scatter.2.cloned.1.call-start
  7.2 0.0 copy-start.4
  7.2 0.7 copy-done.4
  8.0 0.0 copy-start.8
  8.0 0.7 copy-done.8
  8.7 0.0 copy-start.9
  8.7 0.7 copy-done.9
  9.3 0.2 shard_map.113
  9.5 38.0 %all_to_all.40.gathered_ref = bf16[8,144,128]{2,1,0:T(8,128)(2,1)S(1)} all-to-all(bf16[8,144,128]{2,1,0:T(8,128)(2,1)S(1)} %shard_map.113), channel_id=1, replica_groups=mesh['far'=8,'near'=2,'expert'=32] {'far'}, dimensions={0} | all-to-all | bytes 589824 | tf_op jit(solution)/shard_map/all_to_all | solution.py:238
  47.4 0.0 copy-start.3
  47.4 1.2 shard_map.114
  48.6 0.0 copy-start.1
  48.6 0.0 copy-start.2
  48.6 0.0 copy-start.6
  48.6 27.1 %all_to_all.41 = bf16[64,80,128]{2,1,0:T(8,128)(2,1)S(1)} all-to-all(bf16[64,80,128]{2,1,0:T(8,128)(2,1)S(1)} %bitcast.19), channel_id=1, replica_groups=mesh['far'=8,'near'=2,'expert'=32] {'near','expert'}, dimensions={0} | all-to-all | bytes 2621440 | tf_op jit(solution)/shard_map/all_to_all | solution.py:238
  75.8 0.0 copy-done.3
  75.8 0.0 copy-done.1
  75.8 0.0 copy-done.2
  75.8 0.0 copy-done.6
  75.8 1.5 shard_map.115
  77.3 25.2 %all_to_all.42 = bf16[64,80,128]{2,1,0:T(8,128)(2,1)S(1)} all-to-all(bf16[64,80,128]{2,1,0:T(8,128)(2,1)S(1)} %bitcast.22), channel_id=1, replica_groups=mesh['far'=8,'near'=2,'expert'=32] {'near','expert'}, dimensions={0} | all-to-all | bytes 2621440 | tf_op jit(solution)/shard_map/all_to_all | solution.py:238
  102.5 0.0 copy-start
  102.5 0.0 copy-start.5
  102.5 1.7 shard_map.116
  104.2 0.0 copy-start.7
  104.2 0.0 copy-start.10
  104.2 24.3 %all_to_all.43.pieces_ref = bf16[8,128,128]{2,1,0:T(8,128)(2,1)S(1)} all-to-all(bf16[8,128,128]{2,1,0:T(8,128)(2,1)S(1)} %shard_map.116), channel_id=1, replica_groups=mesh['far'=8,'near'=2,'expert'=32] {'far'}, dimensions={0} | all-to-all | bytes 524288 | tf_op jit(solution)/shard_map/all_to_all | solution.py:238
  128.6 0.0 copy-done
  128.6 0.0 copy-done.5
  128.6 0.4 shard_map.117
  129.0 13.8 %all_to_all.44.pieces_ref = bf16[32,64,128]{2,1,0:T(8,128)(2,1)S(1)} all-to-all(bf16[32,64,128]{2,1,0:T(8,128)(2,1)S(1)} %bitcast.26), channel_id=1, replica_groups=mesh['far'=8,'near'=2,'expert'=32] {'expert'}, dimensions={0} | all-to-all | bytes 1048576 | tf_op jit(solution)/shard_map/all_to_all | solution.py:238
  142.8 0.0 copy-done.7
  142.8 0.0 copy-done.10
  142.8 0.1 shard_map.118
  142.9 15.2 %all_to_all.45 = bf16[32,64,128]{2,1,0:T(8,128)(2,1)S(1)} all-to-all(bf16[32,64,128]{2,1,0:T(8,128)(2,1)S(1)} %shard_map.118), channel_id=1, replica_groups=mesh['far'=8,'near'=2,'expert'=32] {'expert'}, dimensions={0} | all-to-all | bytes 1048576 | tf_op jit(solution)/shard_map/all_to_all | solution.py:238
  158.1 1.4 shard_map.119
  159.5 0.0 reduce-scatter.2.cloned.1.call-update
  159.6 26.5 %all_to_all.46.grad_ref = bf16[8,128,128]{2,1,0:T(8,128)(2,1)S(1)} all-to-all(bf16[8,128,128]{2,1,0:T(8,128)(2,1)S(1)} %get-tuple-element.14), channel_id=1, replica_groups=mesh['far'=8,'near'=2,'expert'=32] {'far'}, dimensions={0} | all-to-all | bytes 524288 | tf_op jit(solution)/shard_map/all_to_all | solution.py:238
  186.1 2.2 shard_map.120
  188.3 6.2 %all-to-all-start.7 = ((bf16[64,80,128]{2,1,0:T(8,128)(2,1)}), bf16[64,80,128]{2,1,0:T(8,128)(2,1)}, u32[]{:S(2)}, u32[]{:S(2)}) async-start(bf16[64,80,128]{2,1,0:T(8,128)(2,1)} %bitcast.14), calls=%async_computation.7 | async-start | bytes 2621440 | tf_op jit(solution)/shard_map/all_to_all | solution.py:238
  194.5 29.5 %reduce-scatter.2.cloned.1.call-done = bf16[1,128,128]{2,1,0:T(8,128)(2,1)} async-done(((bf16[16,128,128]{2,1,0:T(8,128)(2,1)}), bf16[1,128,128]{2,1,0:T(8,128)(2,1)}) %reduce-scatter.2.cloned.1.call-update) | async-done | bytes 32784 | tf_op jit(solution)/shard_map/reduce_scatter | solution.py:278
  224.0 0.0 copy-start.11
  224.0 0.8 copy-done.11
  224.8 0.6 shard_map.121
  225.4 0.0 all-to-all-done.7
  225.4 3.0 %shard_map.122 = bf16[128,4096]{1,0:T(8,128)(2,1)} custom-call(bf16[160,128]{1,0:T(8,128)(2,1)S(1)} %get-tuple-element.10.hidden_ref, bf16[2,32,80,128]{3,2,1,0:T(8,128)(2,1)} %bitcast.15.rows_ref), custom_call_target="tpu_custom_call" | custom-call | tf_op jit(solution)/shard_map/pallas_call | solution.py:19
Async XLA Ops:
  7.2 216.9 %reduce-scatter.2.cloned.1.call-start = ((), (), s32[]{:S(2)}) async-start(), calls=%async_computation.9 | async-start | bytes 557056 | tf_op jit(solution)/shard_map/reduce_scatter | solution.py:278
  7.2 0.8 copy-start.4
  8.0 0.7 copy-start.8
  8.7 0.7 copy-start.9
  47.4 28.3 %copy-start.3 = (bf16[1,128,4096]{2,1,0:T(8,128)(2,1)S(1)}, bf16[1,128,4096]{2,1,0:T(8,128)(2,1)}, u32[]{:S(2)}) copy-start(bf16[1,128,4096]{2,1,0:T(8,128)(2,1)} %param.16) | copy-start | bytes 3145732
  48.6 27.2 %copy-start.1 = (bf16[1,4096,128]{2,1,0:T(8,128)(2,1)S(1)}, bf16[1,4096,128]{2,1,0:T(8,128)(2,1)}, u32[]{:S(2)}) copy-start(bf16[1,4096,128]{2,1,0:T(8,128)(2,1)} %param.14) | copy-start | bytes 3145732
  48.6 27.1 %copy-start.2 = (bf16[1,4096,128]{2,1,0:T(8,128)(2,1)S(1)}, bf16[1,4096,128]{2,1,0:T(8,128)(2,1)}, u32[]{:S(2)}) copy-start(bf16[1,4096,128]{2,1,0:T(8,128)(2,1)} %param.15) | copy-start | bytes 3145732
  48.6 27.1 %copy-start.6 = (f32[4096]{0:T(1024)S(1)}, f32[4096]{0:T(1024)}, u32[]{:S(2)}) copy-start(f32[4096]{0:T(1024)} %param.11) | copy-start | bytes 49156
  102.5 26.1 %copy-start = (bf16[128,2048]{1,0:T(8,128)(2,1)S(1)}, bf16[128,2048]{1,0:T(8,128)(2,1)}, u32[]{:S(2)}) copy-start(bf16[128,2048]{1,0:T(8,128)(2,1)} %weight_ref.3) | copy-start | bytes 1572868
  102.5 26.1 %copy-start.5 = (bf16[128,128]{1,0:T(8,128)(2,1)S(1)}, bf16[128,128]{1,0:T(8,128)(2,1)}, u32[]{:S(2)}) copy-start(bf16[128,128]{1,0:T(8,128)(2,1)} %tok_ref.3) | copy-start | bytes 98308
  104.2 38.6 %copy-start.7 = (bf16[128,64]{0,1:T(8,128)(2,1)S(1)}, bf16[128,64]{0,1:T(8,128)(2,1)}, u32[]{:S(2)}) copy-start(bf16[128,64]{0,1:T(8,128)(2,1)} %param.18) | copy-start | bytes 49156
  104.2 38.6 %copy-start.10 = (s32[128]{0:T(128)S(1)}, s32[128]{0:T(128)}, u32[]{:S(2)}) copy-start(s32[128]{0:T(128)} %param.19) | copy-start | bytes 1540
  188.3 37.1 %all-to-all-start.7 = ((bf16[64,80,128]{2,1,0:T(8,128)(2,1)}), bf16[64,80,128]{2,1,0:T(8,128)(2,1)}, u32[]{:S(2)}, u32[]{:S(2)}) async-start(bf16[64,80,128]{2,1,0:T(8,128)(2,1)} %bitcast.14), calls=%async_computation.7 | async-start | bytes 2621440 | tf_op jit(solution)/shard_map/all_to_all | solution.py:238
  224.0 0.8 copy-start.11
Sparse Core Ops, SparseCore 0:
  159.7 64.3 reduce-scatter.1

commit v5 on v3

--- a/solution.py
+++ b/solution.py
@@ -13,13 +13,14 @@
 group = 4
 
 
-def call(body, outs, *operands, limit=16):
+def call(body, outs, *operands, limit=16, scalars=0):
     vmem = pl.BlockSpec(memory_space=pltpu.VMEM)
+    smem = pl.BlockSpec(memory_space=pltpu.SMEM)
     single = not isinstance(outs, (list, tuple))
     return pl.pallas_call(
         body,
         out_shape=outs,
-        in_specs=[vmem] * len(operands),
+        in_specs=[smem] * scalars + [vmem] * (len(operands) - scalars),
         out_specs=vmem if single else [vmem] * len(outs),
         compiler_params=pltpu.CompilerParams(vmem_limit_bytes=limit * 1024 * 1024),
     )(*operands)
@@ -113,7 +114,7 @@
         for inner in range(group):
             block = g * group + inner
             chosen = selection(block_meta(gathered_ref, block, rows), inner, capacity, True)
-            total = total + contract(chosen, grad_ref[block], 1, 1)
+            total = total + contract(chosen, grad_ref[block, 0:rows, :], 1, 1)
         total = total.astype(bf16)
         for e in range(out_ref.shape[1]):
             for pair in range(out_ref.shape[0]):
@@ -185,19 +186,39 @@
         out_ref[p] = scaled
 
 
-def gradients(cot_ref, state_ref, weight_ref, state_grad_ref, pieces_ref):
+def gradients(cot_ref, state_ref, weight_ref, out_ref):
+    width = weight_ref.shape[0]
     state_grad = jnp.dot(
         weight_ref[...], cot_ref[...], preferred_element_type=f32
     ).astype(bf16)
-    for copy in range(state_grad_ref.shape[0]):
-        state_grad_ref[copy] = state_grad
     state = state_ref[...]
-    width = cot_ref.shape[0] // pieces_ref.shape[0]
-    for p in range(pieces_ref.shape[0]):
-        pieces_ref[p] = contract(state, cot_ref[p * width : (p + 1) * width, :], 1, 1).astype(bf16)
-
-
-def down_gradient(hidden_ref, rows_ref, out_ref):
+    near = out_ref.shape[1] // width - 1
+    columns = cot_ref.shape[0] // (out_ref.shape[0] * near)
+    for q in range(out_ref.shape[0]):
+        out_ref[q, 0:width, :] = state_grad
+        for p in range(near):
+            at = (q * near + p) * columns
+            out_ref[q, (p + 1) * width : (p + 2) * width, :] = contract(
+                state, cot_ref[at : at + columns, :], 1, 1
+            ).astype(bf16)
+
+
+def add_parts(parity_ref, parts_ref, mine_ref, other_ref):
+    width = mine_ref.shape[0]
+    totals = [
+        sum(
+            parts_ref[q, (p + 1) * width : (p + 2) * width, :].astype(f32)
+            for q in range(parts_ref.shape[0])
+        )
+        for p in (0, 1)
+    ]
+    even = parity_ref[0] == 0
+    mine_ref[...] = jnp.where(even, totals[0], totals[1])
+    other_ref[...] = jnp.where(even, totals[1], totals[0])
+
+
+def down_gradient(hidden_ref, rows_ref, mine_ref, other_ref, out_ref, key_value_ref):
+    key_value_ref[...] = mine_ref[...] + other_ref[...]
     hidden = hidden_ref[...].astype(f32).T.astype(bf16)
     pairs, parts, half, width = rows_ref.shape
     for p in range(parts):
@@ -263,19 +284,23 @@
         form_cotangent, shape(*proj.shape), proj, key_value_target.T, concept_mask[None, :]
     )
     cotangent = exchange(spread, "expert").reshape(keys, rows)
-    state_grad, pieces = call(
-        gradients,
-        [shape(far, width, rows), shape(blocks, width, keys // blocks)],
-        cotangent,
-        state,
-        key_value_weight,
-    )
-    key_value_grad = lax.psum_scatter(
-        pieces, ("far", "near"), scatter_dimension=0, tiled=True
-    )[0].astype(f32)
-    all_grads = exchange(state_grad, "far")
+    sent = call(
+        gradients, shape(far, (near + 1) * width, rows), cotangent, state, key_value_weight
+    )
+    all_grads = exchange(sent, "far")
+    part = shape(width, keys // blocks, dtype=f32)
+    mine, other = call(
+        add_parts,
+        [part, part],
+        lax.axis_index("near").astype(jnp.int32)[None],
+        all_grads,
+        scalars=1,
+    )
+    other = lax.ppermute(other, "near", [(0, 1), (1, 0)])
     landed = route(call(dispatch_grad, slots, gathered, all_grads))
-    down_grad = call(down_gradient, shape(*down_weight.shape[1:]), hidden, landed)
+    down_grad, key_value_grad = call(
+        down_gradient, [shape(*down_weight.shape[1:]), part], hidden, landed, mine, other
+    )
     return (down_grad[None], key_value_grad)
 
 

time: 270 us -> 230 us (0.85)
  waiting for transfers between devices: 67.3 us -> 15.4 us
  blocking collectives: 167 us -> 184 us
  between operations: 14.1 us -> 0.77 us
  starting transfers between devices: 6.59 us -> 16.2 us
    reduce_scatter x1 -> x0, waiting for transfers between devices: 66.6 us -> none  [per_device(): lax.psum_scatter(pieces, ('far', 'near'), scatter_dimension=0, tiled=True)]
    all_to_all x7, blocking collectives: 167 us -> 184 us  [exchange(): return lax.all_to_all(value, axis, split_axis=0, concat_axis=0, tiled=True)]
    ppermute x0 -> x1, waiting for transfers between devices: none -> 14.3 us  [per_device(): other = lax.ppermute(other, 'near', [(0, 1), (1, 0)])]
    all_to_all x1, starting transfers between devices: 6.55 us -> 12.7 us  [exchange(): return lax.all_to_all(value, axis, split_axis=0, concat_axis=0, tiled=True)]
    ppermute x0 -> x1, starting transfers between devices: none -> 3.51 us  [per_device(): other = lax.ppermute(other, 'near', [(0, 1), (1, 0)])]
    pallas_call x9 -> x10, Pallas kernels: 10.4 us -> 9.65 us  [call(): pl.pallas_call(body, out_shape=outs, in_specs=[smem] * scalars + [vmem] *...]
  transfers between devices with their start and end apart: 2 -> 2, of which waited for: 1 -> 2; matrix products, arithmetic and copies ran while one was open for 1% -> 0% of each run, Pallas kernels for 0% -> 0%
where the time goes in v5:
time: 230 us; the launch traced here: 228 us
  blocking collectives  184 us (80%)
  starting transfers between devices  16.2 us (7%)
  waiting for transfers between devices  15.4 us (7%)
  Pallas kernels  9.65 us (4%)
    all_to_all x7, blocking collectives, exchange(): return lax.all_to_all(value, axis, split_axis=0, concat_axis=0, tiled=True)  184 us
    ppermute x1, waiting for transfers between devices, per_device(): other = lax.ppermute(other, 'near', [(0, 1), (1, 0)])  14.3 us
    all_to_all x1, starting transfers between devices, exchange(): return lax.all_to_all(value, axis, split_axis=0, concat_axis=0, tiled=True)  12.7 us
    pallas_call x10, Pallas kernels, call(): pl.pallas_call(body, out_shape=outs, in_specs=[smem] * scalars + [vmem] *...  9.65 us
  transfers between devices with their start and end apart: 2, of which 2 were waited for; matrix products, arithmetic and copies ran while one was open for 0% of the time, Pallas kernels for 0%

profile of v5, /device:TPU:6, one launch (start us, length us, event | category | flops | bytes accessed | tf_op | source)
XLA Modules:
  0.0 228.0 jit_solution(9890470328097553526)
XLA Ops:
  0.6 0.0 copy-start.4
  0.6 0.7 copy-done.4
  1.4 0.0 copy-start.8
  1.4 0.7 copy-done.8
  2.1 0.0 copy-start.9
  2.1 0.7 copy-done.9
  2.8 0.2 shard_map.113
  2.9 38.0 %all_to_all.40.gathered_ref = bf16[8,144,128]{2,1,0:T(8,128)(2,1)S(1)} all-to-all(bf16[8,144,128]{2,1,0:T(8,128)(2,1)S(1)} %shard_map.113), channel_id=1, replica_groups=mesh['far'=8,'near'=2,'expert'=32] {'far'}, dimensions={0} | all-to-all | bytes 589824 | tf_op jit(solution)/shard_map/all_to_all | solution.py:254
  40.9 0.0 copy-start.3
  40.9 1.2 shard_map.114
  42.0 0.0 copy-start.1
  42.0 0.0 copy-start.2
  42.1 0.0 copy-start.6
  42.1 27.1 %all_to_all.41 = bf16[64,80,128]{2,1,0:T(8,128)(2,1)S(1)} all-to-all(bf16[64,80,128]{2,1,0:T(8,128)(2,1)S(1)} %bitcast.20), channel_id=1, replica_groups=mesh['far'=8,'near'=2,'expert'=32] {'near','expert'}, dimensions={0} | all-to-all | bytes 2621440 | tf_op jit(solution)/shard_map/all_to_all | solution.py:254
  69.2 0.0 copy-done.3
  69.2 0.0 copy-done.1
  69.2 0.0 copy-done.2
  69.2 0.0 copy-done.6
  69.2 1.5 shard_map.115
  70.7 25.2 %all_to_all.42 = bf16[64,80,128]{2,1,0:T(8,128)(2,1)S(1)} all-to-all(bf16[64,80,128]{2,1,0:T(8,128)(2,1)S(1)} %bitcast.23), channel_id=1, replica_groups=mesh['far'=8,'near'=2,'expert'=32] {'near','expert'}, dimensions={0} | all-to-all | bytes 2621440 | tf_op jit(solution)/shard_map/all_to_all | solution.py:254
  95.9 0.0 copy-start
  95.9 0.0 copy-start.5
  95.9 1.7 shard_map.116
  97.6 0.0 copy-start.7
  97.7 0.0 copy-start.10
  97.7 24.3 %all_to_all.43.pieces_ref = bf16[8,128,128]{2,1,0:T(8,128)(2,1)S(1)} all-to-all(bf16[8,128,128]{2,1,0:T(8,128)(2,1)S(1)} %shard_map.116), channel_id=1, replica_groups=mesh['far'=8,'near'=2,'expert'=32] {'far'}, dimensions={0} | all-to-all | bytes 524288 | tf_op jit(solution)/shard_map/all_to_all | solution.py:254
  122.0 0.0 copy-done
  122.0 0.0 copy-done.5
  122.0 0.4 shard_map.117
  122.4 13.8 %all_to_all.44.pieces_ref = bf16[32,64,128]{2,1,0:T(8,128)(2,1)S(1)} all-to-all(bf16[32,64,128]{2,1,0:T(8,128)(2,1)S(1)} %bitcast.27), channel_id=1, replica_groups=mesh['far'=8,'near'=2,'expert'=32] {'expert'}, dimensions={0} | all-to-all | bytes 1048576 | tf_op jit(solution)/shard_map/all_to_all | solution.py:254
  136.2 0.0 copy-done.7
  136.2 0.0 copy-done.10
  136.2 0.1 shard_map.118
  136.3 15.2 %all_to_all.45 = bf16[32,64,128]{2,1,0:T(8,128)(2,1)S(1)} all-to-all(bf16[32,64,128]{2,1,0:T(8,128)(2,1)S(1)} %shard_map.118), channel_id=1, replica_groups=mesh['far'=8,'near'=2,'expert'=32] {'expert'}, dimensions={0} | all-to-all | bytes 1048576 | tf_op jit(solution)/shard_map/all_to_all | solution.py:254
  151.6 0.6 shard_map.119
  152.2 40.2 %all_to_all.46.grad_ref.parts_ref = bf16[8,384,128]{2,1,0:T(8,128)(2,1)S(1)} all-to-all(bf16[8,384,128]{2,1,0:T(8,128)(2,1)S(1)} %shard_map.119), channel_id=1, replica_groups=mesh['far'=8,'near'=2,'expert'=32] {'far'}, dimensions={0} | all-to-all | bytes 1572864 | tf_op jit(solution)/shard_map/all_to_all | solution.py:254
  192.4 2.2 shard_map.120
  194.6 12.7 %all-to-all-start.7 = ((bf16[64,80,128]{2,1,0:T(8,128)(2,1)}), bf16[64,80,128]{2,1,0:T(8,128)(2,1)S(1)}, u32[]{:S(2)}, u32[]{:S(2)}) async-start(bf16[64,80,128]{2,1,0:T(8,128)(2,1)} %bitcast.14), calls=%async_computation.7 | async-start | bytes 2621440 | tf_op jit(solution)/shard_map/all_to_all | solution.py:254
  207.3 0.1 shard_map.121
  207.4 3.5 %collective-permute-start = (f32[128,128]{1,0:T(8,128)S(1)}, f32[128,128]{1,0:T(8,128)S(1)}, u32[]{:S(2)}, u32[]{:S(2)}) collective-permute-start(f32[128,128]{1,0:T(8,128)S(1)} %get-tuple-element.15), channel_id=1, source_target_pairs={{0,32},{32,0},{1,33},{33,1},{2,34},{34,2},{3,35},{35,3},{4,36},{36... | collective-permute-start | bytes 196616 | tf_op jit(solution)/shard_map/ppermute | solution.py:299
  210.9 14.3 %collective-permute-done.other_ref = f32[128,128]{1,0:T(8,128)S(1)} collective-permute-done((f32[128,128]{1,0:T(8,128)S(1)}, f32[128,128]{1,0:T(8,128)S(1)}, u32[]{:S(2)}, u32[]{:S(2)}) %collective-permute-start) | collective-permute-done | bytes 65568 | tf_op jit(solution)/shard_map/ppermute | solution.py:299
  225.2 1.1 all-to-all-done.7
  226.3 1.7 shard_map.122
Async XLA Ops:
  0.6 0.8 copy-start.4
  1.4 0.7 copy-start.8
  2.1 0.7 copy-start.9
  40.9 28.3 %copy-start.3 = (bf16[1,128,4096]{2,1,0:T(8,128)(2,1)S(1)}, bf16[1,128,4096]{2,1,0:T(8,128)(2,1)}, u32[]{:S(2)}) copy-start(bf16[1,128,4096]{2,1,0:T(8,128)(2,1)} %param.16) | copy-start | bytes 3145732
  42.0 27.2 %copy-start.1 = (bf16[1,4096,128]{2,1,0:T(8,128)(2,1)S(1)}, bf16[1,4096,128]{2,1,0:T(8,128)(2,1)}, u32[]{:S(2)}) copy-start(bf16[1,4096,128]{2,1,0:T(8,128)(2,1)} %param.14) | copy-start | bytes 3145732
  42.0 27.1 %copy-start.2 = (bf16[1,4096,128]{2,1,0:T(8,128)(2,1)S(1)}, bf16[1,4096,128]{2,1,0:T(8,128)(2,1)}, u32[]{:S(2)}) copy-start(bf16[1,4096,128]{2,1,0:T(8,128)(2,1)} %param.15) | copy-start | bytes 3145732
  42.1 27.1 %copy-start.6 = (f32[4096]{0:T(1024)S(1)}, f32[4096]{0:T(1024)}, u32[]{:S(2)}) copy-start(f32[4096]{0:T(1024)} %param.11) | copy-start | bytes 49156
  95.9 26.1 %copy-start = (bf16[128,2048]{1,0:T(8,128)(2,1)S(1)}, bf16[128,2048]{1,0:T(8,128)(2,1)}, u32[]{:S(2)}) copy-start(bf16[128,2048]{1,0:T(8,128)(2,1)} %weight_ref.3) | copy-start | bytes 1572868
  95.9 26.1 %copy-start.5 = (bf16[128,128]{1,0:T(8,128)(2,1)S(1)}, bf16[128,128]{1,0:T(8,128)(2,1)}, u32[]{:S(2)}) copy-start(bf16[128,128]{1,0:T(8,128)(2,1)} %tok_ref.3) | copy-start | bytes 98308
  97.6 38.6 %copy-start.7 = (bf16[128,64]{0,1:T(8,128)(2,1)S(1)}, bf16[128,64]{0,1:T(8,128)(2,1)}, u32[]{:S(2)}) copy-start(bf16[128,64]{0,1:T(8,128)(2,1)} %param.18) | copy-start | bytes 49156
  97.7 38.6 %copy-start.10 = (s32[128]{0:T(128)S(1)}, s32[128]{0:T(128)}, u32[]{:S(2)}) copy-start(s32[128]{0:T(128)} %param.19) | copy-start | bytes 1540
  194.6 31.7 %all-to-all-start.7 = ((bf16[64,80,128]{2,1,0:T(8,128)(2,1)}), bf16[64,80,128]{2,1,0:T(8,128)(2,1)S(1)}, u32[]{:S(2)}, u32[]{:S(2)}) async-start(bf16[64,80,128]{2,1,0:T(8,128)(2,1)} %bitcast.14), calls=%async_computation.7 | async-start | bytes 2621440 | tf_op jit(solution)/shard_map/all_to_all | solution.py:254
  207.4 17.8 %collective-permute-start = (f32[128,128]{1,0:T(8,128)S(1)}, f32[128,128]{1,0:T(8,128)S(1)}, u32[]{:S(2)}, u32[]{:S(2)}) collective-permute-start(f32[128,128]{1,0:T(8,128)S(1)} %get-tuple-element.15), channel_id=1, source_target_pairs={{0,32},{32,0},{1,33},{33,1},{2,34},{34,2},{3,35},{35,3},{4,36},{36... | collective-permute-start | bytes 196616 | tf_op jit(solution)/shard_map/ppermute | solution.py:299

commit v6 on v3

--- a/solution.py
+++ b/solution.py
@@ -10,10 +10,11 @@
 bf16 = jnp.bfloat16
 eps_norm = 1e-06
 meta_rows = 16
+half_tile = 32
 group = 4
 
 
-def call(body, outs, *operands, limit=16):
+def call(body, outs, *operands, limit=16, cost=None):
     vmem = pl.BlockSpec(memory_space=pltpu.VMEM)
     single = not isinstance(outs, (list, tuple))
     return pl.pallas_call(
@@ -21,6 +22,7 @@
         out_shape=outs,
         in_specs=[vmem] * len(operands),
         out_specs=vmem if single else [vmem] * len(outs),
+        cost_estimate=cost,
         compiler_params=pltpu.CompilerParams(vmem_limit_bytes=limit * 1024 * 1024),
     )(*operands)
 
@@ -104,9 +106,9 @@
                 out_ref[pair, e, g * tall : (g + 1) * tall, :] = total[e * tall : (e + 1) * tall]
 
 
-def dispatch_grad(gathered_ref, grad_ref, out_ref):
+def dispatch_grad(gathered_ref, grad_ref, same_ref, cross_ref, out_ref):
     blocks, rows = gathered_ref.shape[0], gathered_ref.shape[1] - meta_rows
-    capacity = out_ref.shape[2] // blocks
+    capacity = (out_ref.shape[2] - half_tile) // blocks
     tall = group * capacity
     for g in range(blocks // group):
         total = 0.0
@@ -118,6 +120,15 @@
         for e in range(out_ref.shape[1]):
             for pair in range(out_ref.shape[0]):
                 out_ref[pair, e, g * tall : (g + 1) * tall, :] = total[e * tall : (e + 1) * tall]
+    even = lax.axis_index("near") == 0
+    same, cross = same_ref[...].astype(f32), cross_ref[...].astype(f32)
+    tiles = [
+        jnp.where(even, same, cross).astype(bf16),
+        jnp.where(even, cross, same).astype(bf16),
+    ]
+    for pair in range(out_ref.shape[0]):
+        for e in range(out_ref.shape[1]):
+            out_ref[pair, e, blocks * capacity :, :] = tiles[pair]
 
 
 def expert(rows_ref, gain_ref, gate_ref, up_ref, down_ref, out_ref, hidden_ref):
@@ -165,16 +176,16 @@
             out_ref[block] = jnp.dot(back, chosen, preferred_element_type=f32).astype(bf16)
 
 
-def project(pieces_ref, tok_ref, weight_ref, state_ref, out_ref):
+def project(pieces_ref, tok_ref, weight_ref, out_ref, state_ref):
     total = tok_ref[...].astype(f32).T
     for p in range(pieces_ref.shape[0]):
         total = total + pieces_ref[p].astype(f32)
     state = total.astype(bf16)
-    state_ref[...] = state
+    state_ref[...] = state.astype(f32)
     out_ref[...] = contract(weight_ref[...], state, 0, 0).astype(bf16)
 
 
-def form_cotangent(pieces_ref, target_ref, mask_ref, out_ref):
+def form_cotangent(pieces_ref, target_ref, mask_ref, out_ref, same_ref, cross_ref):
     total = pieces_ref[0].astype(f32)
     for p in range(1, pieces_ref.shape[0]):
         total = total + pieces_ref[p].astype(f32)
@@ -183,28 +194,41 @@
     scaled = scaled.astype(bf16)
     for p in range(out_ref.shape[0]):
         out_ref[p] = scaled
-
-
-def gradients(cot_ref, state_ref, weight_ref, state_grad_ref, pieces_ref):
+    even = (lax.axis_index("expert") // 2) % 2 == 0
+    low, high = scaled[0:half_tile].astype(f32), scaled[half_tile:].astype(f32)
+    same_ref[...] = jnp.where(even, low, high).astype(bf16)
+    cross_ref[...] = jnp.where(even, high, low).astype(bf16)
+
+
+def backpropagate(cot_ref, weight_ref, out_ref):
     state_grad = jnp.dot(
         weight_ref[...], cot_ref[...], preferred_element_type=f32
     ).astype(bf16)
-    for copy in range(state_grad_ref.shape[0]):
-        state_grad_ref[copy] = state_grad
-    state = state_ref[...]
-    width = cot_ref.shape[0] // pieces_ref.shape[0]
-    for p in range(pieces_ref.shape[0]):
-        pieces_ref[p] = contract(state, cot_ref[p * width : (p + 1) * width, :], 1, 1).astype(bf16)
-
-
-def down_gradient(hidden_ref, rows_ref, out_ref):
+    for copy in range(out_ref.shape[0]):
+        out_ref[copy] = state_grad
+
+
+def narrow(state_ref, out_ref):
+    out_ref[...] = state_ref[...].astype(bf16)
+
+
+def down_gradient(hidden_ref, rows_ref, state_ref, out_ref, key_value_ref):
     hidden = hidden_ref[...].astype(f32).T.astype(bf16)
-    pairs, parts, half, width = rows_ref.shape
+    pairs, parts, tall, width = rows_ref.shape
+    half = tall - half_tile
     for p in range(parts):
-        rows = jnp.concatenate([rows_ref[h, p] for h in range(pairs)], axis=0)
+        rows = jnp.concatenate([rows_ref[h, p, 0:half, :] for h in range(pairs)], axis=0)
         out_ref[:, p * width : (p + 1) * width] = jnp.dot(
             hidden, rows, preferred_element_type=f32
         ).astype(bf16)
+    total = 0.0
+    for block in range(state_ref.shape[0]):
+        cotangent = jnp.concatenate(
+            [rows_ref[h, 2 * block + side, half:, :] for side in (0, 1) for h in range(pairs)],
+            axis=0,
+        )
+        total = total + contract(state_ref[block], cotangent, 1, 1)
+    key_value_ref[...] = total
 
 
 def per_device(
@@ -237,10 +261,10 @@
     )
     gathered = exchange(packed, "far")
     slots = shape(near, experts, far * capacity, width)
-    spots = (near * experts, far * capacity, width)
 
     def route(value):
-        return exchange(value.reshape(spots), ("near", "expert")).reshape(slots.shape)
+        flat = value.reshape(near * experts, *value.shape[2:])
+        return exchange(flat, ("near", "expert")).reshape(value.shape)
 
     arrived = route(call(dispatch, slots, gathered))
     out_rows, hidden = call(
@@ -255,27 +279,51 @@
     )
     returned = route(out_rows)
     mixed = exchange(call(combine, shape(far, width, rows), gathered, returned), "far")
-    state, proj = call(
-        project, [shape(width, rows), shape(keys, rows)], mixed, tokens, key_value_weight
+    proj, state = call(
+        project,
+        [shape(keys, rows), shape(width, rows, dtype=f32)],
+        mixed,
+        tokens,
+        key_value_weight,
+    )
+    states = lax.all_gather(state, ("far", "near"), axis=0)
+    states = call(
+        narrow,
+        shape(blocks, width, rows),
+        states,
+        cost=pl.CostEstimate(flops=10**12, bytes_accessed=3 << 19, transcendentals=0),
     )
     proj = exchange(proj.reshape(experts, keys // experts, rows), "expert")
-    spread = call(
-        form_cotangent, shape(*proj.shape), proj, key_value_target.T, concept_mask[None, :]
-    )
+    part = shape(half_tile, rows)
+    spread, same, cross = call(
+        form_cotangent,
+        [shape(*proj.shape), part, part],
+        proj,
+        key_value_target.T,
+        concept_mask[None, :],
+    )
+    moves = [[], []]
+    for block in range(blocks):
+        for c in range(experts):
+            plane, lane = c // 2, 2 * block + c % 2
+            for flip in (0, 1):
+                moves[flip].append((block * experts + c, (plane ^ flip) * experts + lane))
+    everyone = ("far", "near", "expert")
+    same = lax.ppermute(same, everyone, moves[0])
+    cross = lax.ppermute(cross, everyone, moves[1])
     cotangent = exchange(spread, "expert").reshape(keys, rows)
-    state_grad, pieces = call(
-        gradients,
-        [shape(far, width, rows), shape(blocks, width, keys // blocks)],
-        cotangent,
-        state,
-        key_value_weight,
-    )
-    key_value_grad = lax.psum_scatter(
-        pieces, ("far", "near"), scatter_dimension=0, tiled=True
-    )[0].astype(f32)
+    state_grad = call(backpropagate, shape(far, width, rows), cotangent, key_value_weight)
     all_grads = exchange(state_grad, "far")
-    landed = route(call(dispatch_grad, slots, gathered, all_grads))
-    down_grad = call(down_gradient, shape(*down_weight.shape[1:]), hidden, landed)
+    tall_slots = shape(near, experts, far * capacity + half_tile, width)
+    landed = route(call(dispatch_grad, tall_slots, gathered, all_grads, same, cross))
+    landed, states = lax.optimization_barrier((landed, states))
+    down_grad, key_value_grad = call(
+        down_gradient,
+        [shape(*down_weight.shape[1:]), shape(width, keys // blocks, dtype=f32)],
+        hidden,
+        landed,
+        states,
+    )
     return (down_grad[None], key_value_grad)
 
 

time: 270 us -> 241 us (0.89)
  waiting for transfers between devices: 67.3 us -> 37.5 us
  blocking collectives: 167 us -> 144 us
  starting transfers between devices: 6.59 us -> 28.2 us
    reduce_scatter x1 -> x0, waiting for transfers between devices: 66.6 us -> none  [per_device(): lax.psum_scatter(pieces, ('far', 'near'), scatter_dimension=0, tiled=True)]
    all_to_all x1 -> x2, waiting for transfers between devices: 0.01 us -> 29 us  [exchange(): return lax.all_to_all(value, axis, split_axis=0, concat_axis=0, tiled=True)]
    all_to_all x7 -> x6, blocking collectives: 167 us -> 144 us  [exchange(): return lax.all_to_all(value, axis, split_axis=0, concat_axis=0, tiled=True)]
    all_to_all x1 -> x2, starting transfers between devices: 6.55 us -> 18.7 us  [exchange(): return lax.all_to_all(value, axis, split_axis=0, concat_axis=0, tiled=True)]
    ppermute x0 -> x2, starting transfers between devices: none -> 9.46 us  [the longest x1 7.32 us: per_device(): same = lax.ppermute(same, everyone, moves[0])]
    ppermute x0 -> x2, waiting for transfers between devices: none -> 8.45 us  [the longest x1 5.46 us: per_device(): cross = lax.ppermute(cross, everyone, moves[1])]
    pallas_call x9 -> x10, Pallas kernels: 10.4 us -> 12.4 us  [call(): pl.pallas_call(body, out_shape=outs, in_specs=[vmem] * len(operands), out...]
  transfers between devices with their start and end apart: 2 -> 5, of which waited for: 1 -> 4; matrix products, arithmetic and copies ran while one was open for 1% -> 0% of each run, Pallas kernels for 0% -> 1%
where the time goes in v6:
time: 241 us; the launch traced here: 239 us
  blocking collectives  144 us (60%)
  waiting for transfers between devices  37.5 us (16%)
  starting transfers between devices  28.2 us (12%)
  between operations  14.2 us (6%)
  Pallas kernels  12.4 us (5%)
  local copies, waits for them, and re-layouts  3.37 us (1%)
    all_to_all x6, blocking collectives, exchange(): return lax.all_to_all(value, axis, split_axis=0, concat_axis=0, tiled=True)  144 us
    all_to_all x2, waiting for transfers between devices, exchange(): return lax.all_to_all(value, axis, split_axis=0, concat_axis=0, tiled=True)  29 us
    all_to_all x2, starting transfers between devices, exchange(): return lax.all_to_all(value, axis, split_axis=0, concat_axis=0, tiled=True)  18.7 us
    pallas_call x10, Pallas kernels, call(): pl.pallas_call(body, out_shape=outs, in_specs=[vmem] * len(operands), out...  12.4 us
    ppermute x1, starting transfers between devices, per_device(): same = lax.ppermute(same, everyone, moves[0])  7.32 us
    ppermute x1, waiting for transfers between devices, per_device(): cross = lax.ppermute(cross, everyone, moves[1])  5.46 us
  transfers between devices with their start and end apart: 5, of which 4 were waited for; matrix products, arithmetic and copies ran while one was open for 0% of the time, Pallas kernels for 1%

profile of v6, /device:TPU:6, one launch (start us, length us, event | category | flops | bytes accessed | tf_op | source)
XLA Modules:
  0.0 239.2 jit_solution(9474675410034043910)
XLA Ops:
  7.2 0.0 all-gather.3.cloned.1.call-start
  7.2 0.0 copy-start.4
  7.2 0.7 copy-done.4
  8.0 0.0 copy-start.8
  8.0 0.7 copy-done.8
  8.7 0.0 copy-start.9
  8.7 0.7 copy-done.9
  9.3 0.2 shard_map.113
  9.5 38.0 %all_to_all.40.gathered_ref = bf16[8,144,128]{2,1,0:T(8,128)(2,1)S(1)} all-to-all(bf16[8,144,128]{2,1,0:T(8,128)(2,1)S(1)} %shard_map.113), channel_id=1, replica_groups=mesh['far'=8,'near'=2,'expert'=32] {'far'}, dimensions={0} | all-to-all | bytes 589824 | tf_op jit(solution)/shard_map/all_to_all | solution.py:257
  47.4 0.0 copy-start.3
  47.4 1.2 shard_map.114
  48.6 0.0 copy-start.1
  48.6 0.0 copy-start.2
  48.6 0.0 copy-start.6
  48.6 27.1 %all_to_all.41 = bf16[64,80,128]{2,1,0:T(8,128)(2,1)S(1)} all-to-all(bf16[64,80,128]{2,1,0:T(8,128)(2,1)S(1)} %bitcast.19), channel_id=1, replica_groups=mesh['far'=8,'near'=2,'expert'=32] {'near','expert'}, dimensions={0} | all-to-all | bytes 2621440 | tf_op jit(solution)/shard_map/all_to_all | solution.py:257
  75.8 0.0 copy-done.3
  75.8 0.0 copy-done.1
  75.8 0.0 copy-done.2
  75.8 0.0 copy-done.6
  75.8 1.5 shard_map.115
  77.3 25.2 %all_to_all.42 = bf16[64,80,128]{2,1,0:T(8,128)(2,1)S(1)} all-to-all(bf16[64,80,128]{2,1,0:T(8,128)(2,1)S(1)} %bitcast.22), channel_id=1, replica_groups=mesh['far'=8,'near'=2,'expert'=32] {'near','expert'}, dimensions={0} | all-to-all | bytes 2621440 | tf_op jit(solution)/shard_map/all_to_all | solution.py:257
  102.5 0.0 copy-start
  102.5 0.0 copy-start.5
  102.5 1.7 shard_map.116
  104.2 0.0 copy-start.7
  104.2 0.0 copy-start.10
  104.2 24.3 %all_to_all.43.pieces_ref = bf16[8,128,128]{2,1,0:T(8,128)(2,1)S(1)} all-to-all(bf16[8,128,128]{2,1,0:T(8,128)(2,1)S(1)} %shard_map.116), channel_id=1, replica_groups=mesh['far'=8,'near'=2,'expert'=32] {'far'}, dimensions={0} | all-to-all | bytes 524288 | tf_op jit(solution)/shard_map/all_to_all | solution.py:257
  128.6 0.0 copy-done
  128.6 0.0 copy-done.5
  128.6 0.8 shard_map.117
  129.3 0.0 all-gather.3.cloned.1.call-update
  129.3 13.8 %all_to_all.44.pieces_ref = bf16[32,64,128]{2,1,0:T(8,128)(2,1)S(1)} all-to-all(bf16[32,64,128]{2,1,0:T(8,128)(2,1)S(1)} %bitcast.26), channel_id=1, replica_groups=mesh['far'=8,'near'=2,'expert'=32] {'expert'}, dimensions={0} | all-to-all | bytes 1048576 | tf_op jit(solution)/shard_map/all_to_all | solution.py:257
  143.2 0.0 copy-done.7
  143.2 0.0 copy-done.10
  143.2 0.1 shard_map.118
  143.3 15.2 %all_to_all.45 = bf16[32,64,128]{2,1,0:T(8,128)(2,1)S(1)} all-to-all(bf16[32,64,128]{2,1,0:T(8,128)(2,1)S(1)} %get-tuple-element.16), channel_id=1, replica_groups=mesh['far'=8,'near'=2,'expert'=32] {'expert'}, dimensions={0} | all-to-all | bytes 1048576 | tf_op jit(solution)/shard_map/all_to_all | solution.py:257
  158.5 1.0 shard_map.119
  159.5 3.4 %all-to-all-start.6 = ((bf16[8,128,128]{2,1,0:T(8,128)(2,1)}), bf16[8,128,128]{2,1,0:T(8,128)(2,1)S(1)}, u32[]{:S(2)}, u32[]{:S(2)}) async-start(bf16[8,128,128]{2,1,0:T(8,128)(2,1)} %shard_map.119), calls=%async_computation.6 | async-start | bytes 524288 | tf_op jit(solution)/shard_map/all_to_all | solution.py:257
  162.9 7.3 %collective-permute-start = (bf16[32,128]{1,0:T(8,128)(2,1)S(1)}, bf16[32,128]{1,0:T(8,128)(2,1)S(1)}, u32[]{:S(2)}, u32[]{:S(2)}) collective-permute-start(bf16[32,128]{1,0:T(8,128)(2,1)S(1)} %get-tuple-element.17), channel_id=1, source_target_pairs={{0,0},{1,1},{2,32},{3,33},{4,64},{5,65},{6,96},{7,97},{8,128},{9,1... | collective-permute-start | bytes 24584 | tf_op jit(solution)/shard_map/ppermute | solution.py:312
  170.3 2.1 collective-permute-start.1
  172.4 3.0 %collective-permute-done.same_ref = bf16[32,128]{1,0:T(8,128)(2,1)S(1)} collective-permute-done((bf16[32,128]{1,0:T(8,128)(2,1)S(1)}, bf16[32,128]{1,0:T(8,128)(2,1)S(1)}, u32[]{:S(2)}, u32[]{:S(2)}) %collective-permute-start) | collective-permute-done | bytes 8224 | tf_op jit(solution)/shard_map/ppermute | solution.py:312
  175.4 5.5 %collective-permute-done.1.cross_ref = bf16[32,128]{1,0:T(8,128)(2,1)S(1)} collective-permute-done((bf16[32,128]{1,0:T(8,128)(2,1)S(1)}, bf16[32,128]{1,0:T(8,128)(2,1)S(1)}, u32[]{:S(2)}, u32[]{:S(2)}) %collective-permute-start.1) | collective-permute-done | bytes 8224 | tf_op jit(solution)/shard_map/ppermute | solution.py:313
  180.9 5.9 %all-to-all-done.6.grad_ref = bf16[8,128,128]{2,1,0:T(8,128)(2,1)S(1)} async-done(((bf16[8,128,128]{2,1,0:T(8,128)(2,1)}), bf16[8,128,128]{2,1,0:T(8,128)(2,1)S(1)}, u32[]{:S(2)}, u32[]{:S(2)}) %all-to-all-start.6) | async-done | bytes 262176 | tf_op jit(solution)/shard_map/all_to_all | solution.py:257
  186.7 2.4 shard_map.120
  189.1 15.3 %all-to-all-start.7 = ((bf16[64,112,128]{2,1,0:T(8,128)(2,1)}), bf16[64,112,128]{2,1,0:T(8,128)(2,1)}, u32[]{:S(2)}, u32[]{:S(2)}) async-start(bf16[64,112,128]{2,1,0:T(8,128)(2,1)} %bitcast.14), calls=%async_computation.7 | async-start | bytes 3670016 | tf_op jit(solution)/shard_map/all_to_all | solution.py:257
  204.4 0.0 all-gather.3.cloned.1.call-done
  204.4 0.0 copy-start.11
  204.4 1.2 copy-done.11
  205.7 0.1 shard_map.121.state_ref
  205.7 23.1 %all-to-all-done.7 = bf16[64,112,128]{2,1,0:T(8,128)(2,1)} async-done(((bf16[64,112,128]{2,1,0:T(8,128)(2,1)}), bf16[64,112,128]{2,1,0:T(8,128)(2,1)}, u32[]{:S(2)}, u32[]{:S(2)}) %all-to-all-start.7) | async-done | bytes 1835040 | tf_op jit(solution)/shard_map/all_to_all | solution.py:257
  228.8 3.5 %shard_map.122 = (bf16[128,4096]{1,0:T(8,128)(2,1)}, f32[128,128]{1,0:T(8,128)}) custom-call(bf16[160,128]{1,0:T(8,128)(2,1)S(1)} %get-tuple-element.13.hidden_ref, bf16[2,32,112,128]{3,2,1,0:T(8,128)(2,1)} %bitcast.15.rows_ref, bf16[16,128,128]{2,1,0:T(8,128)(2,1)S(1)} %shard_map.121.state_ref), custom_call_target="tpu_custom_call" | custom-call | tf_op jit(solution)/shard_map/pallas_call | solution.py:20
Async XLA Ops:
  7.2 197.3 %all-gather.3.cloned.1.call-start = ((), (), s32[]{:S(2)}) async-start(), calls=%async_computation.8 | async-start | bytes 1114112 | tf_op jit(solution)/shard_map/all_gather | solution.py:289
  7.2 0.8 copy-start.4
  8.0 0.7 copy-start.8
  8.7 0.7 copy-start.9
  47.4 28.3 %copy-start.3 = (bf16[1,128,4096]{2,1,0:T(8,128)(2,1)S(1)}, bf16[1,128,4096]{2,1,0:T(8,128)(2,1)}, u32[]{:S(2)}) copy-start(bf16[1,128,4096]{2,1,0:T(8,128)(2,1)} %param.16) | copy-start | bytes 3145732
  48.6 27.2 %copy-start.1 = (bf16[1,4096,128]{2,1,0:T(8,128)(2,1)S(1)}, bf16[1,4096,128]{2,1,0:T(8,128)(2,1)}, u32[]{:S(2)}) copy-start(bf16[1,4096,128]{2,1,0:T(8,128)(2,1)} %param.14) | copy-start | bytes 3145732
  48.6 27.1 %copy-start.2 = (bf16[1,4096,128]{2,1,0:T(8,128)(2,1)S(1)}, bf16[1,4096,128]{2,1,0:T(8,128)(2,1)}, u32[]{:S(2)}) copy-start(bf16[1,4096,128]{2,1,0:T(8,128)(2,1)} %param.15) | copy-start | bytes 3145732
  48.6 27.1 %copy-start.6 = (f32[4096]{0:T(1024)S(1)}, f32[4096]{0:T(1024)}, u32[]{:S(2)}) copy-start(f32[4096]{0:T(1024)} %param.11) | copy-start | bytes 49156
  102.5 26.1 %copy-start = (bf16[128,2048]{1,0:T(8,128)(2,1)S(1)}, bf16[128,2048]{1,0:T(8,128)(2,1)}, u32[]{:S(2)}) copy-start(bf16[128,2048]{1,0:T(8,128)(2,1)} %weight_ref.3) | copy-start | bytes 1572868
  102.5 26.1 %copy-start.5 = (bf16[128,128]{1,0:T(8,128)(2,1)S(1)}, bf16[128,128]{1,0:T(8,128)(2,1)}, u32[]{:S(2)}) copy-start(bf16[128,128]{1,0:T(8,128)(2,1)} %tok_ref.3) | copy-start | bytes 98308
  104.2 39.0 %copy-start.7 = (bf16[128,64]{0,1:T(8,128)(2,1)S(1)}, bf16[128,64]{0,1:T(8,128)(2,1)}, u32[]{:S(2)}) copy-start(bf16[128,64]{0,1:T(8,128)(2,1)} %param.18) | copy-start | bytes 49156
  104.2 38.9 %copy-start.10 = (s32[128]{0:T(128)S(1)}, s32[128]{0:T(128)}, u32[]{:S(2)}) copy-start(s32[128]{0:T(128)} %param.19) | copy-start | bytes 1540
  159.5 27.2 %all-to-all-start.6 = ((bf16[8,128,128]{2,1,0:T(8,128)(2,1)}), bf16[8,128,128]{2,1,0:T(8,128)(2,1)S(1)}, u32[]{:S(2)}, u32[]{:S(2)}) async-start(bf16[8,128,128]{2,1,0:T(8,128)(2,1)} %shard_map.119), calls=%async_computation.6 | async-start | bytes 524288 | tf_op jit(solution)/shard_map/all_to_all | solution.py:257
  162.9 12.5 %collective-permute-start = (bf16[32,128]{1,0:T(8,128)(2,1)S(1)}, bf16[32,128]{1,0:T(8,128)(2,1)S(1)}, u32[]{:S(2)}, u32[]{:S(2)}) collective-permute-start(bf16[32,128]{1,0:T(8,128)(2,1)S(1)} %get-tuple-element.17), channel_id=1, source_target_pairs={{0,0},{1,1},{2,32},{3,33},{4,64},{5,65},{6,96},{7,97},{8,128},{9,1... | collective-permute-start | bytes 24584 | tf_op jit(solution)/shard_map/ppermute | solution.py:312
  170.3 10.6 %collective-permute-start.1 = (bf16[32,128]{1,0:T(8,128)(2,1)S(1)}, bf16[32,128]{1,0:T(8,128)(2,1)S(1)}, u32[]{:S(2)}, u32[]{:S(2)}) collective-permute-start(bf16[32,128]{1,0:T(8,128)(2,1)S(1)} %get-tuple-element.18), channel_id=1, source_target_pairs={{0,32},{1,33},{2,0},{3,1},{4,96},{5,97},{6,64},{7,65},{8,160},{9,1... | collective-permute-start | bytes 24584 | tf_op jit(solution)/shard_map/ppermute | solution.py:313
  189.1 39.7 %all-to-all-start.7 = ((bf16[64,112,128]{2,1,0:T(8,128)(2,1)}), bf16[64,112,128]{2,1,0:T(8,128)(2,1)}, u32[]{:S(2)}, u32[]{:S(2)}) async-start(bf16[64,112,128]{2,1,0:T(8,128)(2,1)} %bitcast.14), calls=%async_computation.7 | async-start | bytes 3670016 | tf_op jit(solution)/shard_map/all_to_all | solution.py:257
  204.4 1.2 copy-start.11
Sparse Core Ops, SparseCore 0:
  129.5 65.3 all-gather.2

commit v7 on v3

--- a/solution.py
+++ b/solution.py
@@ -113,7 +113,7 @@
         for inner in range(group):
             block = g * group + inner
             chosen = selection(block_meta(gathered_ref, block, rows), inner, capacity, True)
-            total = total + contract(chosen, grad_ref[block], 1, 1)
+            total = total + contract(chosen, grad_ref[block, 0:rows, :], 1, 1)
         total = total.astype(bf16)
         for e in range(out_ref.shape[1]):
             for pair in range(out_ref.shape[0]):
@@ -185,19 +185,25 @@
         out_ref[p] = scaled
 
 
-def gradients(cot_ref, state_ref, weight_ref, state_grad_ref, pieces_ref):
+def gradients(cot_ref, state_ref, partner_ref, weight_ref, out_ref):
+    width = weight_ref.shape[0]
+    me = lax.axis_index("near")
     state_grad = jnp.dot(
-        weight_ref[...], cot_ref[...], preferred_element_type=f32
+        weight_ref[...], cot_ref[me], preferred_element_type=f32
     ).astype(bf16)
-    for copy in range(state_grad_ref.shape[0]):
-        state_grad_ref[copy] = state_grad
-    state = state_ref[...]
-    width = cot_ref.shape[0] // pieces_ref.shape[0]
-    for p in range(pieces_ref.shape[0]):
-        pieces_ref[p] = contract(state, cot_ref[p * width : (p + 1) * width, :], 1, 1).astype(bf16)
-
-
-def down_gradient(hidden_ref, rows_ref, out_ref):
+    columns = cot_ref.shape[1] // (2 * out_ref.shape[0])
+    for q in range(out_ref.shape[0]):
+        out_ref[q, 0:width, :] = state_grad
+        at = pl.ds(pl.multiple_of((2 * q + me) * columns, columns), columns)
+        part = contract(state_ref[...], cot_ref[me, at, :], 1, 1)
+        part = part + contract(partner_ref[...], cot_ref[1 - me, at, :], 1, 1)
+        out_ref[q, width:, :] = part.astype(bf16)
+
+
+def down_gradient(hidden_ref, rows_ref, parts_ref, out_ref, key_value_ref):
+    key_value_ref[...] = sum(
+        parts_ref[q, key_value_ref.shape[0] :, :].astype(f32) for q in range(parts_ref.shape[0])
+    )
     hidden = hidden_ref[...].astype(f32).T.astype(bf16)
     pairs, parts, half, width = rows_ref.shape
     for p in range(parts):
@@ -259,23 +265,32 @@
         project, [shape(width, rows), shape(keys, rows)], mixed, tokens, key_value_weight
     )
     proj = exchange(proj.reshape(experts, keys // experts, rows), "expert")
+    partner = lax.ppermute(state, "near", [(0, 1), (1, 0)])
     spread = call(
-        form_cotangent, shape(*proj.shape), proj, key_value_target.T, concept_mask[None, :]
-    )
-    cotangent = exchange(spread, "expert").reshape(keys, rows)
-    state_grad, pieces = call(
+        form_cotangent,
+        shape(near * experts, *proj.shape[1:]),
+        proj,
+        key_value_target.T,
+        concept_mask[None, :],
+    )
+    cotangents = exchange(spread, ("near", "expert")).reshape(near, keys, rows)
+    sent = call(
         gradients,
-        [shape(far, width, rows), shape(blocks, width, keys // blocks)],
-        cotangent,
+        shape(far, 2 * width, rows),
+        cotangents,
         state,
+        partner,
         key_value_weight,
     )
-    key_value_grad = lax.psum_scatter(
-        pieces, ("far", "near"), scatter_dimension=0, tiled=True
-    )[0].astype(f32)
-    all_grads = exchange(state_grad, "far")
+    all_grads = exchange(sent, "far")
     landed = route(call(dispatch_grad, slots, gathered, all_grads))
-    down_grad = call(down_gradient, shape(*down_weight.shape[1:]), hidden, landed)
+    down_grad, key_value_grad = call(
+        down_gradient,
+        [shape(*down_weight.shape[1:]), shape(width, keys // blocks, dtype=f32)],
+        hidden,
+        landed,
+        all_grads,
+    )
     return (down_grad[None], key_value_grad)
 
 

time: 270 us -> 226 us (0.84)
  waiting for transfers between devices: 67.3 us -> 12.7 us
  blocking collectives: 167 us -> 188 us
  between operations: 14.1 us -> 0.76 us
  starting transfers between devices: 6.59 us -> 10.3 us
    reduce_scatter x1 -> x0, waiting for transfers between devices: 66.6 us -> none  [per_device(): lax.psum_scatter(pieces, ('far', 'near'), scatter_dimension=0, tiled=True)]
    all_to_all x7, blocking collectives: 167 us -> 188 us  [exchange(): return lax.all_to_all(value, axis, split_axis=0, concat_axis=0, tiled=True)]
    ppermute x0 -> x1, waiting for transfers between devices: none -> 10.9 us  [per_device(): partner = lax.ppermute(state, 'near', [(0, 1), (1, 0)])]
    ppermute x0 -> x1, starting transfers between devices: none -> 3.59 us  [per_device(): partner = lax.ppermute(state, 'near', [(0, 1), (1, 0)])]
  transfers between devices with their start and end apart: 2 -> 2, of which waited for: 1 -> 2; matrix products, arithmetic and copies ran while one was open for 1% -> 0% of each run, Pallas kernels for 0% -> 0%
where the time goes in v7:
time: 226 us; the launch traced here: 224 us
  blocking collectives  188 us (83%)
  waiting for transfers between devices  12.7 us (6%)
  starting transfers between devices  10.3 us (5%)
  Pallas kernels  9.54 us (4%)
    all_to_all x7, blocking collectives, exchange(): return lax.all_to_all(value, axis, split_axis=0, concat_axis=0, tiled=True)  188 us
    ppermute x1, waiting for transfers between devices, per_device(): partner = lax.ppermute(state, 'near', [(0, 1), (1, 0)])  10.9 us
    pallas_call x9, Pallas kernels, call(): pl.pallas_call(body, out_shape=outs, in_specs=[vmem] * len(operands), out...  9.54 us
    all_to_all x1, starting transfers between devices, exchange(): return lax.all_to_all(value, axis, split_axis=0, concat_axis=0, tiled=True)  6.75 us
  transfers between devices with their start and end apart: 2, of which 2 were waited for; matrix products, arithmetic and copies ran while one was open for 0% of the time, Pallas kernels for 0%

profile of v7, /device:TPU:6, one launch (start us, length us, event | category | flops | bytes accessed | tf_op | source)
XLA Modules:
  0.0 223.8 jit_solution(3497935437506143433)
XLA Ops:
  0.6 0.0 copy-start.4
  0.6 0.7 copy-done.4
  1.4 0.0 copy-start.8
  1.4 0.7 copy-done.8
  2.1 0.0 copy-start.9
  2.1 0.7 copy-done.9
  2.8 0.2 shard_map.113
  2.9 38.0 %all_to_all.40.gathered_ref = bf16[8,144,128]{2,1,0:T(8,128)(2,1)S(1)} all-to-all(bf16[8,144,128]{2,1,0:T(8,128)(2,1)S(1)} %shard_map.113), channel_id=1, replica_groups=mesh['far'=8,'near'=2,'expert'=32] {'far'}, dimensions={0} | all-to-all | bytes 589824 | tf_op jit(solution)/shard_map/all_to_all | solution.py:239
  40.9 0.0 copy-start.3
  40.9 1.2 shard_map.114
  42.0 0.0 copy-start.1
  42.0 0.0 copy-start.2
  42.1 0.0 copy-start.6
  42.1 27.1 %all_to_all.41 = bf16[64,80,128]{2,1,0:T(8,128)(2,1)S(1)} all-to-all(bf16[64,80,128]{2,1,0:T(8,128)(2,1)S(1)} %bitcast.20), channel_id=1, replica_groups=mesh['far'=8,'near'=2,'expert'=32] {'near','expert'}, dimensions={0} | all-to-all | bytes 2621440 | tf_op jit(solution)/shard_map/all_to_all | solution.py:239
  69.2 0.0 copy-done.3
  69.2 0.0 copy-done.1
  69.2 0.0 copy-done.2
  69.2 0.0 copy-done.6
  69.2 1.5 shard_map.115
  70.7 25.2 %all_to_all.42 = bf16[64,80,128]{2,1,0:T(8,128)(2,1)S(1)} all-to-all(bf16[64,80,128]{2,1,0:T(8,128)(2,1)S(1)} %bitcast.23), channel_id=1, replica_groups=mesh['far'=8,'near'=2,'expert'=32] {'near','expert'}, dimensions={0} | all-to-all | bytes 2621440 | tf_op jit(solution)/shard_map/all_to_all | solution.py:239
  95.9 0.0 copy-start
  95.9 0.0 copy-start.5
  95.9 1.7 shard_map.116
  97.6 0.0 copy-start.7
  97.7 0.0 copy-start.10
  97.7 24.3 %all_to_all.43.pieces_ref = bf16[8,128,128]{2,1,0:T(8,128)(2,1)S(1)} all-to-all(bf16[8,128,128]{2,1,0:T(8,128)(2,1)S(1)} %shard_map.116), channel_id=1, replica_groups=mesh['far'=8,'near'=2,'expert'=32] {'far'}, dimensions={0} | all-to-all | bytes 524288 | tf_op jit(solution)/shard_map/all_to_all | solution.py:239
  122.0 0.0 copy-done
  122.0 0.0 copy-done.5
  122.0 0.4 shard_map.117
  122.4 13.8 %all_to_all.44.pieces_ref = bf16[32,64,128]{2,1,0:T(8,128)(2,1)S(1)} all-to-all(bf16[32,64,128]{2,1,0:T(8,128)(2,1)S(1)} %bitcast.27), channel_id=1, replica_groups=mesh['far'=8,'near'=2,'expert'=32] {'expert'}, dimensions={0} | all-to-all | bytes 1048576 | tf_op jit(solution)/shard_map/all_to_all | solution.py:239
  136.2 0.0 copy-done.7
  136.2 0.0 copy-done.10
  136.2 1.2 shard_map.118
  137.4 6.8 %all-to-all-start.5 = ((bf16[64,64,128]{2,1,0:T(8,128)(2,1)}), bf16[64,64,128]{2,1,0:T(8,128)(2,1)S(1)}, u32[]{:S(2)}, u32[]{:S(2)}) async-start(bf16[64,64,128]{2,1,0:T(8,128)(2,1)} %shard_map.118), calls=%async_computation.5 | async-start | bytes 2097152 | tf_op jit(solution)/shard_map/all_to_all | solution.py:239
  144.1 3.6 %collective-permute-start = (bf16[128,128]{1,0:T(8,128)(2,1)S(1)}, bf16[128,128]{1,0:T(8,128)(2,1)S(1)}, u32[]{:S(2)}, u32[]{:S(2)}) collective-permute-start(bf16[128,128]{1,0:T(8,128)(2,1)S(1)} %get-tuple-element.11.state_ref), channel_id=1, source_target_pairs={{0,32},{32,0},{1,33},{33,1},{2,34},{34,2},{3,35},{35,3},{4,36},{36... | collective-permute-start | bytes 98312 | tf_op jit(solution)/shard_map/ppermute | solution.py:268
  147.7 10.9 %collective-permute-done.partner_ref = bf16[128,128]{1,0:T(8,128)(2,1)S(1)} collective-permute-done((bf16[128,128]{1,0:T(8,128)(2,1)S(1)}, bf16[128,128]{1,0:T(8,128)(2,1)S(1)}, u32[]{:S(2)}, u32[]{:S(2)}) %collective-permute-start) | collective-permute-done | bytes 32800 | tf_op jit(solution)/shard_map/ppermute | solution.py:268
  158.6 1.9 all-to-all-done.5
  160.5 0.6 shard_map.119
  161.1 35.8 %all_to_all.45.grad_ref.parts_ref = bf16[8,256,128]{2,1,0:T(8,128)(2,1)S(1)} all-to-all(bf16[8,256,128]{2,1,0:T(8,128)(2,1)S(1)} %shard_map.119), channel_id=1, replica_groups=mesh['far'=8,'near'=2,'expert'=32] {'far'}, dimensions={0} | all-to-all | bytes 1048576 | tf_op jit(solution)/shard_map/all_to_all | solution.py:239
  196.8 1.2 shard_map.120
  198.0 24.1 %all_to_all.46 = bf16[64,80,128]{2,1,0:T(8,128)(2,1)S(1)} all-to-all(bf16[64,80,128]{2,1,0:T(8,128)(2,1)S(1)} %bitcast.19), channel_id=1, replica_groups=mesh['far'=8,'near'=2,'expert'=32] {'near','expert'}, dimensions={0} | all-to-all | bytes 2621440 | tf_op jit(solution)/shard_map/all_to_all | solution.py:239
  222.1 1.7 shard_map.121
Async XLA Ops:
  0.6 0.8 copy-start.4
  1.4 0.7 copy-start.8
  2.1 0.7 copy-start.9
  40.9 28.3 %copy-start.3 = (bf16[1,128,4096]{2,1,0:T(8,128)(2,1)S(1)}, bf16[1,128,4096]{2,1,0:T(8,128)(2,1)}, u32[]{:S(2)}) copy-start(bf16[1,128,4096]{2,1,0:T(8,128)(2,1)} %param.16) | copy-start | bytes 3145732
  42.0 27.2 %copy-start.1 = (bf16[1,4096,128]{2,1,0:T(8,128)(2,1)S(1)}, bf16[1,4096,128]{2,1,0:T(8,128)(2,1)}, u32[]{:S(2)}) copy-start(bf16[1,4096,128]{2,1,0:T(8,128)(2,1)} %param.14) | copy-start | bytes 3145732
  42.0 27.1 %copy-start.2 = (bf16[1,4096,128]{2,1,0:T(8,128)(2,1)S(1)}, bf16[1,4096,128]{2,1,0:T(8,128)(2,1)}, u32[]{:S(2)}) copy-start(bf16[1,4096,128]{2,1,0:T(8,128)(2,1)} %param.15) | copy-start | bytes 3145732
  42.1 27.1 %copy-start.6 = (f32[4096]{0:T(1024)S(1)}, f32[4096]{0:T(1024)}, u32[]{:S(2)}) copy-start(f32[4096]{0:T(1024)} %param.11) | copy-start | bytes 49156
  95.9 26.1 %copy-start = (bf16[128,2048]{1,0:T(8,128)(2,1)S(1)}, bf16[128,2048]{1,0:T(8,128)(2,1)}, u32[]{:S(2)}) copy-start(bf16[128,2048]{1,0:T(8,128)(2,1)} %weight_ref.3) | copy-start | bytes 1572868
  95.9 26.1 %copy-start.5 = (bf16[128,128]{1,0:T(8,128)(2,1)S(1)}, bf16[128,128]{1,0:T(8,128)(2,1)}, u32[]{:S(2)}) copy-start(bf16[128,128]{1,0:T(8,128)(2,1)} %tok_ref.3) | copy-start | bytes 98308
  97.6 38.6 %copy-start.7 = (bf16[128,64]{0,1:T(8,128)(2,1)S(1)}, bf16[128,64]{0,1:T(8,128)(2,1)}, u32[]{:S(2)}) copy-start(bf16[128,64]{0,1:T(8,128)(2,1)} %param.18) | copy-start | bytes 49156
  97.7 38.6 %copy-start.10 = (s32[128]{0:T(128)S(1)}, s32[128]{0:T(128)}, u32[]{:S(2)}) copy-start(s32[128]{0:T(128)} %param.19) | copy-start | bytes 1540
  137.4 23.1 %all-to-all-start.5 = ((bf16[64,64,128]{2,1,0:T(8,128)(2,1)}), bf16[64,64,128]{2,1,0:T(8,128)(2,1)S(1)}, u32[]{:S(2)}, u32[]{:S(2)}) async-start(bf16[64,64,128]{2,1,0:T(8,128)(2,1)} %shard_map.118), calls=%async_computation.5 | async-start | bytes 2097152 | tf_op jit(solution)/shard_map/all_to_all | solution.py:239
  144.1 14.5 %collective-permute-start = (bf16[128,128]{1,0:T(8,128)(2,1)S(1)}, bf16[128,128]{1,0:T(8,128)(2,1)S(1)}, u32[]{:S(2)}, u32[]{:S(2)}) collective-permute-start(bf16[128,128]{1,0:T(8,128)(2,1)S(1)} %get-tuple-element.11.state_ref), channel_id=1, source_target_pairs={{0,32},{32,0},{1,33},{33,1},{2,34},{34,2},{3,35},{35,3},{4,36},{36... | collective-permute-start | bytes 98312 | tf_op jit(solution)/shard_map/ppermute | solution.py:268

commit v8 on v7

--- a/solution.py
+++ b/solution.py
@@ -9,7 +9,7 @@
 f32 = jnp.float32
 bf16 = jnp.bfloat16
 eps_norm = 1e-06
-meta_rows = 16
+meta_rows = 8
 group = 4
 
 
@@ -33,10 +33,9 @@
     return lax.dot_general(a, b, (((da,), (db,)), ((), ())), preferred_element_type=f32)
 
 
-def prepare(tok_ref, routes_ref, prob_ref, out_ref):
+def prepare(tok_ref, choices_ref, out_ref):
     rows, experts = tok_ref.shape[0], 32
-    routes = routes_ref[...].astype(f32)
-    first, second = routes[0:1, :], routes[1:2, :]
+    first, second = choices_ref[0:1, :], choices_ref[1:2, :]
     names = iota((experts, rows), 0).astype(f32)
     is_first, is_second = names == first, names == second
     named = jnp.where(is_first | is_second, 1.0, 0.0).astype(bf16)
@@ -57,7 +56,7 @@
                 jnp.where(
                     row == 3,
                     slot_second,
-                    jnp.where(row == 4, prob_ref[0:1, :], jnp.where(row == 5, prob_ref[1:2, :], 0.0)),
+                    jnp.where(row == 4, choices_ref[2:3, :], jnp.where(row == 5, choices_ref[3:4, :], 0.0)),
                 ),
             ),
         ),
@@ -238,9 +237,8 @@
     def exchange(value, axis):
         return lax.all_to_all(value, axis, split_axis=0, concat_axis=0, tiled=True)
 
-    packed = call(
-        prepare, shape(far, rows + meta_rows, width), tokens, routes.T, route_prob.T
-    )
+    choices = jnp.concatenate([routes.T.astype(f32), route_prob.T], axis=0)
+    packed = call(prepare, shape(far, rows + meta_rows, width), tokens, choices)
     gathered = exchange(packed, "far")
     slots = shape(near, experts, far * capacity, width)
     spots = (near * experts, far * capacity, width)
@@ -266,6 +264,7 @@
     )
     proj = exchange(proj.reshape(experts, keys // experts, rows), "expert")
     partner = lax.ppermute(state, "near", [(0, 1), (1, 0)])
+    proj, partner = lax.optimization_barrier((proj, partner))
     spread = call(
         form_cotangent,
         shape(near * experts, *proj.shape[1:]),

time: 226 us -> 225 us (level)
  blocking collectives: 188 us -> 197 us
  waiting for transfers between devices: 12.7 us -> 6.62 us
  starting transfers between devices: 10.3 us -> 7.42 us
    all_to_all x7, blocking collectives: 188 us -> 197 us  [exchange(): return lax.all_to_all(value, axis, split_axis=0, concat_axis=0, tiled=True)]
    ppermute x1, waiting for transfers between devices: 10.9 us -> 3.06 us  [per_device(): partner = lax.ppermute(state, 'near', [(0, 1), (1, 0)])]
where the time goes in v8:
time: 225 us; the launch traced here: 223 us
  blocking collectives  197 us (88%)
  Pallas kernels  9.36 us (4%)
  starting transfers between devices  7.42 us (3%)
  waiting for transfers between devices  6.62 us (3%)
    all_to_all x7, blocking collectives, exchange(): return lax.all_to_all(value, axis, split_axis=0, concat_axis=0, tiled=True)  197 us
    pallas_call x9, Pallas kernels, call(): pl.pallas_call(body, out_shape=outs, in_specs=[vmem] * len(operands), out...  9.36 us
    all_to_all x1, starting transfers between devices, exchange(): return lax.all_to_all(value, axis, split_axis=0, concat_axis=0, tiled=True)  4.68 us
  transfers between devices with their start and end apart: 2, of which 2 were waited for; matrix products, arithmetic and copies ran while one was open for 0% of the time, Pallas kernels for 0%

profile of v8, /device:TPU:6, one launch (start us, length us, event | category | flops | bytes accessed | tf_op | source)
XLA Modules:
  0.0 222.9 jit_solution(4364894287722619749)
XLA Ops:
  0.6 0.7 convert_bitcast_fusion
  1.3 0.7 pad_maximum_fusion.choices_ref
  2.0 0.0 copy-start.4
  2.0 0.8 copy-done.4
  2.8 0.2 shard_map.113
  2.9 37.3 %all_to_all.40.gathered_ref = bf16[8,136,128]{2,1,0:T(8,128)(2,1)S(1)} all-to-all(bf16[8,136,128]{2,1,0:T(8,128)(2,1)S(1)} %shard_map.113), channel_id=1, replica_groups=mesh['far'=8,'near'=2,'expert'=32] {'far'}, dimensions={0} | all-to-all | bytes 557056 | tf_op jit(solution)/shard_map/all_to_all | solution.py:238
  40.2 0.0 copy-start.3
  40.2 1.2 shard_map.114
  41.4 0.0 copy-start.1
  41.4 0.0 copy-start.2
  41.4 0.0 copy-start.6
  41.4 26.9 %all_to_all.41 = bf16[64,80,128]{2,1,0:T(8,128)(2,1)S(1)} all-to-all(bf16[64,80,128]{2,1,0:T(8,128)(2,1)S(1)} %bitcast.21), channel_id=1, replica_groups=mesh['far'=8,'near'=2,'expert'=32] {'near','expert'}, dimensions={0} | all-to-all | bytes 2621440 | tf_op jit(solution)/shard_map/all_to_all | solution.py:238
  68.3 0.0 copy-done.3
  68.3 0.0 copy-done.1
  68.3 0.0 copy-done.2
  68.3 0.0 copy-done.6
  68.3 1.5 shard_map.115
  69.8 25.2 %all_to_all.42 = bf16[64,80,128]{2,1,0:T(8,128)(2,1)S(1)} all-to-all(bf16[64,80,128]{2,1,0:T(8,128)(2,1)S(1)} %bitcast.24), channel_id=1, replica_groups=mesh['far'=8,'near'=2,'expert'=32] {'near','expert'}, dimensions={0} | all-to-all | bytes 2621440 | tf_op jit(solution)/shard_map/all_to_all | solution.py:238
  95.0 0.0 copy-start
  95.0 0.0 copy-start.5
  95.0 1.7 shard_map.116
  96.8 0.0 copy-start.7
  96.8 0.0 copy-start.8
  96.8 24.3 %all_to_all.43.pieces_ref = bf16[8,128,128]{2,1,0:T(8,128)(2,1)S(1)} all-to-all(bf16[8,128,128]{2,1,0:T(8,128)(2,1)S(1)} %shard_map.116), channel_id=1, replica_groups=mesh['far'=8,'near'=2,'expert'=32] {'far'}, dimensions={0} | all-to-all | bytes 524288 | tf_op jit(solution)/shard_map/all_to_all | solution.py:238
  121.1 0.0 copy-done
  121.1 0.0 copy-done.5
  121.1 1.2 shard_map.117
  122.3 4.7 %all-to-all-start.4 = ((bf16[32,64,128]{2,1,0:T(8,128)(2,1)}), bf16[32,64,128]{2,1,0:T(8,128)(2,1)S(1)}, u32[]{:S(2)}, u32[]{:S(2)}) async-start(bf16[32,64,128]{2,1,0:T(8,128)(2,1)} %bitcast.10), calls=%async_computation.4 | async-start | bytes 1048576 | tf_op jit(solution)/shard_map/all_to_all | solution.py:238
  127.0 2.7 %collective-permute-start = (bf16[128,128]{1,0:T(8,128)(2,1)S(1)}, bf16[128,128]{1,0:T(8,128)(2,1)S(1)}, u32[]{:S(2)}, u32[]{:S(2)}) collective-permute-start(bf16[128,128]{1,0:T(8,128)(2,1)S(1)} %get-tuple-element.13.state_ref), channel_id=1, source_target_pairs={{0,32},{32,0},{1,33},{33,1},{2,34},{34,2},{3,35},{35,3},{4,36},{36... | collective-permute-start | bytes 98312 | tf_op jit(solution)/shard_map/ppermute | solution.py:266
  129.7 3.1 %collective-permute-done.partner_ref = bf16[128,128]{1,0:T(8,128)(2,1)S(1)} collective-permute-done((bf16[128,128]{1,0:T(8,128)(2,1)S(1)}, bf16[128,128]{1,0:T(8,128)(2,1)S(1)}, u32[]{:S(2)}, u32[]{:S(2)}) %collective-permute-start) | collective-permute-done | bytes 32800 | tf_op jit(solution)/shard_map/ppermute | solution.py:266
  132.8 3.6 %all-to-all-done.4.pieces_ref = bf16[32,64,128]{2,1,0:T(8,128)(2,1)S(1)} async-done(((bf16[32,64,128]{2,1,0:T(8,128)(2,1)}), bf16[32,64,128]{2,1,0:T(8,128)(2,1)S(1)}, u32[]{:S(2)}, u32[]{:S(2)}) %all-to-all-start.4) | async-done | bytes 524320 | tf_op jit(solution)/shard_map/all_to_all | solution.py:238
  136.3 0.0 copy-done.7
  136.3 0.0 copy-done.8
  136.3 0.2 shard_map.118
  136.5 22.9 %all_to_all.44 = bf16[64,64,128]{2,1,0:T(8,128)(2,1)S(1)} all-to-all(bf16[64,64,128]{2,1,0:T(8,128)(2,1)S(1)} %shard_map.118), channel_id=1, replica_groups=mesh['far'=8,'near'=2,'expert'=32] {'near','expert'}, dimensions={0} | all-to-all | bytes 2097152 | tf_op jit(solution)/shard_map/all_to_all | solution.py:238
  159.4 0.6 shard_map.119
  160.0 35.7 %all_to_all.45.grad_ref.parts_ref = bf16[8,256,128]{2,1,0:T(8,128)(2,1)S(1)} all-to-all(bf16[8,256,128]{2,1,0:T(8,128)(2,1)S(1)} %shard_map.119), channel_id=1, replica_groups=mesh['far'=8,'near'=2,'expert'=32] {'far'}, dimensions={0} | all-to-all | bytes 1048576 | tf_op jit(solution)/shard_map/all_to_all | solution.py:238
  195.8 1.1 shard_map.120
  196.9 24.3 %all_to_all.46 = bf16[64,80,128]{2,1,0:T(8,128)(2,1)S(1)} all-to-all(bf16[64,80,128]{2,1,0:T(8,128)(2,1)S(1)} %bitcast.20), channel_id=1, replica_groups=mesh['far'=8,'near'=2,'expert'=32] {'near','expert'}, dimensions={0} | all-to-all | bytes 2621440 | tf_op jit(solution)/shard_map/all_to_all | solution.py:238
  221.2 1.7 shard_map.121
Async XLA Ops:
  2.0 0.8 copy-start.4
  40.2 28.1 %copy-start.3 = (bf16[1,128,4096]{2,1,0:T(8,128)(2,1)S(1)}, bf16[1,128,4096]{2,1,0:T(8,128)(2,1)}, u32[]{:S(2)}) copy-start(bf16[1,128,4096]{2,1,0:T(8,128)(2,1)} %param.16) | copy-start | bytes 3145732
  41.4 26.9 %copy-start.1 = (bf16[1,4096,128]{2,1,0:T(8,128)(2,1)S(1)}, bf16[1,4096,128]{2,1,0:T(8,128)(2,1)}, u32[]{:S(2)}) copy-start(bf16[1,4096,128]{2,1,0:T(8,128)(2,1)} %param.14) | copy-start | bytes 3145732
  41.4 26.9 %copy-start.2 = (bf16[1,4096,128]{2,1,0:T(8,128)(2,1)S(1)}, bf16[1,4096,128]{2,1,0:T(8,128)(2,1)}, u32[]{:S(2)}) copy-start(bf16[1,4096,128]{2,1,0:T(8,128)(2,1)} %param.15) | copy-start | bytes 3145732
  41.4 26.9 %copy-start.6 = (f32[4096]{0:T(1024)S(1)}, f32[4096]{0:T(1024)}, u32[]{:S(2)}) copy-start(f32[4096]{0:T(1024)} %param.11) | copy-start | bytes 49156
  95.0 26.1 %copy-start = (bf16[128,2048]{1,0:T(8,128)(2,1)S(1)}, bf16[128,2048]{1,0:T(8,128)(2,1)}, u32[]{:S(2)}) copy-start(bf16[128,2048]{1,0:T(8,128)(2,1)} %weight_ref.3) | copy-start | bytes 1572868
  95.0 26.1 %copy-start.5 = (bf16[128,128]{1,0:T(8,128)(2,1)S(1)}, bf16[128,128]{1,0:T(8,128)(2,1)}, u32[]{:S(2)}) copy-start(bf16[128,128]{1,0:T(8,128)(2,1)} %tok_ref.3) | copy-start | bytes 98308
  96.8 39.6 %copy-start.7 = (bf16[128,64]{0,1:T(8,128)(2,1)S(1)}, bf16[128,64]{0,1:T(8,128)(2,1)}, u32[]{:S(2)}) copy-start(bf16[128,64]{0,1:T(8,128)(2,1)} %param.18) | copy-start | bytes 49156
  96.8 39.6 %copy-start.8 = (s32[128]{0:T(128)S(1)}, s32[128]{0:T(128)}, u32[]{:S(2)}) copy-start(s32[128]{0:T(128)} %param.19) | copy-start | bytes 1540
  122.3 14.1 %all-to-all-start.4 = ((bf16[32,64,128]{2,1,0:T(8,128)(2,1)}), bf16[32,64,128]{2,1,0:T(8,128)(2,1)S(1)}, u32[]{:S(2)}, u32[]{:S(2)}) async-start(bf16[32,64,128]{2,1,0:T(8,128)(2,1)} %bitcast.10), calls=%async_computation.4 | async-start | bytes 1048576 | tf_op jit(solution)/shard_map/all_to_all | solution.py:238
  127.0 5.8 %collective-permute-start = (bf16[128,128]{1,0:T(8,128)(2,1)S(1)}, bf16[128,128]{1,0:T(8,128)(2,1)S(1)}, u32[]{:S(2)}, u32[]{:S(2)}) collective-permute-start(bf16[128,128]{1,0:T(8,128)(2,1)S(1)} %get-tuple-element.13.state_ref), channel_id=1, source_target_pairs={{0,32},{32,0},{1,33},{33,1},{2,34},{34,2},{3,35},{35,3},{4,36},{36... | collective-permute-start | bytes 98312 | tf_op jit(solution)/shard_map/ppermute | solution.py:266

commit v9 on v8

--- a/solution.py
+++ b/solution.py
@@ -184,25 +184,25 @@
         out_ref[p] = scaled
 
 
-def gradients(cot_ref, state_ref, partner_ref, weight_ref, out_ref):
-    width = weight_ref.shape[0]
-    me = lax.axis_index("near")
+def gradients(cot_ref, state_ref, partner_ref, weight_ref, out_ref, *part_refs):
+    me, place = lax.axis_index("near"), lax.axis_index("far")
     state_grad = jnp.dot(
         weight_ref[...], cot_ref[me], preferred_element_type=f32
     ).astype(bf16)
-    columns = cot_ref.shape[1] // (2 * out_ref.shape[0])
-    for q in range(out_ref.shape[0]):
-        out_ref[q, 0:width, :] = state_grad
-        at = pl.ds(pl.multiple_of((2 * q + me) * columns, columns), columns)
+    peers = out_ref.shape[0]
+    columns = cot_ref.shape[1] // (2 * peers)
+    for d in range(peers):
+        out_ref[d] = state_grad
+        plane = 2 * ((place + d) % peers) + me
+        at = pl.ds(pl.multiple_of(plane * columns, columns), columns)
         part = contract(state_ref[...], cot_ref[me, at, :], 1, 1)
         part = part + contract(partner_ref[...], cot_ref[1 - me, at, :], 1, 1)
-        out_ref[q, width:, :] = part.astype(bf16)
-
-
-def down_gradient(hidden_ref, rows_ref, parts_ref, out_ref, key_value_ref):
-    key_value_ref[...] = sum(
-        parts_ref[q, key_value_ref.shape[0] :, :].astype(f32) for q in range(parts_ref.shape[0])
-    )
+        part_refs[d][...] = part.astype(bf16)
+
+
+def down_gradient(hidden_ref, rows_ref, *refs):
+    part_refs, (out_ref, key_value_ref) = refs[:-2], refs[-2:]
+    key_value_ref[...] = sum(part[...].astype(f32) for part in part_refs)
     hidden = hidden_ref[...].astype(f32).T.astype(bf16)
     pairs, parts, half, width = rows_ref.shape
     for p in range(parts):
@@ -273,22 +273,24 @@
         concept_mask[None, :],
     )
     cotangents = exchange(spread, ("near", "expert")).reshape(near, keys, rows)
-    sent = call(
+    sent, *parts = call(
         gradients,
-        shape(far, 2 * width, rows),
+        [shape(far, width, rows)] + [shape(width, keys // blocks)] * far,
         cotangents,
         state,
         partner,
         key_value_weight,
     )
     all_grads = exchange(sent, "far")
+    for d in range(1, far):
+        parts[d] = lax.ppermute(parts[d], "far", [(i, (i + d) % far) for i in range(far)])
     landed = route(call(dispatch_grad, slots, gathered, all_grads))
     down_grad, key_value_grad = call(
         down_gradient,
         [shape(*down_weight.shape[1:]), shape(width, keys // blocks, dtype=f32)],
         hidden,
         landed,
-        all_grads,
+        *parts,
     )
     return (down_grad[None], key_value_grad)
 

time: 225 us -> 234 us (1.040)
  starting transfers between devices: 7.42 us -> 46.5 us
  blocking collectives: 197 us -> 161 us
  waiting for transfers between devices: 6.62 us -> 11 us
    all_to_all x7 -> x6, blocking collectives: 197 us -> 161 us  [exchange(): return lax.all_to_all(value, axis, split_axis=0, concat_axis=0, tiled=True)]
    ppermute x0 -> x7, starting transfers between devices: none -> 33.6 us  [per_device(): lax.ppermute(parts[d], 'far', [(i, (i + d) % far) for i in range(far)])]
    all_to_all x1 -> x2, starting transfers between devices: 4.68 us -> 10.2 us  [exchange(): return lax.all_to_all(value, axis, split_axis=0, concat_axis=0, tiled=True)]
    ppermute x0 -> x7, waiting for transfers between devices: none -> 4.4 us  [per_device(): lax.ppermute(parts[d], 'far', [(i, (i + d) % far) for i in range(far)])]
  transfers between devices with their start and end apart: 2 -> 10, of which waited for: 2 -> 5; matrix products, arithmetic and copies ran while one was open for 0% -> 0% of each run, Pallas kernels for 0% -> 0%
where the time goes in v9:
time: 234 us; the launch traced here: 232 us
  blocking collectives  161 us (69%)
  starting transfers between devices  46.5 us (20%)
  waiting for transfers between devices  11 us (5%)
  Pallas kernels  10.4 us (4%)
    all_to_all x6, blocking collectives, exchange(): return lax.all_to_all(value, axis, split_axis=0, concat_axis=0, tiled=True)  161 us
    ppermute x7, starting transfers between devices, per_device(): lax.ppermute(parts[d], 'far', [(i, (i + d) % far) for i in range(far)])  33.6 us
    pallas_call x9, Pallas kernels, call(): pl.pallas_call(body, out_shape=outs, in_specs=[vmem] * len(operands), out...  10.4 us
    all_to_all x2, starting transfers between devices, exchange(): return lax.all_to_all(value, axis, split_axis=0, concat_axis=0, tiled=True)  10.2 us
  transfers between devices with their start and end apart: 10, of which 5 were waited for; matrix products, arithmetic and copies ran while one was open for 0% of the time, Pallas kernels for 0%

profile of v9, /device:TPU:6, one launch (start us, length us, event | category | flops | bytes accessed | tf_op | source)
XLA Modules:
  0.0 232.1 jit_solution(16697314250679384413)
XLA Ops:
  0.6 0.7 convert_bitcast_fusion
  1.3 0.7 pad_maximum_fusion.choices_ref
  2.0 0.0 copy-start.4
  2.0 0.8 copy-done.4
  2.8 0.2 shard_map.113
  2.9 37.3 %all_to_all.40.gathered_ref = bf16[8,136,128]{2,1,0:T(8,128)(2,1)S(1)} all-to-all(bf16[8,136,128]{2,1,0:T(8,128)(2,1)S(1)} %shard_map.113), channel_id=1, replica_groups=mesh['far'=8,'near'=2,'expert'=32] {'far'}, dimensions={0} | all-to-all | bytes 557056 | tf_op jit(solution)/shard_map/all_to_all | solution.py:238
  40.2 0.0 copy-start.3
  40.2 1.2 shard_map.114
  41.4 0.0 copy-start.1
  41.4 0.0 copy-start.2
  41.4 0.0 copy-start.6
  41.4 26.9 %all_to_all.41 = bf16[64,80,128]{2,1,0:T(8,128)(2,1)S(1)} all-to-all(bf16[64,80,128]{2,1,0:T(8,128)(2,1)S(1)} %bitcast.20), channel_id=1, replica_groups=mesh['far'=8,'near'=2,'expert'=32] {'near','expert'}, dimensions={0} | all-to-all | bytes 2621440 | tf_op jit(solution)/shard_map/all_to_all | solution.py:238
  68.3 0.0 copy-done.3
  68.3 0.0 copy-done.1
  68.3 0.0 copy-done.2
  68.3 0.0 copy-done.6
  68.3 1.5 shard_map.115
  69.8 25.2 %all_to_all.42 = bf16[64,80,128]{2,1,0:T(8,128)(2,1)S(1)} all-to-all(bf16[64,80,128]{2,1,0:T(8,128)(2,1)S(1)} %bitcast.23), channel_id=1, replica_groups=mesh['far'=8,'near'=2,'expert'=32] {'near','expert'}, dimensions={0} | all-to-all | bytes 2621440 | tf_op jit(solution)/shard_map/all_to_all | solution.py:238
  95.0 0.0 copy-start
  95.0 0.0 copy-start.5
  95.0 1.7 shard_map.116
  96.8 0.0 copy-start.7
  96.8 0.0 copy-start.8
  96.8 24.3 %all_to_all.43.pieces_ref = bf16[8,128,128]{2,1,0:T(8,128)(2,1)S(1)} all-to-all(bf16[8,128,128]{2,1,0:T(8,128)(2,1)S(1)} %shard_map.116), channel_id=1, replica_groups=mesh['far'=8,'near'=2,'expert'=32] {'far'}, dimensions={0} | all-to-all | bytes 524288 | tf_op jit(solution)/shard_map/all_to_all | solution.py:238
  121.1 0.0 copy-done
  121.1 0.0 copy-done.5
  121.1 1.2 shard_map.117
  122.3 4.7 %all-to-all-start.4 = ((bf16[32,64,128]{2,1,0:T(8,128)(2,1)}), bf16[32,64,128]{2,1,0:T(8,128)(2,1)S(1)}, u32[]{:S(2)}, u32[]{:S(2)}) async-start(bf16[32,64,128]{2,1,0:T(8,128)(2,1)} %bitcast.10), calls=%async_computation.4 | async-start | bytes 1048576 | tf_op jit(solution)/shard_map/all_to_all | solution.py:238
  127.0 2.7 %collective-permute-start = (bf16[128,128]{1,0:T(8,128)(2,1)S(1)}, bf16[128,128]{1,0:T(8,128)(2,1)S(1)}, u32[]{:S(2)}, u32[]{:S(2)}) collective-permute-start(bf16[128,128]{1,0:T(8,128)(2,1)S(1)} %get-tuple-element.22.state_ref), channel_id=1, source_target_pairs={{0,32},{32,0},{1,33},{33,1},{2,34},{34,2},{3,35},{35,3},{4,36},{36... | collective-permute-start | bytes 98312 | tf_op jit(solution)/shard_map/ppermute | solution.py:266
  129.7 3.1 %collective-permute-done.partner_ref = bf16[128,128]{1,0:T(8,128)(2,1)S(1)} collective-permute-done((bf16[128,128]{1,0:T(8,128)(2,1)S(1)}, bf16[128,128]{1,0:T(8,128)(2,1)S(1)}, u32[]{:S(2)}, u32[]{:S(2)}) %collective-permute-start) | collective-permute-done | bytes 32800 | tf_op jit(solution)/shard_map/ppermute | solution.py:266
  132.8 3.6 %all-to-all-done.4.pieces_ref = bf16[32,64,128]{2,1,0:T(8,128)(2,1)S(1)} async-done(((bf16[32,64,128]{2,1,0:T(8,128)(2,1)}), bf16[32,64,128]{2,1,0:T(8,128)(2,1)S(1)}, u32[]{:S(2)}, u32[]{:S(2)}) %all-to-all-start.4) | async-done | bytes 524320 | tf_op jit(solution)/shard_map/all_to_all | solution.py:238
  136.3 0.0 copy-done.7
  136.3 0.0 copy-done.8
  136.3 0.2 shard_map.118
  136.5 22.9 %all_to_all.44 = bf16[64,64,128]{2,1,0:T(8,128)(2,1)S(1)} all-to-all(bf16[64,64,128]{2,1,0:T(8,128)(2,1)S(1)} %shard_map.118), channel_id=1, replica_groups=mesh['far'=8,'near'=2,'expert'=32] {'near','expert'}, dimensions={0} | all-to-all | bytes 2097152 | tf_op jit(solution)/shard_map/all_to_all | solution.py:238
  159.4 0.6 shard_map.119
  160.0 24.5 %all_to_all.45.grad_ref = bf16[8,128,128]{2,1,0:T(8,128)(2,1)S(1)} all-to-all(bf16[8,128,128]{2,1,0:T(8,128)(2,1)S(1)} %get-tuple-element.25), channel_id=1, replica_groups=mesh['far'=8,'near'=2,'expert'=32] {'far'}, dimensions={0} | all-to-all | bytes 524288 | tf_op jit(solution)/shard_map/all_to_all | solution.py:238
  184.5 2.2 shard_map.120
  186.8 5.5 %all-to-all-start.7 = ((bf16[64,80,128]{2,1,0:T(8,128)(2,1)}), bf16[64,80,128]{2,1,0:T(8,128)(2,1)S(1)}, u32[]{:S(2)}, u32[]{:S(2)}) async-start(bf16[64,80,128]{2,1,0:T(8,128)(2,1)} %bitcast.14), calls=%async_computation.7 | async-start | bytes 2621440 | tf_op jit(solution)/shard_map/all_to_all | solution.py:238
  192.2 3.4 %collective-permute-start.1 = (bf16[128,128]{1,0:T(8,128)(2,1)S(1)}, bf16[128,128]{1,0:T(8,128)(2,1)S(1)}, u32[]{:S(2)}, u32[]{:S(2)}) collective-permute-start(bf16[128,128]{1,0:T(8,128)(2,1)S(1)} %get-tuple-element.27), channel_id=1, source_target_pairs={{0,64},{64,128},{128,192},{192,256},{256,320},{320,384},{384,448},... | collective-permute-start | bytes 98312 | tf_op jit(solution)/shard_map/ppermute | solution.py:286
  195.7 2.3 %collective-permute-start.2 = (bf16[128,128]{1,0:T(8,128)(2,1)S(1)}, bf16[128,128]{1,0:T(8,128)(2,1)S(1)}, u32[]{:S(2)}, u32[]{:S(2)}) collective-permute-start(bf16[128,128]{1,0:T(8,128)(2,1)S(1)} %get-tuple-element.28), channel_id=1, source_target_pairs={{0,128},{64,192},{128,256},{192,320},{256,384},{320,448},{384,0},{... | collective-permute-start | bytes 98312 | tf_op jit(solution)/shard_map/ppermute | solution.py:286
  198.0 7.5 %collective-permute-start.3 = (bf16[128,128]{1,0:T(8,128)(2,1)S(1)}, bf16[128,128]{1,0:T(8,128)(2,1)S(1)}, u32[]{:S(2)}, u32[]{:S(2)}) collective-permute-start(bf16[128,128]{1,0:T(8,128)(2,1)S(1)} %get-tuple-element.29), channel_id=1, source_target_pairs={{0,192},{64,256},{128,320},{192,384},{256,448},{320,0},{384,64},{4... | collective-permute-start | bytes 98312 | tf_op jit(solution)/shard_map/ppermute | solution.py:286
  205.5 7.4 %collective-permute-start.4 = (bf16[128,128]{1,0:T(8,128)(2,1)S(1)}, bf16[128,128]{1,0:T(8,128)(2,1)S(1)}, u32[]{:S(2)}, u32[]{:S(2)}) collective-permute-start(bf16[128,128]{1,0:T(8,128)(2,1)S(1)} %get-tuple-element.30), channel_id=1, source_target_pairs={{0,256},{64,320},{128,384},{192,448},{256,0},{320,64},{384,128},{4... | collective-permute-start | bytes 98312 | tf_op jit(solution)/shard_map/ppermute | solution.py:286
  212.9 7.2 %collective-permute-start.5 = (bf16[128,128]{1,0:T(8,128)(2,1)S(1)}, bf16[128,128]{1,0:T(8,128)(2,1)S(1)}, u32[]{:S(2)}, u32[]{:S(2)}) collective-permute-start(bf16[128,128]{1,0:T(8,128)(2,1)S(1)} %get-tuple-element.31), channel_id=1, source_target_pairs={{0,320},{64,384},{128,448},{192,0},{256,64},{320,128},{384,192},{4... | collective-permute-start | bytes 98312 | tf_op jit(solution)/shard_map/ppermute | solution.py:286
  220.1 0.0 collective-permute-done.1.refs_1_
  220.2 3.3 %collective-permute-start.6 = (bf16[128,128]{1,0:T(8,128)(2,1)S(1)}, bf16[128,128]{1,0:T(8,128)(2,1)S(1)}, u32[]{:S(2)}, u32[]{:S(2)}) collective-permute-start(bf16[128,128]{1,0:T(8,128)(2,1)S(1)} %get-tuple-element.32), channel_id=1, source_target_pairs={{0,384},{64,448},{128,0},{192,64},{256,128},{320,192},{384,256},{4... | collective-permute-start | bytes 98312 | tf_op jit(solution)/shard_map/ppermute | solution.py:286
  223.5 0.0 collective-permute-done.2.refs_2_
  223.5 2.5 %collective-permute-start.7 = (bf16[128,128]{1,0:T(8,128)(2,1)S(1)}, bf16[128,128]{1,0:T(8,128)(2,1)S(1)}, u32[]{:S(2)}, u32[]{:S(2)}) collective-permute-start(bf16[128,128]{1,0:T(8,128)(2,1)S(1)} %get-tuple-element.33), channel_id=1, source_target_pairs={{0,448},{64,0},{128,64},{192,128},{256,192},{320,256},{384,320},{4... | collective-permute-start | bytes 98312 | tf_op jit(solution)/shard_map/ppermute | solution.py:286
  226.0 0.0 collective-permute-done.3.refs_3_
  226.0 0.0 collective-permute-done.4.refs_4_
  226.0 0.7 collective-permute-done.5.refs_5_
  226.7 3.5 %collective-permute-done.6.refs_6_ = bf16[128,128]{1,0:T(8,128)(2,1)S(1)} collective-permute-done((bf16[128,128]{1,0:T(8,128)(2,1)S(1)}, bf16[128,128]{1,0:T(8,128)(2,1)S(1)}, u32[]{:S(2)}, u32[]{:S(2)}) %collective-permute-start.6) | collective-permute-done | bytes 32800 | tf_op jit(solution)/shard_map/ppermute | solution.py:286
  230.2 0.2 collective-permute-done.7.refs_7_
  230.4 0.0 all-to-all-done.7
  230.4 1.7 shard_map.121
Async XLA Ops:
  2.0 0.8 copy-start.4
  40.2 28.1 %copy-start.3 = (bf16[1,128,4096]{2,1,0:T(8,128)(2,1)S(1)}, bf16[1,128,4096]{2,1,0:T(8,128)(2,1)}, u32[]{:S(2)}) copy-start(bf16[1,128,4096]{2,1,0:T(8,128)(2,1)} %param.16) | copy-start | bytes 3145732
  41.4 26.9 %copy-start.1 = (bf16[1,4096,128]{2,1,0:T(8,128)(2,1)S(1)}, bf16[1,4096,128]{2,1,0:T(8,128)(2,1)}, u32[]{:S(2)}) copy-start(bf16[1,4096,128]{2,1,0:T(8,128)(2,1)} %param.14) | copy-start | bytes 3145732
  41.4 26.9 %copy-start.2 = (bf16[1,4096,128]{2,1,0:T(8,128)(2,1)S(1)}, bf16[1,4096,128]{2,1,0:T(8,128)(2,1)}, u32[]{:S(2)}) copy-start(bf16[1,4096,128]{2,1,0:T(8,128)(2,1)} %param.15) | copy-start | bytes 3145732
  41.4 26.9 %copy-start.6 = (f32[4096]{0:T(1024)S(1)}, f32[4096]{0:T(1024)}, u32[]{:S(2)}) copy-start(f32[4096]{0:T(1024)} %param.11) | copy-start | bytes 49156
  95.0 26.1 %copy-start = (bf16[128,2048]{1,0:T(8,128)(2,1)S(1)}, bf16[128,2048]{1,0:T(8,128)(2,1)}, u32[]{:S(2)}) copy-start(bf16[128,2048]{1,0:T(8,128)(2,1)} %weight_ref.3) | copy-start | bytes 1572868
  95.0 26.1 %copy-start.5 = (bf16[128,128]{1,0:T(8,128)(2,1)S(1)}, bf16[128,128]{1,0:T(8,128)(2,1)}, u32[]{:S(2)}) copy-start(bf16[128,128]{1,0:T(8,128)(2,1)} %tok_ref.3) | copy-start | bytes 98308
  96.8 39.6 %copy-start.7 = (bf16[128,64]{0,1:T(8,128)(2,1)S(1)}, bf16[128,64]{0,1:T(8,128)(2,1)}, u32[]{:S(2)}) copy-start(bf16[128,64]{0,1:T(8,128)(2,1)} %param.18) | copy-start | bytes 49156
  96.8 39.6 %copy-start.8 = (s32[128]{0:T(128)S(1)}, s32[128]{0:T(128)}, u32[]{:S(2)}) copy-start(s32[128]{0:T(128)} %param.19) | copy-start | bytes 1540
  122.3 14.1 %all-to-all-start.4 = ((bf16[32,64,128]{2,1,0:T(8,128)(2,1)}), bf16[32,64,128]{2,1,0:T(8,128)(2,1)S(1)}, u32[]{:S(2)}, u32[]{:S(2)}) async-start(bf16[32,64,128]{2,1,0:T(8,128)(2,1)} %bitcast.10), calls=%async_computation.4 | async-start | bytes 1048576 | tf_op jit(solution)/shard_map/all_to_all | solution.py:238
  127.0 5.8 %collective-permute-start = (bf16[128,128]{1,0:T(8,128)(2,1)S(1)}, bf16[128,128]{1,0:T(8,128)(2,1)S(1)}, u32[]{:S(2)}, u32[]{:S(2)}) collective-permute-start(bf16[128,128]{1,0:T(8,128)(2,1)S(1)} %get-tuple-element.22.state_ref), channel_id=1, source_target_pairs={{0,32},{32,0},{1,33},{33,1},{2,34},{34,2},{3,35},{35,3},{4,36},{36... | collective-permute-start | bytes 98312 | tf_op jit(solution)/shard_map/ppermute | solution.py:266
  186.8 43.6 %all-to-all-start.7 = ((bf16[64,80,128]{2,1,0:T(8,128)(2,1)}), bf16[64,80,128]{2,1,0:T(8,128)(2,1)S(1)}, u32[]{:S(2)}, u32[]{:S(2)}) async-start(bf16[64,80,128]{2,1,0:T(8,128)(2,1)} %bitcast.14), calls=%async_computation.7 | async-start | bytes 2621440 | tf_op jit(solution)/shard_map/all_to_all | solution.py:238
  192.2 27.9 %collective-permute-start.1 = (bf16[128,128]{1,0:T(8,128)(2,1)S(1)}, bf16[128,128]{1,0:T(8,128)(2,1)S(1)}, u32[]{:S(2)}, u32[]{:S(2)}) collective-permute-start(bf16[128,128]{1,0:T(8,128)(2,1)S(1)} %get-tuple-element.27), channel_id=1, source_target_pairs={{0,64},{64,128},{128,192},{192,256},{256,320},{320,384},{384,448},... | collective-permute-start | bytes 98312 | tf_op jit(solution)/shard_map/ppermute | solution.py:286
  195.7 27.8 %collective-permute-start.2 = (bf16[128,128]{1,0:T(8,128)(2,1)S(1)}, bf16[128,128]{1,0:T(8,128)(2,1)S(1)}, u32[]{:S(2)}, u32[]{:S(2)}) collective-permute-start(bf16[128,128]{1,0:T(8,128)(2,1)S(1)} %get-tuple-element.28), channel_id=1, source_target_pairs={{0,128},{64,192},{128,256},{192,320},{256,384},{320,448},{384,0},{... | collective-permute-start | bytes 98312 | tf_op jit(solution)/shard_map/ppermute | solution.py:286
  198.0 28.0 %collective-permute-start.3 = (bf16[128,128]{1,0:T(8,128)(2,1)S(1)}, bf16[128,128]{1,0:T(8,128)(2,1)S(1)}, u32[]{:S(2)}, u32[]{:S(2)}) collective-permute-start(bf16[128,128]{1,0:T(8,128)(2,1)S(1)} %get-tuple-element.29), channel_id=1, source_target_pairs={{0,192},{64,256},{128,320},{192,384},{256,448},{320,0},{384,64},{4... | collective-permute-start | bytes 98312 | tf_op jit(solution)/shard_map/ppermute | solution.py:286
  205.5 20.4 %collective-permute-start.4 = (bf16[128,128]{1,0:T(8,128)(2,1)S(1)}, bf16[128,128]{1,0:T(8,128)(2,1)S(1)}, u32[]{:S(2)}, u32[]{:S(2)}) collective-permute-start(bf16[128,128]{1,0:T(8,128)(2,1)S(1)} %get-tuple-element.30), channel_id=1, source_target_pairs={{0,256},{64,320},{128,384},{192,448},{256,0},{320,64},{384,128},{4... | collective-permute-start | bytes 98312 | tf_op jit(solution)/shard_map/ppermute | solution.py:286
  212.9 13.8 %collective-permute-start.5 = (bf16[128,128]{1,0:T(8,128)(2,1)S(1)}, bf16[128,128]{1,0:T(8,128)(2,1)S(1)}, u32[]{:S(2)}, u32[]{:S(2)}) collective-permute-start(bf16[128,128]{1,0:T(8,128)(2,1)S(1)} %get-tuple-element.31), channel_id=1, source_target_pairs={{0,320},{64,384},{128,448},{192,0},{256,64},{320,128},{384,192},{4... | collective-permute-start | bytes 98312 | tf_op jit(solution)/shard_map/ppermute | solution.py:286
  220.2 10.0 %collective-permute-start.6 = (bf16[128,128]{1,0:T(8,128)(2,1)S(1)}, bf16[128,128]{1,0:T(8,128)(2,1)S(1)}, u32[]{:S(2)}, u32[]{:S(2)}) collective-permute-start(bf16[128,128]{1,0:T(8,128)(2,1)S(1)} %get-tuple-element.32), channel_id=1, source_target_pairs={{0,384},{64,448},{128,0},{192,64},{256,128},{320,192},{384,256},{4... | collective-permute-start | bytes 98312 | tf_op jit(solution)/shard_map/ppermute | solution.py:286
  223.5 6.9 %collective-permute-start.7 = (bf16[128,128]{1,0:T(8,128)(2,1)S(1)}, bf16[128,128]{1,0:T(8,128)(2,1)S(1)}, u32[]{:S(2)}, u32[]{:S(2)}) collective-permute-start(bf16[128,128]{1,0:T(8,128)(2,1)S(1)} %get-tuple-element.33), channel_id=1, source_target_pairs={{0,448},{64,0},{128,64},{192,128},{256,192},{320,256},{384,320},{4... | collective-permute-start | bytes 98312 | tf_op jit(solution)/shard_map/ppermute | solution.py:286

commit v10 on v7

--- a/solution.py
+++ b/solution.py
@@ -9,7 +9,7 @@
 f32 = jnp.float32
 bf16 = jnp.bfloat16
 eps_norm = 1e-06
-meta_rows = 16
+meta_rows = 8
 group = 4
 
 
@@ -238,9 +238,7 @@
     def exchange(value, axis):
         return lax.all_to_all(value, axis, split_axis=0, concat_axis=0, tiled=True)
 
-    packed = call(
-        prepare, shape(far, rows + meta_rows, width), tokens, routes.T, route_prob.T
-    )
+    packed = call(prepare, shape(far, rows + meta_rows, width), tokens, routes.T, route_prob.T)
     gathered = exchange(packed, "far")
     slots = shape(near, experts, far * capacity, width)
     spots = (near * experts, far * capacity, width)

time: 226 us -> 225 us (level)
  no operation moved by 1% of the time
where the time goes in v10:
time: 225 us; the launch traced here: 223 us
  blocking collectives  187 us (83%)
  waiting for transfers between devices  12.7 us (6%)
  starting transfers between devices  10.3 us (5%)
  Pallas kernels  9.56 us (4%)
    all_to_all x7, blocking collectives, exchange(): return lax.all_to_all(value, axis, split_axis=0, concat_axis=0, tiled=True)  187 us
    ppermute x1, waiting for transfers between devices, per_device(): partner = lax.ppermute(state, 'near', [(0, 1), (1, 0)])  10.9 us
    pallas_call x9, Pallas kernels, call(): pl.pallas_call(body, out_shape=outs, in_specs=[vmem] * len(operands), out...  9.56 us
    all_to_all x1, starting transfers between devices, exchange(): return lax.all_to_all(value, axis, split_axis=0, concat_axis=0, tiled=True)  6.75 us
  transfers between devices with their start and end apart: 2, of which 2 were waited for; matrix products, arithmetic and copies ran while one was open for 0% of the time, Pallas kernels for 0%

profile of v10, /device:TPU:6, one launch (start us, length us, event | category | flops | bytes accessed | tf_op | source)
XLA Modules:
  0.0 222.9 jit_solution(10867959896289882938)
XLA Ops:
  0.6 0.0 copy-start.4
  0.6 0.7 copy-done.4
  1.4 0.0 copy-start.8
  1.4 0.7 copy-done.8
  2.1 0.0 copy-start.9
  2.1 0.7 copy-done.9
  2.8 0.2 shard_map.113
  2.9 37.3 %all_to_all.40.gathered_ref = bf16[8,136,128]{2,1,0:T(8,128)(2,1)S(1)} all-to-all(bf16[8,136,128]{2,1,0:T(8,128)(2,1)S(1)} %shard_map.113), channel_id=1, replica_groups=mesh['far'=8,'near'=2,'expert'=32] {'far'}, dimensions={0} | all-to-all | bytes 557056 | tf_op jit(solution)/shard_map/all_to_all | solution.py:239
  40.2 0.0 copy-start.3
  40.2 1.2 shard_map.114
  41.4 0.0 copy-start.1
  41.4 0.0 copy-start.2
  41.4 0.0 copy-start.6
  41.4 26.9 %all_to_all.41 = bf16[64,80,128]{2,1,0:T(8,128)(2,1)S(1)} all-to-all(bf16[64,80,128]{2,1,0:T(8,128)(2,1)S(1)} %bitcast.20), channel_id=1, replica_groups=mesh['far'=8,'near'=2,'expert'=32] {'near','expert'}, dimensions={0} | all-to-all | bytes 2621440 | tf_op jit(solution)/shard_map/all_to_all | solution.py:239
  68.3 0.0 copy-done.3
  68.3 0.0 copy-done.1
  68.3 0.0 copy-done.2
  68.3 0.0 copy-done.6
  68.3 1.5 shard_map.115
  69.8 25.2 %all_to_all.42 = bf16[64,80,128]{2,1,0:T(8,128)(2,1)S(1)} all-to-all(bf16[64,80,128]{2,1,0:T(8,128)(2,1)S(1)} %bitcast.23), channel_id=1, replica_groups=mesh['far'=8,'near'=2,'expert'=32] {'near','expert'}, dimensions={0} | all-to-all | bytes 2621440 | tf_op jit(solution)/shard_map/all_to_all | solution.py:239
  95.0 0.0 copy-start
  95.0 0.0 copy-start.5
  95.0 1.7 shard_map.116
  96.8 0.0 copy-start.7
  96.8 0.0 copy-start.10
  96.8 24.3 %all_to_all.43.pieces_ref = bf16[8,128,128]{2,1,0:T(8,128)(2,1)S(1)} all-to-all(bf16[8,128,128]{2,1,0:T(8,128)(2,1)S(1)} %shard_map.116), channel_id=1, replica_groups=mesh['far'=8,'near'=2,'expert'=32] {'far'}, dimensions={0} | all-to-all | bytes 524288 | tf_op jit(solution)/shard_map/all_to_all | solution.py:239
  121.1 0.0 copy-done
  121.1 0.0 copy-done.5
  121.1 0.4 shard_map.117
  121.5 13.9 %all_to_all.44.pieces_ref = bf16[32,64,128]{2,1,0:T(8,128)(2,1)S(1)} all-to-all(bf16[32,64,128]{2,1,0:T(8,128)(2,1)S(1)} %bitcast.27), channel_id=1, replica_groups=mesh['far'=8,'near'=2,'expert'=32] {'expert'}, dimensions={0} | all-to-all | bytes 1048576 | tf_op jit(solution)/shard_map/all_to_all | solution.py:239
  135.3 0.0 copy-done.7
  135.3 0.0 copy-done.10
  135.3 1.2 shard_map.118
  136.5 6.8 %all-to-all-start.5 = ((bf16[64,64,128]{2,1,0:T(8,128)(2,1)}), bf16[64,64,128]{2,1,0:T(8,128)(2,1)S(1)}, u32[]{:S(2)}, u32[]{:S(2)}) async-start(bf16[64,64,128]{2,1,0:T(8,128)(2,1)} %shard_map.118), calls=%async_computation.5 | async-start | bytes 2097152 | tf_op jit(solution)/shard_map/all_to_all | solution.py:239
  143.3 3.6 %collective-permute-start = (bf16[128,128]{1,0:T(8,128)(2,1)S(1)}, bf16[128,128]{1,0:T(8,128)(2,1)S(1)}, u32[]{:S(2)}, u32[]{:S(2)}) collective-permute-start(bf16[128,128]{1,0:T(8,128)(2,1)S(1)} %get-tuple-element.11.state_ref), channel_id=1, source_target_pairs={{0,32},{32,0},{1,33},{33,1},{2,34},{34,2},{3,35},{35,3},{4,36},{36... | collective-permute-start | bytes 98312 | tf_op jit(solution)/shard_map/ppermute | solution.py:266
  146.9 10.9 %collective-permute-done.partner_ref = bf16[128,128]{1,0:T(8,128)(2,1)S(1)} collective-permute-done((bf16[128,128]{1,0:T(8,128)(2,1)S(1)}, bf16[128,128]{1,0:T(8,128)(2,1)S(1)}, u32[]{:S(2)}, u32[]{:S(2)}) %collective-permute-start) | collective-permute-done | bytes 32800 | tf_op jit(solution)/shard_map/ppermute | solution.py:266
  157.7 1.9 all-to-all-done.5
  159.6 0.6 shard_map.119
  160.2 35.8 %all_to_all.45.grad_ref.parts_ref = bf16[8,256,128]{2,1,0:T(8,128)(2,1)S(1)} all-to-all(bf16[8,256,128]{2,1,0:T(8,128)(2,1)S(1)} %shard_map.119), channel_id=1, replica_groups=mesh['far'=8,'near'=2,'expert'=32] {'far'}, dimensions={0} | all-to-all | bytes 1048576 | tf_op jit(solution)/shard_map/all_to_all | solution.py:239
  196.0 1.1 shard_map.120
  197.1 24.1 %all_to_all.46 = bf16[64,80,128]{2,1,0:T(8,128)(2,1)S(1)} all-to-all(bf16[64,80,128]{2,1,0:T(8,128)(2,1)S(1)} %bitcast.19), channel_id=1, replica_groups=mesh['far'=8,'near'=2,'expert'=32] {'near','expert'}, dimensions={0} | all-to-all | bytes 2621440 | tf_op jit(solution)/shard_map/all_to_all | solution.py:239
  221.2 1.7 shard_map.121
Async XLA Ops:
  0.6 0.8 copy-start.4
  1.4 0.7 copy-start.8
  2.1 0.7 copy-start.9
  40.2 28.1 %copy-start.3 = (bf16[1,128,4096]{2,1,0:T(8,128)(2,1)S(1)}, bf16[1,128,4096]{2,1,0:T(8,128)(2,1)}, u32[]{:S(2)}) copy-start(bf16[1,128,4096]{2,1,0:T(8,128)(2,1)} %param.16) | copy-start | bytes 3145732
  41.4 26.9 %copy-start.1 = (bf16[1,4096,128]{2,1,0:T(8,128)(2,1)S(1)}, bf16[1,4096,128]{2,1,0:T(8,128)(2,1)}, u32[]{:S(2)}) copy-start(bf16[1,4096,128]{2,1,0:T(8,128)(2,1)} %param.14) | copy-start | bytes 3145732
  41.4 26.9 %copy-start.2 = (bf16[1,4096,128]{2,1,0:T(8,128)(2,1)S(1)}, bf16[1,4096,128]{2,1,0:T(8,128)(2,1)}, u32[]{:S(2)}) copy-start(bf16[1,4096,128]{2,1,0:T(8,128)(2,1)} %param.15) | copy-start | bytes 3145732
  41.4 26.9 %copy-start.6 = (f32[4096]{0:T(1024)S(1)}, f32[4096]{0:T(1024)}, u32[]{:S(2)}) copy-start(f32[4096]{0:T(1024)} %param.11) | copy-start | bytes 49156
  95.0 26.1 %copy-start = (bf16[128,2048]{1,0:T(8,128)(2,1)S(1)}, bf16[128,2048]{1,0:T(8,128)(2,1)}, u32[]{:S(2)}) copy-start(bf16[128,2048]{1,0:T(8,128)(2,1)} %weight_ref.3) | copy-start | bytes 1572868
  95.0 26.1 %copy-start.5 = (bf16[128,128]{1,0:T(8,128)(2,1)S(1)}, bf16[128,128]{1,0:T(8,128)(2,1)}, u32[]{:S(2)}) copy-start(bf16[128,128]{1,0:T(8,128)(2,1)} %tok_ref.3) | copy-start | bytes 98308
  96.8 38.6 %copy-start.7 = (bf16[128,64]{0,1:T(8,128)(2,1)S(1)}, bf16[128,64]{0,1:T(8,128)(2,1)}, u32[]{:S(2)}) copy-start(bf16[128,64]{0,1:T(8,128)(2,1)} %param.18) | copy-start | bytes 49156
  96.8 38.6 %copy-start.10 = (s32[128]{0:T(128)S(1)}, s32[128]{0:T(128)}, u32[]{:S(2)}) copy-start(s32[128]{0:T(128)} %param.19) | copy-start | bytes 1540
  136.5 23.1 %all-to-all-start.5 = ((bf16[64,64,128]{2,1,0:T(8,128)(2,1)}), bf16[64,64,128]{2,1,0:T(8,128)(2,1)S(1)}, u32[]{:S(2)}, u32[]{:S(2)}) async-start(bf16[64,64,128]{2,1,0:T(8,128)(2,1)} %shard_map.118), calls=%async_computation.5 | async-start | bytes 2097152 | tf_op jit(solution)/shard_map/all_to_all | solution.py:239
  143.3 14.5 %collective-permute-start = (bf16[128,128]{1,0:T(8,128)(2,1)S(1)}, bf16[128,128]{1,0:T(8,128)(2,1)S(1)}, u32[]{:S(2)}, u32[]{:S(2)}) collective-permute-start(bf16[128,128]{1,0:T(8,128)(2,1)S(1)} %get-tuple-element.11.state_ref), channel_id=1, source_target_pairs={{0,32},{32,0},{1,33},{33,1},{2,34},{34,2},{3,35},{35,3},{4,36},{36... | collective-permute-start | bytes 98312 | tf_op jit(solution)/shard_map/ppermute | solution.py:266
